TPU v7x, 32 devices: a whole 2x2x4 slice. The times are simulated.
32 devices in a mesh: heads: 4 (over y, x), fsdp: 8 (over z, core).
Axes of the slice: x: 2, y: 2, z: 4, core: 2. Of those that a mesh axis runs over, the one named last changes fastest.
Arguments:
- inputs: bfloat16 [8, 3072, 1280], P('fsdp', 'heads'), may hold values from -6 to 6
- cotangent: bfloat16 [8, 3072, 1280], P('fsdp', 'heads'), may hold values from -6 to 6
- lengths: int32 [8, 3], P('fsdp'), may hold values from 1 to 1024, 1536 in all within a row
- adapter_ids: int32 [8, 4], P('fsdp'), may hold values from 0 to 7
- query_weight: bfloat16 [1280, 1280], P('fsdp'), may hold values from -0.15625 to 0.15625
- key_weight: bfloat16 [1280, 1280], P('fsdp'), may hold values from -0.15625 to 0.15625
- value_weight: bfloat16 [1280, 1280], P('fsdp'), may hold values from -0.15625 to 0.15625
- out_weight: bfloat16 [1280, 1280], P('fsdp'), may hold values from -1.25 to 1.25
- up_weight: bfloat16 [1280, 1280], P('fsdp'), may hold values from -0.15625 to 0.15625
- down_weight: bfloat16 [1280, 1280], P('fsdp'), may hold values from -0.15625 to 0.15625
- attn_gain: bfloat16 [1280], replicated, may hold values from 0.099609375 to 1.8984375
- mlp_gain: bfloat16 [1280], replicated, may hold values from 0.099609375 to 1.8984375
- query_scale: float32 [80], replicated, may hold values from 0.5 to 2
- adapter_in: bfloat16 [4, 8, 1280, 16], replicated, may hold values from -0.15625 to 0.15625
- adapter_out: bfloat16 [4, 8, 16, 1280], replicated, may hold values from -1.5 to 1.5
Outputs:
- outputs: bfloat16 [8, 3072, 1280], P('fsdp', 'heads')
- grad_inputs: float32 [8, 3072, 1280], P('fsdp', 'heads')
- grad_adapter_in: float32 [4, 8, 1280, 16], replicated
- grad_adapter_out: float32 [4, 8, 16, 1280], replicated
Inputs may be any that keep to these rules, and one draw needn't show every extreme that they name: In every group the 3 lengths sum to 1536, and the longest is 1024.
All inputs are finite; a program needn't handle non-finite values.
Results may differ from a plain program's by a relative error of at most 0.015.
The roundings to bfloat16 on the way count: a program that leaves them out, or rounds other values in their place, can miss the bound.
Values may be sent and summed in bfloat16 or wider, within the bound.
No kernel may reach another device: no remote copies, remote signals or barrier semaphores. Data moves between devices by JAX's collectives and lax.ppermute only.
A program may use at most 256 MiB of HBM per device.

v0:
```python
import jax
import jax.numpy as jnp
from jax import lax
from jax.sharding import PartitionSpec as P

D = 1280
HEADS = 16
HEAD_DIM = 80
RANK = 16
ADAPTERS = 8
CONTS = 3
CONT_LEN = 512
PROMPT_LEN = 1536
GROUP_TOK = 3072


EPSILON = 1e-06


def product(left, right):
    return jnp.dot(left, right, preferred_element_type=jnp.float32)


def contract_rows(left, right):
    return lax.dot_general(
        left, right, (((0,), (0,)), ((), ())), preferred_element_type=jnp.float32
    )


def contract_cols(left, right):
    return lax.dot_general(
        left, right, (((1,), (1,)), ((), ())), preferred_element_type=jnp.float32
    )


def normalize(values, gain_vec):
    scaling = lax.rsqrt(jnp.mean(values * values, axis=-1, keepdims=True) + EPSILON)
    return (values * scaling * gain_vec, scaling)


def normalize_back(values, scaling, gain_vec, upstream):
    weighted = gain_vec * upstream
    return scaling * weighted - values * scaling**3 * jnp.mean(
        values * weighted, axis=-1, keepdims=True
    )


def segment_of(length_row):
    places = jnp.arange(GROUP_TOK, dtype=jnp.int32)
    bounds = jnp.cumsum(length_row)
    passed = jnp.sum((places[:, None] - PROMPT_LEN >= bounds[None, :]).astype(jnp.int32), axis=1)
    return jnp.where(places < PROMPT_LEN, 0, 1 + passed)


def picker(segments, id_row):
    member = (segments[:, None] == jnp.arange(CONTS + 1, dtype=jnp.int32)[None, :]).astype(
        jnp.int32
    )
    token_ids = jnp.sum(member * id_row[None, :], axis=1)
    columns = jnp.arange(ADAPTERS * RANK, dtype=jnp.int32) // RANK
    return (token_ids[:, None] == columns[None, :]).astype(jnp.float32)


def adapter_forward(normed_low, flat_down, flat_up, chosen):
    inner_low = (product(normed_low, flat_down) * chosen).astype(jnp.bfloat16)
    return (inner_low, product(inner_low, flat_up))


def adapter_backward(normed_low, inner_low, upstream_low, flat_down, flat_up, chosen):
    grad_up = contract_rows(inner_low, upstream_low)
    spread = (contract_cols(upstream_low, flat_up) * chosen).astype(jnp.bfloat16)
    grad_down = contract_rows(normed_low, spread)
    return (grad_down, grad_up, contract_cols(spread, flat_down))


def block_masks(segments):
    places = jnp.arange(GROUP_TOK, dtype=jnp.int32)
    block_count = GROUP_TOK // CONT_LEN
    return (
        places,
        segments == 0,
        places.reshape(block_count, CONT_LEN),
        segments.reshape(block_count, CONT_LEN),
    )


def attend_forward(query_heads, key_heads, value_heads, segments):
    block_count = GROUP_TOK // CONT_LEN
    width_here = query_heads.shape[1]
    heads_here = width_here // HEAD_DIM
    key_split = key_heads.reshape(GROUP_TOK, heads_here, HEAD_DIM)
    value_split = value_heads.reshape(GROUP_TOK, heads_here, HEAD_DIM)
    places, prompt_col, row_place_blocks, row_segment_blocks = block_masks(segments)

    def one_block(pieces):
        query_block, row_places, row_segments = pieces
        scores = jnp.einsum(
            "qhd,khd->hqk", query_block, key_split, preferred_element_type=jnp.float32
        )
        allowed = (places[None, :] <= row_places[:, None]) & (
            prompt_col[None, :] | (segments[None, :] == row_segments[:, None])
        )
        scores = jnp.where(allowed[None], scores, -1e30)
        largest = jnp.max(scores, axis=-1, keepdims=True)
        exponent = jnp.exp(scores - largest)
        row_total = jnp.sum(exponent, axis=-1, keepdims=True)
        probability = (exponent / row_total).astype(jnp.bfloat16)
        mixture = jnp.einsum(
            "hqk,khd->qhd", probability, value_split, preferred_element_type=jnp.float32
        )
        return (
            mixture.reshape(CONT_LEN, width_here).astype(jnp.bfloat16),
            (largest + jnp.log(row_total))[..., 0],
        )

    query_blocks = query_heads.reshape(block_count, CONT_LEN, heads_here, HEAD_DIM)
    mixture, logsum = lax.map(one_block, (query_blocks, row_place_blocks, row_segment_blocks))
    return (mixture.reshape(GROUP_TOK, width_here), logsum)


def attend_backward(query_heads, key_heads, value_heads, grad_heads, logsum, segments):
    block_count = GROUP_TOK // CONT_LEN
    width_here = query_heads.shape[1]
    heads_here = width_here // HEAD_DIM
    key_split = key_heads.reshape(GROUP_TOK, heads_here, HEAD_DIM)
    value_split = value_heads.reshape(GROUP_TOK, heads_here, HEAD_DIM)
    places, prompt_col, row_place_blocks, row_segment_blocks = block_masks(segments)

    def one_block(carry, pieces):
        grad_key_sum, grad_value_sum = carry
        query_block, grad_block, logsum_block, row_places, row_segments = pieces
        scores = jnp.einsum(
            "qhd,khd->hqk", query_block, key_split, preferred_element_type=jnp.float32
        )
        allowed = (places[None, :] <= row_places[:, None]) & (
            prompt_col[None, :] | (segments[None, :] == row_segments[:, None])
        )
        scores = jnp.where(allowed[None], scores, -1e30)
        probability = jnp.exp(scores - logsum_block[..., None])
        upstream = jnp.einsum(
            "qhd,khd->hqk", grad_block, value_split, preferred_element_type=jnp.float32
        )
        centre = jnp.sum(upstream * probability, axis=-1, keepdims=True)
        grad_scores = (probability * (upstream - centre)).astype(jnp.bfloat16)
        grad_query = jnp.einsum(
            "hqk,khd->qhd", grad_scores, key_split, preferred_element_type=jnp.float32
        )
        grad_key_sum = grad_key_sum + jnp.einsum(
            "hqk,qhd->khd", grad_scores, query_block, preferred_element_type=jnp.float32
        )
        grad_value_sum = grad_value_sum + jnp.einsum(
            "hqk,qhd->khd",
            probability.astype(jnp.bfloat16),
            grad_block,
            preferred_element_type=jnp.float32,
        )
        return (
            (grad_key_sum, grad_value_sum),
            grad_query.reshape(CONT_LEN, width_here).astype(jnp.bfloat16),
        )

    query_blocks = query_heads.reshape(block_count, CONT_LEN, heads_here, HEAD_DIM)
    grad_blocks = grad_heads.reshape(block_count, CONT_LEN, heads_here, HEAD_DIM)
    zeros_start = jnp.zeros((GROUP_TOK, heads_here, HEAD_DIM), jnp.float32)
    (grad_key_sum, grad_value_sum), grad_queries = lax.scan(
        one_block,
        (zeros_start, zeros_start),
        (query_blocks, grad_blocks, logsum, row_place_blocks, row_segment_blocks),
    )
    return (
        grad_queries.reshape(GROUP_TOK, width_here),
        grad_key_sum.reshape(GROUP_TOK, width_here).astype(jnp.bfloat16),
        grad_value_sum.reshape(GROUP_TOK, width_here).astype(jnp.bfloat16),
    )


def body(
    inputs,
    cotangent,
    lengths,
    adapter_ids,
    query_weight,
    key_weight,
    value_weight,
    out_weight,
    up_weight,
    down_weight,
    attn_gain,
    mlp_gain,
    query_scale,
    adapter_in,
    adapter_out,
):
    row_count = inputs.shape[1]
    offset = lax.axis_index("heads") * row_count
    segments = segment_of(lengths[0])
    chosen = picker(lax.dynamic_slice_in_dim(segments, offset, row_count), adapter_ids[0])
    flat_down = jnp.transpose(adapter_in, (0, 2, 1, 3)).reshape(4, D, ADAPTERS * RANK)
    flat_up = adapter_out.reshape(4, ADAPTERS * RANK, D)
    gain_attn = attn_gain.astype(jnp.float32)
    gain_mlp = mlp_gain.astype(jnp.float32)
    scale_row = jnp.tile(query_scale, HEADS) * HEAD_DIM ** (-0.5)
    w_query, w_key, w_value, w_out, w_up, w_down = (
        lax.all_gather(query_weight, "fsdp", axis=0, tiled=True),
        lax.all_gather(key_weight, "fsdp", axis=0, tiled=True),
        lax.all_gather(value_weight, "fsdp", axis=0, tiled=True),
        lax.all_gather(out_weight, "fsdp", axis=0, tiled=True),
        lax.all_gather(up_weight, "fsdp", axis=0, tiled=True),
        lax.all_gather(down_weight, "fsdp", axis=0, tiled=True),
    )
    rows_in = inputs[0].astype(jnp.float32)
    normed, scaling_attn = normalize(rows_in, gain_attn)
    normed_low = normed.astype(jnp.bfloat16)
    inner_query, extra_query = adapter_forward(normed_low, flat_down[0], flat_up[0], chosen)
    inner_value, extra_value = adapter_forward(normed_low, flat_down[1], flat_up[1], chosen)
    query_send = ((product(normed_low, w_query) + extra_query) * scale_row).astype(jnp.bfloat16)
    key_send = product(normed_low, w_key).astype(jnp.bfloat16)
    value_send = (product(normed_low, w_value) + extra_value).astype(jnp.bfloat16)
    query_heads, key_heads, value_heads = (
        lax.all_to_all(query_send, "heads", split_axis=1, concat_axis=0, tiled=True),
        lax.all_to_all(key_send, "heads", split_axis=1, concat_axis=0, tiled=True),
        lax.all_to_all(value_send, "heads", split_axis=1, concat_axis=0, tiled=True),
    )
    mixture, logsum = attend_forward(query_heads, key_heads, value_heads, segments)
    mixed_rows = lax.all_to_all(mixture, "heads", split_axis=0, concat_axis=1, tiled=True)
    middle = rows_in + product(mixed_rows, w_out)
    normed_mlp, scaling_mlp = normalize(middle, gain_mlp)
    normed_mlp_low = normed_mlp.astype(jnp.bfloat16)
    inner_up, extra_up = adapter_forward(normed_mlp_low, flat_down[2], flat_up[2], chosen)
    before = product(normed_mlp_low, w_up) + extra_up
    sigmoid_gate = jax.nn.sigmoid(before)
    hidden_low = (before * sigmoid_gate).astype(jnp.bfloat16)
    inner_down, extra_down = adapter_forward(hidden_low, flat_down[3], flat_up[3], chosen)
    outputs = (middle + (product(hidden_low, w_down) + extra_down)).astype(jnp.bfloat16)
    w_query, w_key, w_value, w_out, w_up, w_down = (
        lax.all_gather(query_weight, "fsdp", axis=0, tiled=True),
        lax.all_gather(key_weight, "fsdp", axis=0, tiled=True),
        lax.all_gather(value_weight, "fsdp", axis=0, tiled=True),
        lax.all_gather(out_weight, "fsdp", axis=0, tiled=True),
        lax.all_gather(up_weight, "fsdp", axis=0, tiled=True),
        lax.all_gather(down_weight, "fsdp", axis=0, tiled=True),
    )
    upstream = cotangent[0].astype(jnp.float32)
    grad_after = cotangent[0]
    down_first, down_second, back_down = adapter_backward(
        hidden_low, inner_down, grad_after, flat_down[3], flat_up[3], chosen
    )
    grad_hidden = contract_cols(grad_after, w_down) + back_down
    grad_before = (grad_hidden * sigmoid_gate * (1.0 + before * (1.0 - sigmoid_gate))).astype(
        jnp.bfloat16
    )
    up_first, up_second, back_up = adapter_backward(
        normed_mlp_low, inner_up, grad_before, flat_down[2], flat_up[2], chosen
    )
    grad_normed_mlp = contract_cols(grad_before, w_up) + back_up
    grad_middle = upstream + normalize_back(middle, scaling_mlp, gain_mlp, grad_normed_mlp)
    grad_branch = grad_middle.astype(jnp.bfloat16)
    grad_mixed = contract_cols(grad_branch, w_out).astype(jnp.bfloat16)
    grad_heads = lax.all_to_all(grad_mixed, "heads", split_axis=1, concat_axis=0, tiled=True)
    grad_query_heads, grad_key_heads, grad_value_heads = attend_backward(
        query_heads, key_heads, value_heads, grad_heads, logsum, segments
    )
    grad_query_rows, grad_key_rows, grad_value_rows = (
        lax.all_to_all(grad_query_heads, "heads", split_axis=0, concat_axis=1, tiled=True),
        lax.all_to_all(grad_key_heads, "heads", split_axis=0, concat_axis=1, tiled=True),
        lax.all_to_all(grad_value_heads, "heads", split_axis=0, concat_axis=1, tiled=True),
    )
    grad_query_pre = (grad_query_rows.astype(jnp.float32) * scale_row).astype(jnp.bfloat16)
    query_first, query_second, back_query = adapter_backward(
        normed_low, inner_query, grad_query_pre, flat_down[0], flat_up[0], chosen
    )
    value_first, value_second, back_value = adapter_backward(
        normed_low, inner_value, grad_value_rows, flat_down[1], flat_up[1], chosen
    )
    grad_normed = (
        contract_cols(grad_query_pre, w_query)
        + contract_cols(grad_key_rows, w_key)
        + contract_cols(grad_value_rows, w_value)
        + back_query
        + back_value
    )
    grad_inputs = grad_middle + normalize_back(rows_in, scaling_attn, gain_attn, grad_normed)
    first_terms = jnp.stack([query_first, value_first, up_first, down_first])
    second_terms = jnp.stack([query_second, value_second, up_second, down_second])
    first_total, second_total = lax.psum((first_terms, second_terms), ("heads", "fsdp"))
    grad_first = jnp.transpose(first_total.reshape(4, D, ADAPTERS, RANK), (0, 2, 1, 3))
    grad_second = second_total.reshape(4, ADAPTERS, RANK, D)
    return (outputs[None], grad_inputs[None], grad_first, grad_second)


def solution(mesh):
    placed = (
        P("fsdp", "heads", None),
        P("fsdp", "heads", None),
        P("fsdp", None),
        P("fsdp", None),
        P("fsdp", None),
        P("fsdp", None),
        P("fsdp", None),
        P("fsdp", None),
        P("fsdp", None),
        P("fsdp", None),
        P(),
        P(),
        P(),
        P(),
        P(),
    )
    return jax.shard_map(
        body,
        mesh=mesh,
        in_specs=placed,
        out_specs=(P("fsdp", "heads", None), P("fsdp", "heads", None), P(), P()),
        check_vma=False,
    )
```

profile of v0, /device:TPU:9, one launch (start us, length us, event | category | flops | bytes accessed | tf_op | source)
XLA Modules:
  0.0 1297.4 jit_solution(6721409575038360464)
XLA Ops:
  15.8 33.8 %all-gather.9.cloned.1.call-done = bf16[1280,1280]{1,0:T(8,128)(2,1)} async-done(((bf16[160,1280]{1,0:T(8,128)(2,1)}), bf16[1280,1280]{1,0:T(8,128)(2,1)}) %all-gather.9.cloned.1.call-update) | async-done | bytes 3276816 | tf_op jit(solution)/shard_map/all_gather | solution.py:205
  66.3 23.2 %all-gather.11.cloned.1.call-done = bf16[1280,1280]{1,0:T(8,128)(2,1)} async-done(((bf16[160,1280]{1,0:T(8,128)(2,1)}), bf16[1280,1280]{1,0:T(8,128)(2,1)}) %all-gather.11.cloned.1.call-update) | async-done | bytes 3276816 | tf_op jit(solution)/shard_map/all_gather | solution.py:206
  105.5 23.9 %all-gather.7.cloned.1.call-done = bf16[1280,1280]{1,0:T(8,128)(2,1)} async-done(((bf16[160,1280]{1,0:T(8,128)(2,1)}), bf16[1280,1280]{1,0:T(8,128)(2,1)}) %all-gather.7.cloned.1.call-update) | async-done | bytes 3276816 | tf_op jit(solution)/shard_map/all_gather | solution.py:204
  179.5 230.1 %while.28 = (s32[]{:T(128)}, bf16[6,512,320]{1,2,0:T(8,128)(2,1)}, f32[6,4,512]{2,1,0:T(4,128)}, s32[6,512]{1,0:T(8,128)S(1)}, pred[3072]{0:T(1024)(128)(4,1)S(1...) while((s32[]{:T(128)}, bf16[6,512,320]{1,2,0:T(8,128)(2,1)}, ...), condition=%wide.region_7.8_spmd.clone, body=%wide.region_4.7_spmd.clone.sunk | while | flops 2076342272 | bytes 94989472 | solution.py:117
  193.5 11.9 fusion.193
  232.1 11.9 fusion.193
  270.5 11.7 fusion.193
  308.7 11.7 fusion.193
  346.9 11.7 fusion.193
  385.1 11.7 fusion.193
  432.3 13.1 %all-to-all-done.3 = bf16[4,768,320]{1,2,0:T(8,128)(2,1)} async-done(((bf16[4,768,320]{1,2,0:T(8,128)(2,1)}), bf16[4,768,320]{1,2,0:T(8,128)(2,1)}, u32[]{:S(2)}, u32[]{:S(2)}) %all-to-all-start.3) | async-done | bytes 1966112 | tf_op jit(solution)/shard_map/all_to_all | solution.py:225
  485.6 23.0 %all-to-all-done.4 = bf16[768,4,320]{0,2,1:T(8,128)(2,1)} async-done(((bf16[768,4,320]{0,2,1:T(8,128)(2,1)}), bf16[768,4,320]{0,2,1:T(8,128)(2,1)}, u32[]{:S(2)}, u32[]{:S(2)}) %all-to-all-start.4) | async-done | bytes 1966112 | tf_op jit(solution)/shard_map/all_to_all | solution.py:259
  523.4 526.7 %while.29 = (s32[]{:T(128)}, f32[3072,4,80]{0,2,1:T(8,128)}, f32[3072,4,80]{0,2,1:T(8,128)}, bf16[6,512,320]{1,2,0:T(8,128)(2,1)}, bf16[6,512,4,80]{1,3,2,0:T(8,...) while((s32[]{:T(128)}, f32[3072,4,80]{0,2,1:T(8,128)}, ...), condition=%wide.region_12.13_spmd.clone, body=%wide.region_10.12_spmd.clone.sunk | while | flops 5119047680 | bytes 219360688 | solution.py:165
  539.0 12.8 fusion.207
  551.8 17.6 %multiply_reduce_fusion.4 = (f32[4,512]{1,0:T(4,128)S(1)}, f32[4,512,3072]{2,1,0:T(8,128)}) fusion(f32[4,512,3072]{2,1,0:T(8,128)} %fusion.204, f32[4,512]{1,0:T(4,128)S(1)} %dynamic-slice_bitcast_fusion.2, pred[512,3072]{1,0:T(8,128)(4,1)S(1)} %fusion.205, bf16[3072,4,80]{0,2,1:T(8,128)(2,1)} %get-tuple-element.610, ...), kind=kOutput, calls=%fused_computation.20.clone.1 | convolution fusion | flops 1031796736 | bytes 54214660 | tf_op jit(solution)/shard_map/while/body/eval_jaxpr/qhd,khd->hqk/dot_general | solution.py:140
  569.3 21.8 %multiply_convert_fusion.8 = bf16[4,512,3072]{2,1,0:T(8,128)(2,1)} fusion(f32[4,512,3072]{2,1,0:T(8,128)} %get-tuple-element.533, f32[4,512,3072]{2,1,0:T(8,128)} %fusion.204, f32[4,512]{1,0:T(4,128)S(1)} %get-tuple-element.534, f32[4,512]{1,0:T(4,128)S(1)} %dynamic-slice_bitcast_fusion.2, pred[512,3072]{1,0:T(8,128)(4,1)S(1)} %fusion.205), kind=kLoop, calls=%fused_computation.19.clone.1 | loop fusion | flops 31457280 | bytes 64503808 | tf_op jit(solution)/shard_map/while/body/eval_jaxpr/convert_element_type | solution.py:144
  624.8 13.9 %fusion.207 = f32[3072,4,80]{0,2,1:T(8,128)} fusion(f32[4,512,3072]{2,1,0:T(8,128)} %fusion.204, f32[4,512]{1,0:T(4,128)S(1)} %dynamic-slice_bitcast_fusion.2, pred[512,3072]{1,0:T(8,128)(4,1)S(1)} %fusion.205, f32[3072,4,80]{0,2,1:T(8,128)} %get-tuple-element.585, pred[]{:T(512)S(6)} %compare.7, bf16[6,512,4,80]{1,3,2,0:T(8,128)(2,1)} %get-tuple-element.609, ...), kind=kOutput, calls=%fused_computation.32.clone.1 | convolution fusion | flops 1027473408 | bytes 34938884 | tf_op jit(solution)/shard_map/while/body/eval_jaxpr/hqk,qhd->khd/dot_general | solution.py:151
  638.7 17.6 %multiply_reduce_fusion.4 = (f32[4,512]{1,0:T(4,128)S(1)}, f32[4,512,3072]{2,1,0:T(8,128)}) fusion(f32[4,512,3072]{2,1,0:T(8,128)} %fusion.204, f32[4,512]{1,0:T(4,128)S(1)} %dynamic-slice_bitcast_fusion.2, pred[512,3072]{1,0:T(8,128)(4,1)S(1)} %fusion.205, bf16[3072,4,80]{0,2,1:T(8,128)(2,1)} %get-tuple-element.610, ...), kind=kOutput, calls=%fused_computation.20.clone.1 | convolution fusion | flops 1031796736 | bytes 54214660 | tf_op jit(solution)/shard_map/while/body/eval_jaxpr/qhd,khd->hqk/dot_general | solution.py:140
  656.3 21.8 %multiply_convert_fusion.8 = bf16[4,512,3072]{2,1,0:T(8,128)(2,1)} fusion(f32[4,512,3072]{2,1,0:T(8,128)} %get-tuple-element.533, f32[4,512,3072]{2,1,0:T(8,128)} %fusion.204, f32[4,512]{1,0:T(4,128)S(1)} %get-tuple-element.534, f32[4,512]{1,0:T(4,128)S(1)} %dynamic-slice_bitcast_fusion.2, pred[512,3072]{1,0:T(8,128)(4,1)S(1)} %fusion.205), kind=kLoop, calls=%fused_computation.19.clone.1 | loop fusion | flops 31457280 | bytes 64503808 | tf_op jit(solution)/shard_map/while/body/eval_jaxpr/convert_element_type | solution.py:144
  712.9 13.9 %fusion.207 = f32[3072,4,80]{0,2,1:T(8,128)} fusion(f32[4,512,3072]{2,1,0:T(8,128)} %fusion.204, f32[4,512]{1,0:T(4,128)S(1)} %dynamic-slice_bitcast_fusion.2, pred[512,3072]{1,0:T(8,128)(4,1)S(1)} %fusion.205, f32[3072,4,80]{0,2,1:T(8,128)} %get-tuple-element.585, pred[]{:T(512)S(6)} %compare.7, bf16[6,512,4,80]{1,3,2,0:T(8,128)(2,1)} %get-tuple-element.609, ...), kind=kOutput, calls=%fused_computation.32.clone.1 | convolution fusion | flops 1027473408 | bytes 34938884 | tf_op jit(solution)/shard_map/while/body/eval_jaxpr/hqk,qhd->khd/dot_general | solution.py:151
  726.8 17.6 %multiply_reduce_fusion.4 = (f32[4,512]{1,0:T(4,128)S(1)}, f32[4,512,3072]{2,1,0:T(8,128)}) fusion(f32[4,512,3072]{2,1,0:T(8,128)} %fusion.204, f32[4,512]{1,0:T(4,128)S(1)} %dynamic-slice_bitcast_fusion.2, pred[512,3072]{1,0:T(8,128)(4,1)S(1)} %fusion.205, bf16[3072,4,80]{0,2,1:T(8,128)(2,1)} %get-tuple-element.610, ...), kind=kOutput, calls=%fused_computation.20.clone.1 | convolution fusion | flops 1031796736 | bytes 54214660 | tf_op jit(solution)/shard_map/while/body/eval_jaxpr/qhd,khd->hqk/dot_general | solution.py:140
  744.3 21.8 %multiply_convert_fusion.8 = bf16[4,512,3072]{2,1,0:T(8,128)(2,1)} fusion(f32[4,512,3072]{2,1,0:T(8,128)} %get-tuple-element.533, f32[4,512,3072]{2,1,0:T(8,128)} %fusion.204, f32[4,512]{1,0:T(4,128)S(1)} %get-tuple-element.534, f32[4,512]{1,0:T(4,128)S(1)} %dynamic-slice_bitcast_fusion.2, pred[512,3072]{1,0:T(8,128)(4,1)S(1)} %fusion.205), kind=kLoop, calls=%fused_computation.19.clone.1 | loop fusion | flops 31457280 | bytes 64503808 | tf_op jit(solution)/shard_map/while/body/eval_jaxpr/convert_element_type | solution.py:144
  801.0 13.9 %fusion.207 = f32[3072,4,80]{0,2,1:T(8,128)} fusion(f32[4,512,3072]{2,1,0:T(8,128)} %fusion.204, f32[4,512]{1,0:T(4,128)S(1)} %dynamic-slice_bitcast_fusion.2, pred[512,3072]{1,0:T(8,128)(4,1)S(1)} %fusion.205, f32[3072,4,80]{0,2,1:T(8,128)} %get-tuple-element.585, pred[]{:T(512)S(6)} %compare.7, bf16[6,512,4,80]{1,3,2,0:T(8,128)(2,1)} %get-tuple-element.609, ...), kind=kOutput, calls=%fused_computation.32.clone.1 | convolution fusion | flops 1027473408 | bytes 34938884 | tf_op jit(solution)/shard_map/while/body/eval_jaxpr/hqk,qhd->khd/dot_general | solution.py:151
  814.8 17.6 %multiply_reduce_fusion.4 = (f32[4,512]{1,0:T(4,128)S(1)}, f32[4,512,3072]{2,1,0:T(8,128)}) fusion(f32[4,512,3072]{2,1,0:T(8,128)} %fusion.204, f32[4,512]{1,0:T(4,128)S(1)} %dynamic-slice_bitcast_fusion.2, pred[512,3072]{1,0:T(8,128)(4,1)S(1)} %fusion.205, bf16[3072,4,80]{0,2,1:T(8,128)(2,1)} %get-tuple-element.610, ...), kind=kOutput, calls=%fused_computation.20.clone.1 | convolution fusion | flops 1031796736 | bytes 54214660 | tf_op jit(solution)/shard_map/while/body/eval_jaxpr/qhd,khd->hqk/dot_general | solution.py:140
  832.4 21.8 %multiply_convert_fusion.8 = bf16[4,512,3072]{2,1,0:T(8,128)(2,1)} fusion(f32[4,512,3072]{2,1,0:T(8,128)} %get-tuple-element.533, f32[4,512,3072]{2,1,0:T(8,128)} %fusion.204, f32[4,512]{1,0:T(4,128)S(1)} %get-tuple-element.534, f32[4,512]{1,0:T(4,128)S(1)} %dynamic-slice_bitcast_fusion.2, pred[512,3072]{1,0:T(8,128)(4,1)S(1)} %fusion.205), kind=kLoop, calls=%fused_computation.19.clone.1 | loop fusion | flops 31457280 | bytes 64503808 | tf_op jit(solution)/shard_map/while/body/eval_jaxpr/convert_element_type | solution.py:144
  889.0 13.9 %fusion.207 = f32[3072,4,80]{0,2,1:T(8,128)} fusion(f32[4,512,3072]{2,1,0:T(8,128)} %fusion.204, f32[4,512]{1,0:T(4,128)S(1)} %dynamic-slice_bitcast_fusion.2, pred[512,3072]{1,0:T(8,128)(4,1)S(1)} %fusion.205, f32[3072,4,80]{0,2,1:T(8,128)} %get-tuple-element.585, pred[]{:T(512)S(6)} %compare.7, bf16[6,512,4,80]{1,3,2,0:T(8,128)(2,1)} %get-tuple-element.609, ...), kind=kOutput, calls=%fused_computation.32.clone.1 | convolution fusion | flops 1027473408 | bytes 34938884 | tf_op jit(solution)/shard_map/while/body/eval_jaxpr/hqk,qhd->khd/dot_general | solution.py:151
  902.9 17.6 %multiply_reduce_fusion.4 = (f32[4,512]{1,0:T(4,128)S(1)}, f32[4,512,3072]{2,1,0:T(8,128)}) fusion(f32[4,512,3072]{2,1,0:T(8,128)} %fusion.204, f32[4,512]{1,0:T(4,128)S(1)} %dynamic-slice_bitcast_fusion.2, pred[512,3072]{1,0:T(8,128)(4,1)S(1)} %fusion.205, bf16[3072,4,80]{0,2,1:T(8,128)(2,1)} %get-tuple-element.610, ...), kind=kOutput, calls=%fused_computation.20.clone.1 | convolution fusion | flops 1031796736 | bytes 54214660 | tf_op jit(solution)/shard_map/while/body/eval_jaxpr/qhd,khd->hqk/dot_general | solution.py:140
  920.5 21.8 %multiply_convert_fusion.8 = bf16[4,512,3072]{2,1,0:T(8,128)(2,1)} fusion(f32[4,512,3072]{2,1,0:T(8,128)} %get-tuple-element.533, f32[4,512,3072]{2,1,0:T(8,128)} %fusion.204, f32[4,512]{1,0:T(4,128)S(1)} %get-tuple-element.534, f32[4,512]{1,0:T(4,128)S(1)} %dynamic-slice_bitcast_fusion.2, pred[512,3072]{1,0:T(8,128)(4,1)S(1)} %fusion.205), kind=kLoop, calls=%fused_computation.19.clone.1 | loop fusion | flops 31457280 | bytes 64503808 | tf_op jit(solution)/shard_map/while/body/eval_jaxpr/convert_element_type | solution.py:144
  977.1 13.9 %fusion.207 = f32[3072,4,80]{0,2,1:T(8,128)} fusion(f32[4,512,3072]{2,1,0:T(8,128)} %fusion.204, f32[4,512]{1,0:T(4,128)S(1)} %dynamic-slice_bitcast_fusion.2, pred[512,3072]{1,0:T(8,128)(4,1)S(1)} %fusion.205, f32[3072,4,80]{0,2,1:T(8,128)} %get-tuple-element.585, pred[]{:T(512)S(6)} %compare.7, bf16[6,512,4,80]{1,3,2,0:T(8,128)(2,1)} %get-tuple-element.609, ...), kind=kOutput, calls=%fused_computation.32.clone.1 | convolution fusion | flops 1027473408 | bytes 34938884 | tf_op jit(solution)/shard_map/while/body/eval_jaxpr/hqk,qhd->khd/dot_general | solution.py:151
  991.0 17.6 %multiply_reduce_fusion.4 = (f32[4,512]{1,0:T(4,128)S(1)}, f32[4,512,3072]{2,1,0:T(8,128)}) fusion(f32[4,512,3072]{2,1,0:T(8,128)} %fusion.204, f32[4,512]{1,0:T(4,128)S(1)} %dynamic-slice_bitcast_fusion.2, pred[512,3072]{1,0:T(8,128)(4,1)S(1)} %fusion.205, bf16[3072,4,80]{0,2,1:T(8,128)(2,1)} %get-tuple-element.610, ...), kind=kOutput, calls=%fused_computation.20.clone.1 | convolution fusion | flops 1031796736 | bytes 54214660 | tf_op jit(solution)/shard_map/while/body/eval_jaxpr/qhd,khd->hqk/dot_general | solution.py:140
  1008.6 21.8 %multiply_convert_fusion.8 = bf16[4,512,3072]{2,1,0:T(8,128)(2,1)} fusion(f32[4,512,3072]{2,1,0:T(8,128)} %get-tuple-element.533, f32[4,512,3072]{2,1,0:T(8,128)} %fusion.204, f32[4,512]{1,0:T(4,128)S(1)} %get-tuple-element.534, f32[4,512]{1,0:T(4,128)S(1)} %dynamic-slice_bitcast_fusion.2, pred[512,3072]{1,0:T(8,128)(4,1)S(1)} %fusion.205), kind=kLoop, calls=%fused_computation.19.clone.1 | loop fusion | flops 31457280 | bytes 64503808 | tf_op jit(solution)/shard_map/while/body/eval_jaxpr/convert_element_type | solution.py:144
  1164.5 120.8 %all-reduce.3.cloned.1.call-done = (f32[4,8,1280,16]{2,3,1,0:T(8,128)}, f32[4,8,16,1280]{3,2,1,0:T(8,128)}) async-done(((f32[4,8,1280,16]{2,3,1,0:T(8,128)}, f32[4,8,16,1280]{3,2,1,0:T(8,128)}), (f32[4,8,1280,16]{2,3,1,0:T(8,128)}, f32[4,8,16,1280]{3,2,1,0:T(8,128)})) %all-reduce.3.cloned.1.call-update) | async-done | bytes 5242896 | tf_op jit(solution)/shard_map/psum | solution.py:285
  (475 shorter events, 653.5 us)
Async XLA Ops:
  7.2 42.4 %all-gather.9.cloned.1.call-start = ((), (), s32[]{:S(2)}) async-start(), calls=%async_computation.9 | async-start | bytes 3686400 | tf_op jit(solution)/shard_map/all_gather | solution.py:205
  7.9 81.6 %all-gather.11.cloned.1.call-start = ((), (), s32[]{:S(2)}) async-start(), calls=%async_computation.10 | async-start | bytes 3686400 | tf_op jit(solution)/shard_map/all_gather | solution.py:206
  8.7 120.7 %all-gather.7.cloned.1.call-start = ((), (), s32[]{:S(2)}) async-start(), calls=%async_computation.8 | async-start | bytes 3686400 | tf_op jit(solution)/shard_map/all_gather | solution.py:204
  9.4 415.6 %all-gather.17.cloned.1.call-start = ((), (), s32[]{:S(2)}) async-start(), calls=%async_computation.13 | async-start | bytes 3686400 | tf_op jit(solution)/shard_map/all_gather | solution.py:209
  10.0 422.3 %all-gather.13.cloned.1.call-start = ((), (), s32[]{:S(2)}) async-start(), calls=%async_computation.11 | async-start | bytes 3686400 | tf_op jit(solution)/shard_map/all_gather | solution.py:207
  12.5 116.9 %copy-start.68 = (f32[768]{0:T(1024)}, f32[768]{0:T(1024)S(1)}, u32[]{:S(2)}) copy-start(f32[768]{0:T(1024)S(1)} %get-tuple-element.366) | copy-start | bytes 9220
  12.5 116.9 %copy-start.65 = (f32[1280]{0:T(1024)}, f32[1280]{0:T(1024)S(1)}, u32[]{:S(2)}) copy-start(f32[1280]{0:T(1024)S(1)} %convert_element_type.166) | copy-start | bytes 15364
  12.8 91.9 %copy-start.76 = (s32[768]{0:T(1024)}, s32[768]{0:T(1024)S(1)}, u32[]{:S(2)}) copy-start(s32[768]{0:T(1024)S(1)} %select_reduce_fusion.1) | copy-start | bytes 9220
  12.8 91.9 %copy-start.85 = (s32[128]{0:T(128)}, s32[128]{0:T(128)S(1)}, u32[]{:S(2)}) copy-start(s32[128]{0:T(128)S(1)} %and_select_fusion) | copy-start | bytes 1540
  15.1 40.5 %copy-start.30 = (bf16[1,1280,8,16]{1,3,2,0:T(8,128)(2,1)}, bf16[1,1280,8,16]{1,3,2,0:T(8,128)(2,1)S(1)}, u32[]{:S(2)}) copy-start(bf16[1,1280,8,16]{1,3,2,0:T(8,128)(2,1)S(1)} %get-tuple-element.361) | copy-start | bytes 983044
  15.1 89.6 %copy-start.39 = (bf16[1,1280,8,16]{1,3,2,0:T(8,128)(2,1)}, bf16[1,1280,8,16]{1,3,2,0:T(8,128)(2,1)S(1)}, u32[]{:S(2)}) copy-start(bf16[1,1280,8,16]{1,3,2,0:T(8,128)(2,1)S(1)} %get-tuple-element.362) | copy-start | bytes 983044
  15.8 78.3 %copy-start.43 = (bf16[768,128]{1,0:T(8,128)(2,1)}, bf16[768,128]{1,0:T(8,128)(2,1)S(1)}, u32[]{:S(2)}) copy-start(bf16[768,128]{1,0:T(8,128)(2,1)S(1)} %fusion.79) | copy-start | bytes 589828
  59.6 40.6 %all-to-all-start.1 = ((bf16[768,4,320]{0,2,1:T(8,128)(2,1)}), bf16[768,4,320]{0,2,1:T(8,128)(2,1)}, u32[]{:S(2)}, u32[]{:S(2)}) async-start(bf16[768,4,320]{0,2,1:T(8,128)(2,1)} %bitcast.288), calls=%async_computation.1 | async-start | bytes 3932160 | tf_op jit(solution)/shard_map/all_to_all | solution.py:221
  66.3 27.9 %copy-start.34 = (bf16[1,8,16,1280]{3,2,1,0:T(8,128)(2,1)}, bf16[1,8,16,1280]{3,2,1,0:T(8,128)(2,1)S(1)}, u32[]{:S(2)}) copy-start(bf16[1,8,16,1280]{3,2,1,0:T(8,128)(2,1)S(1)} %get-tuple-element.356) | copy-start | bytes 983044
  66.3 67.8 %copy-start.32 = (bf16[1,8,16,1280]{3,2,1,0:T(8,128)(2,1)}, bf16[1,8,16,1280]{3,2,1,0:T(8,128)(2,1)S(1)}, u32[]{:S(2)}) copy-start(bf16[1,8,16,1280]{3,2,1,0:T(8,128)(2,1)S(1)} %get-tuple-element.357) | copy-start | bytes 983044
  100.2 36.9 %all-to-all-start.2 = ((bf16[768,4,320]{0,2,1:T(8,128)(2,1)}), bf16[768,4,320]{0,2,1:T(8,128)(2,1)}, u32[]{:S(2)}, u32[]{:S(2)}) async-start(bf16[768,4,320]{0,2,1:T(8,128)(2,1)} %bitcast.287), calls=%async_computation.2 | async-start | bytes 3932160 | tf_op jit(solution)/shard_map/all_to_all | solution.py:222
  104.6 29.5 %copy-start.79 = (f32[80]{0:T(128)}, f32[80]{0:T(128)S(1)}, u32[]{:S(2)}) copy-start(f32[80]{0:T(128)S(1)} %broadcast_multiply_fusion.2) | copy-start | bytes 964
  104.7 29.4 %copy-start.61 = (f32[1280]{0:T(1024)}, f32[1280]{0:T(1024)S(1)}, u32[]{:S(2)}) copy-start(f32[1280]{0:T(1024)S(1)} %mul.223) | copy-start | bytes 15364
  105.5 28.6 %copy-start.41 = (bf16[768,128]{1,0:T(8,128)(2,1)}, bf16[768,128]{1,0:T(8,128)(2,1)S(1)}, u32[]{:S(2)}) copy-start(bf16[768,128]{1,0:T(8,128)(2,1)S(1)} %fusion.78) | copy-start | bytes 589828
  137.0 27.8 %all-to-all-start = ((bf16[768,4,320]{0,2,1:T(8,128)(2,1)}), bf16[768,4,320]{0,2,1:T(8,128)(2,1)}, u32[]{:S(2)}, u32[]{:S(2)}) async-start(bf16[768,4,320]{0,2,1:T(8,128)(2,1)} %bitcast.8), calls=%async_computation | async-start | bytes 3932160 | tf_op jit(solution)/shard_map/all_to_all | solution.py:220
  141.5 314.3 %all-gather.15.cloned.1.call-start = ((), (), s32[]{:S(2)}) async-start(), calls=%async_computation.12 | async-start | bytes 3686400 | tf_op jit(solution)/shard_map/all_gather | solution.py:208
  417.9 27.5 %all-to-all-start.3 = ((bf16[4,768,320]{1,2,0:T(8,128)(2,1)}), bf16[4,768,320]{1,2,0:T(8,128)(2,1)}, u32[]{:S(2)}, u32[]{:S(2)}) async-start(bf16[4,768,320]{1,2,0:T(8,128)(2,1)} %copy.81), calls=%async_computation.3 | async-start | bytes 3932160 | tf_op jit(solution)/shard_map/all_to_all | solution.py:225
  425.0 38.7 %copy-start.53 = (bf16[768,128]{1,0:T(8,128)(2,1)}, bf16[768,128]{1,0:T(8,128)(2,1)S(1)}, u32[]{:S(2)}) copy-start(bf16[768,128]{1,0:T(8,128)(2,1)S(1)} %fusion.85) | copy-start | bytes 589828
  451.5 18.2 %copy-start.63 = (f32[768]{0:T(1024)}, f32[768]{0:T(1024)S(1)}, u32[]{:S(2)}) copy-start(f32[768]{0:T(1024)S(1)} %get-tuple-element.368) | copy-start | bytes 9220
  451.5 18.2 %copy-start.70 = (f32[768]{0:T(1024)}, f32[768]{0:T(1024)S(1)}, u32[]{:S(2)}) copy-start(f32[768]{0:T(1024)S(1)} %get-tuple-element.367) | copy-start | bytes 9220
  481.1 27.5 %all-to-all-start.4 = ((bf16[768,4,320]{0,2,1:T(8,128)(2,1)}), bf16[768,4,320]{0,2,1:T(8,128)(2,1)}, u32[]{:S(2)}, u32[]{:S(2)}) async-start(bf16[768,4,320]{0,2,1:T(8,128)(2,1)} %bitcast.289), calls=%async_computation.4 | async-start | bytes 3932160 | tf_op jit(solution)/shard_map/all_to_all | solution.py:259
  523.6 15.4 %copy-start.48 = (pred[3072]{0:T(1024)(128)(4,1)}, pred[3072]{0:T(1024)(128)(4,1)S(1)}, u32[]{:S(2)}) copy-start(pred[3072]{0:T(1024)(128)(4,1)S(1)} %get-tuple-element.604) | copy-start | bytes 9220 | tf_op jit(solution)/shard_map/while
  609.4 15.4 %copy-start.48 = (pred[3072]{0:T(1024)(128)(4,1)}, pred[3072]{0:T(1024)(128)(4,1)S(1)}, u32[]{:S(2)}) copy-start(pred[3072]{0:T(1024)(128)(4,1)S(1)} %get-tuple-element.604) | copy-start | bytes 9220 | tf_op jit(solution)/shard_map/while
  1058.1 27.6 %all-to-all-start.7 = ((bf16[4,768,320]{1,2,0:T(8,128)(2,1)}), bf16[4,768,320]{1,2,0:T(8,128)(2,1)}, u32[]{:S(2)}, u32[]{:S(2)}) async-start(bf16[4,768,320]{1,2,0:T(8,128)(2,1)} %copy.90), calls=%async_computation.7 | async-start | bytes 3932160 | tf_op jit(solution)/shard_map/all_to_all | solution.py:266
  1085.7 26.7 %all-to-all-start.5 = ((bf16[4,768,320]{1,2,0:T(8,128)(2,1)}), bf16[4,768,320]{1,2,0:T(8,128)(2,1)S(1)}, u32[]{:S(2)}, u32[]{:S(2)}) async-start(bf16[4,768,320]{1,2,0:T(8,128)(2,1)} %copy.87), calls=%async_computation.5 | async-start | bytes 3932160 | tf_op jit(solution)/shard_map/all_to_all | solution.py:264
  1113.7 36.9 %all-to-all-start.6 = ((bf16[4,768,320]{1,2,0:T(8,128)(2,1)}), bf16[4,768,320]{1,2,0:T(8,128)(2,1)}, u32[]{:S(2)}, u32[]{:S(2)}) async-start(bf16[4,768,320]{1,2,0:T(8,128)(2,1)} %copy.89), calls=%async_computation.6 | async-start | bytes 3932160 | tf_op jit(solution)/shard_map/all_to_all | solution.py:265
  1118.2 167.1 %all-reduce.3.cloned.1.call-start = ((), (), s32[]{:S(2)}) async-start(), calls=%async_computation.14 | async-start | bytes 10485760 | tf_op jit(solution)/shard_map/psum | solution.py:285
  (117 other events, 692.4 us)
Sparse Core Ops, SparseCore 0:
  9.6 39.9 all-gather.8
  51.3 38.1 all-gather.10
  91.1 38.1 all-gather.6
  130.9 38.1 all-gather.16
  170.6 38.1 all-gather.12
  210.3 38.1 all-gather.14
  1138.6 146.6 all-reduce.2
where the time goes:
time: 1310 us; the launch traced here: 1300 us
  matrix products  603 us (46%)
  waiting for transfers between devices  256 us (20%)
  other arithmetic  252 us (19%)
  local copies, waits for them, and re-layouts  133 us (10%)
  starting transfers between devices  35.9 us (3%)
  between operations  15.4 us (1%)
    dot_general x12, matrix products, one_block(): jnp.einsum('qhd,khd->hqk', query_block, key_split, preferred_element_type...  137 us
    convert_element_type x6, other arithmetic, one_block(): grad_scores = (probability * (upstream - centre)).astype(jnp.bfloat16)  131 us
    psum x1, waiting for transfers between devices, body(): lax.psum((first_terms, second_terms), ('heads', 'fsdp'))  121 us
    dot_general x6, matrix products, one_block(): jnp.einsum('qhd,khd->hqk', grad_block, value_split, preferred_element_typ...  106 us
    dot_general x6, matrix products, one_block(): jnp.einsum('hqk,qhd->khd', probability.astype(jnp.bfloat16), grad_block,...  82 us
    reduce_sum x6, other arithmetic, one_block(): row_total = jnp.sum(exponent, axis=-1, keepdims=True)  70.7 us
    dot_general x6, matrix products, one_block(): jnp.einsum('hqk,khd->qhd', probability, value_split, preferred_element_ty...  68.5 us
    dot_general x6, matrix products, one_block(): jnp.einsum('hqk,qhd->khd', grad_scores, query_block, preferred_element_ty...  59.4 us
  transfers between devices with their start and end apart: 15, of which 8 were waited for; matrix products, arithmetic and copies ran while one was open for 31% of the time, Pallas kernels for 0%

commit v1 on v0

v1 whole, which is shorter than its diff:
```python
import jax
import jax.numpy as jnp
from jax import lax
from jax.experimental import pallas as pl
from jax.experimental.pallas import tpu as pltpu
from jax.sharding import PartitionSpec as P

D = 1280
HEADS = 16
HD = 80
RANK = 16
ADAPTERS = 8
AR = ADAPTERS * RANK
TOK = 3072
PROMPT = 1536
ROWS = 768
PARTS = TOK // ROWS
LH = HEADS // PARTS
EPSILON = 1e-06
B = 256
f32, bf16 = jnp.float32, jnp.bfloat16


def nt(a, b):
    return lax.dot_general(a, b, (((1,), (1,)), ((), ())), preferred_element_type=f32)


def tn(a, b):
    return lax.dot_general(a, b, (((0,), (0,)), ((), ())), preferred_element_type=f32)


def qkv_kernel(bounds, ids, x_ref, gain_ref, w_ref, down_ref, up_ref, scale_ref, out_ref, wt, ut):
    @pl.when(pl.program_id(0) == 0)
    def _():
        wt[...] = w_ref[...].T
        ut[...] = up_ref[...].T

    x = x_ref[...].astype(f32)
    q = lax.rsqrt(jnp.mean(x * x, axis=1, keepdims=True) + EPSILON)
    normed = (x * q * gain_ref[...]).astype(bf16)
    pos = pl.program_id(0) * B + lax.broadcasted_iota(jnp.int32, (B, 1), 0)
    token = jnp.where(
        pos < PROMPT, ids[0], jnp.where(pos < bounds[0], ids[1], jnp.where(pos < bounds[1], ids[2], ids[3]))
    )
    lane = lax.broadcasted_iota(jnp.int32, (B, 2 * AR), 1)
    chosen = (lane % AR) // RANK == token
    inner = jnp.where(chosen, nn(normed, down_ref[...]), 0.0).astype(bf16)
    out = nt(wt[...], normed) + nt(ut[...], inner)
    out_ref[...] = (out * scale_ref[...]).astype(bf16)


def qkv_project(bounds, ids, x, gain, w, down, up, scale):
    width = w.shape[1]
    return pl.pallas_call(
        qkv_kernel,
        out_shape=jax.ShapeDtypeStruct((width, TOK), bf16),
        grid_spec=pltpu.PrefetchScalarGridSpec(
            num_scalar_prefetch=2,
            grid=(TOK // B,),
            in_specs=[
                pl.BlockSpec((B, D), lambda i, *_: (i, 0)),
                pl.BlockSpec((1, D), lambda i, *_: (0, 0)),
                pl.BlockSpec((D, width), lambda i, *_: (0, 0)),
                pl.BlockSpec((D, 2 * AR), lambda i, *_: (0, 0)),
                pl.BlockSpec((2 * AR, width), lambda i, *_: (0, 0)),
                pl.BlockSpec((width, 1), lambda i, *_: (0, 0)),
            ],
            out_specs=pl.BlockSpec((width, B), lambda i, *_: (0, i)),
            scratch_shapes=[pltpu.VMEM((width, D), bf16), pltpu.VMEM((width, 2 * AR), bf16)],
        ),
        compiler_params=pltpu.CompilerParams(dimension_semantics=("arbitrary",), vmem_limit_bytes=60 << 20),
        cost_estimate=pl.CostEstimate(flops=2 * TOK * D * width, bytes_accessed=TOK * D * 2, transcendentals=0),
        name="qkv_project",
    )(bounds, ids, x, gain, w, down, up, scale)


NEG = -1e30

def nn(a, b):
    return lax.dot_general(a, b, (((1,), (0,)), ((), ())), preferred_element_type=f32)

def start_row(qpos, b1, b2):
    return jnp.where(qpos < PROMPT, 0, jnp.where(qpos < b1, PROMPT, jnp.where(qpos < b2, b1, b2)))

def first_block(i, b1, b2):
    q0 = i * B
    return jnp.where(q0 < b1, PROMPT, jnp.where(q0 < b2, b1, b2)) // B


HPB = 4
FW = 512
def fwd_kernel(bounds, qkv_ref, o_ref, lse_ref, kp, qt, vt):
    b1, b2 = bounds[0], bounds[1]
    zpad = jnp.zeros((128 - HD, 128), bf16)
    for h in range(HPB):
        r = h * 3 * HD
        qt[h, 0:HD, :] = qkv_ref[r:r + HD, :]
        qt[h, HD:128, :] = jnp.zeros((128 - HD, TOK), bf16)
        vt[h, 0:HD, :] = qkv_ref[r + 2 * HD:r + 3 * HD, :]
        vt[h, HD:96, :] = (lax.broadcasted_iota(jnp.int32, (16, TOK), 0) == 0).astype(bf16)
        for t in range(TOK // 128):
            kt = qkv_ref[r + HD:r + 2 * HD, t * 128:(t + 1) * 128]
            kp[h, t * 128:(t + 1) * 128, :] = jnp.concatenate([kt, zpad], axis=0).T

    def qblock(i, _):
        q0 = pl.multiple_of(i * B, B)
        qpos = q0 + lax.broadcasted_iota(jnp.int32, (1, B), 1)
        srow = start_row(qpos, b1, b2)

        def step(k0, width, masked, carry):
            ks = pl.ds(k0, width)
            ss = [nn(kp[h, ks, :], qt[h, :, pl.ds(q0, B)]) for h in range(HPB)]
            if masked:
                kpos = k0 + lax.broadcasted_iota(jnp.int32, (width, B), 0)
                ok = (kpos >= srow) & (kpos <= qpos)
                ss = [jnp.where(ok, s, NEG) for s in ss]
            out = []
            for h in range(HPB):
                m, acc = carry[h]
                m_new = jnp.maximum(m, jnp.max(ss[h], axis=0, keepdims=True))
                p = jnp.exp(ss[h] - m_new).astype(bf16)
                a = jnp.exp(m - m_new)
                out.append((m_new, acc * a + nn(vt[h, :, ks], p)))
            return tuple(out)

        full = jnp.minimum(i * B // FW, PROMPT // FW)
        lo = jnp.where(i < PROMPT // B, (FW // B) * (i * B // FW), first_block(i, b1, b2))
        carry = tuple((jnp.full((1, B), NEG, f32), jnp.zeros((96, B), f32)) for _ in range(HPB))
        carry = lax.fori_loop(0, full, lambda j, c: step(pl.multiple_of(j * FW, FW), FW, False, c), carry)
        carry = lax.fori_loop(lo, i + 1, lambda j, c: step(pl.multiple_of(j * B, B), B, True, c), carry)
        for h in range(HPB):
            m, acc = carry[h]
            l = acc[HD:HD + 1, :]
            o_ref[i // 3, h * HD:(h + 1) * HD, pl.ds(pl.multiple_of((i % 3) * B, B), B)] = (acc[0:HD, :] / l).astype(bf16)
            lse_ref[h, :, pl.ds(q0, B)] = m + jnp.log(l)
        return 0
    lax.fori_loop(0, TOK // B, qblock, 0)

def attn_fwd(bounds, qkvt):
    nh = qkvt.shape[0] // (3 * HD)
    return pl.pallas_call(
        fwd_kernel,
        out_shape=(jax.ShapeDtypeStruct((4, nh * HD, 768), bf16), jax.ShapeDtypeStruct((nh, 1, TOK), f32)),
        grid_spec=pltpu.PrefetchScalarGridSpec(
            num_scalar_prefetch=1, grid=(nh // HPB,),
            in_specs=[pl.BlockSpec((HPB * 3 * HD, TOK), lambda h, b: (h, 0))],
            out_specs=[pl.BlockSpec((4, HPB * HD, 768), lambda h, b: (0, h, 0)), pl.BlockSpec((HPB, 1, TOK), lambda h, b: (h, 0, 0))],
            scratch_shapes=[pltpu.VMEM((HPB, TOK, 128), bf16), pltpu.VMEM((HPB, 128, TOK), bf16), pltpu.VMEM((HPB, 96, TOK), bf16)]),
        compiler_params=pltpu.CompilerParams(dimension_semantics=("arbitrary",), vmem_limit_bytes=60 << 20),
        name="attn_fwd",
    )(bounds, qkvt)

def parts3(x):
    hi = x.astype(bf16)
    r = x - hi.astype(f32)
    mid = r.astype(bf16)
    lo = (r - mid.astype(f32)).astype(bf16)
    return hi, mid, lo

def bwd_kernel(bounds, scale_ref, qkv_ref, do_ref, o_ref, lse_ref, out_ref, kp, vp, qt, dot_, qr, dor, dk, dv, dqt):
    b1, b2 = bounds[0], bounds[1]
    row16 = lax.broadcasted_iota(jnp.int32, (16, 128), 0)
    ones3 = (row16 < 3).astype(bf16)
    z32 = jnp.zeros((32, 128), bf16)
    for t in range(TOK // 128):
        sl = slice(t * 128, (t + 1) * 128)
        c, off = t // 6, (t % 6) * 128
        q = qkv_ref[0:HD, sl]; k = qkv_ref[HD:2 * HD, sl]; v = qkv_ref[2 * HD:3 * HD, sl]
        do = do_ref[c, :, off:off + 128]; o = o_ref[c, :, off:off + 128]
        delta = jnp.sum(do.astype(f32) * o.astype(f32), axis=0, keepdims=True)
        def tail(x):
            h, m, l = parts3(-x)
            return (jnp.where(row16 == 0, h.astype(f32), jnp.where(row16 == 1, m.astype(f32), jnp.where(row16 == 2, l.astype(f32), 0.0)))).astype(bf16)
        qa = jnp.concatenate([q, tail(lse_ref[0, :, sl]), z32], axis=0)
        da = jnp.concatenate([do, tail(delta), z32], axis=0)
        qt[:, sl] = qa; dot_[:, sl] = da
        qr[sl, :] = qa.T; dor[sl, :] = da.T
        kp[sl, :] = jnp.concatenate([k, ones3, z32], axis=0).T
        vp[sl, :] = jnp.concatenate([v, ones3, z32], axis=0).T
    dk[...] = jnp.zeros_like(dk); dv[...] = jnp.zeros_like(dv); dqt[...] = jnp.zeros_like(dqt)

    def block(k0, q0, kw, qw, masked):
        ks, qs = pl.ds(k0, kw), pl.ds(q0, qw)
        p = jnp.exp(nn(kp[ks, :], qt[:, qs]))
        if masked:
            qpos = q0 + lax.broadcasted_iota(jnp.int32, (1, qw), 1)
            srow = start_row(qpos, b1, b2)
            kpos = k0 + lax.broadcasted_iota(jnp.int32, (kw, qw), 0)
            p = jnp.where((kpos >= srow) & (kpos <= qpos), p, 0.0)
        ds = (p * nn(vp[ks, :], dot_[:, qs])).astype(bf16)
        dv[ks, :] += nn(p.astype(bf16), dor[qs, :])
        dk[ks, :] += nn(ds, qr[qs, :])
        dqt[:, qs] += nn(qkv_ref[HD:2 * HD, ks], ds)

    F = 512
    def full(n, _):
        block(pl.multiple_of((n % 3) * F, F), pl.multiple_of(PROMPT + (n // 3) * F, F), F, F, False)
        return 0
    lax.fori_loop(0, 9, full, 0)
    def tri(n, _):
        qb = jnp.where(n == 0, 1, 2); kb = jnp.where(n == 2, 1, 0)
        block(pl.multiple_of(kb * F, F), pl.multiple_of(qb * F, F), F, F, False)
        return 0
    lax.fori_loop(0, 3, tri, 0)
    def outer(i, _):
        lo = jnp.where(i < PROMPT // B, 2 * (i // 2), first_block(i, b1, b2))
        def inner(j, _):
            block(pl.multiple_of(j * B, B), pl.multiple_of(i * B, B), B, B, True)
            return 0
        return lax.fori_loop(lo, i + 1, inner, 0)
    lax.fori_loop(0, TOK // B, outer, 0)

    scale = scale_ref[...]
    for t in range(TOK // 128):
        sl = slice(t * 128, (t + 1) * 128)
        c, off = t // 6, (t % 6) * 128
        dq = dqt[:, sl].astype(bf16).astype(f32) * scale
        out_ref[c, 0:HD, off:off + 128] = dq.astype(bf16)
        out_ref[c, HD:2 * HD, off:off + 128] = dk[sl, :].T[0:HD, :].astype(bf16)
        out_ref[c, 2 * HD:3 * HD, off:off + 128] = dv[sl, :].T[0:HD, :].astype(bf16)

def attn_bwd(bounds, scale, qkvt, dot_, ot, lse):
    nh = qkvt.shape[0] // (3 * HD)
    return pl.pallas_call(
        bwd_kernel,
        out_shape=jax.ShapeDtypeStruct((4, nh * 3 * HD, 768), bf16),
        grid_spec=pltpu.PrefetchScalarGridSpec(
            num_scalar_prefetch=1, grid=(nh,),
            in_specs=[pl.BlockSpec((HD, 1), lambda h, b: (0, 0)),
                      pl.BlockSpec((3 * HD, TOK), lambda h, b: (h, 0)),
                      pl.BlockSpec((4, HD, 768), lambda h, b: (0, h, 0)),
                      pl.BlockSpec((4, HD, 768), lambda h, b: (0, h, 0)),
                      pl.BlockSpec((1, 1, TOK), lambda h, b: (h, 0, 0))],
            out_specs=pl.BlockSpec((4, 3 * HD, 768), lambda h, b: (0, h, 0)),
            scratch_shapes=[pltpu.VMEM((TOK, 128), bf16), pltpu.VMEM((TOK, 128), bf16), pltpu.VMEM((128, TOK), bf16), pltpu.VMEM((128, TOK), bf16),
                            pltpu.VMEM((TOK, 128), bf16), pltpu.VMEM((TOK, 128), bf16),
                            pltpu.VMEM((TOK, 128), f32), pltpu.VMEM((TOK, 128), f32), pltpu.VMEM((HD, TOK), f32)]),
        compiler_params=pltpu.CompilerParams(dimension_semantics=("arbitrary",), vmem_limit_bytes=60 << 20),
        name="attn_bwd",
    )(bounds, scale, qkvt, dot_, ot, lse)


def normalize(values, gain_vec):
    scaling = lax.rsqrt(jnp.mean(values * values, axis=-1, keepdims=True) + EPSILON)
    return (values * scaling * gain_vec, scaling)


def normalize_back(values, scaling, gain_vec, upstream):
    weighted = gain_vec * upstream
    return scaling * weighted - values * scaling**3 * jnp.mean(values * weighted, axis=-1, keepdims=True)


def by_head(query, key, value):
    rows, width = query.shape
    split = (rows, width // HD, 1, HD)
    stacked = jnp.concatenate([query.reshape(split), key.reshape(split), value.reshape(split)], axis=2)
    return stacked.reshape(rows, 3 * width)


def exchange(value):
    return lax.all_to_all(value, "heads", split_axis=0, concat_axis=0, tiled=True)


def body(
    inputs,
    cotangent,
    lengths,
    adapter_ids,
    query_weight,
    key_weight,
    value_weight,
    out_weight,
    up_weight,
    down_weight,
    attn_gain,
    mlp_gain,
    query_scale,
    adapter_in,
    adapter_out,
):
    part = lax.axis_index("heads")
    offset = part * ROWS
    ends = PROMPT + jnp.cumsum(lengths[0])
    bounds = ends[:2].astype(jnp.int32)
    ids = adapter_ids[0]
    places = offset + jnp.arange(ROWS, dtype=jnp.int32)
    token = jnp.where(
        places < PROMPT,
        ids[0],
        jnp.where(places < bounds[0], ids[1], jnp.where(places < bounds[1], ids[2], ids[3])),
    )
    chosen = (token[:, None] == (jnp.arange(AR, dtype=jnp.int32) // RANK)[None, :]).astype(f32)
    chosen2 = jnp.concatenate([chosen, chosen], axis=1)
    flat_down = jnp.transpose(adapter_in, (0, 2, 1, 3)).reshape(4, D, AR)
    flat_up = adapter_out.reshape(4, AR, D)
    gain_attn = attn_gain.astype(f32)
    gain_mlp = mlp_gain.astype(f32)
    width = LH * HD

    def mine(weight):
        return lax.dynamic_slice_in_dim(weight, part * width, width, axis=1)

    weights_mine = by_head(mine(query_weight), mine(key_weight), mine(value_weight))
    weights_mine = lax.all_gather(weights_mine, "fsdp", axis=0, tiled=True)
    rows_all = lax.all_gather(inputs[0], "heads", axis=0, tiled=True)
    w_out = lax.all_gather(out_weight, "fsdp", axis=0, tiled=True)
    w_up = lax.all_gather(up_weight, "fsdp", axis=0, tiled=True)
    w_down = lax.all_gather(down_weight, "fsdp", axis=0, tiled=True)
    weights_all = lax.all_gather(by_head(query_weight, key_weight, value_weight), "fsdp", axis=0, tiled=True)

    down_pair = jnp.concatenate([flat_down[0], flat_down[1]], axis=1)
    zero = jnp.zeros((AR, D), bf16)
    up_pair = jnp.concatenate(
        [by_head(flat_up[0], zero, zero), by_head(zero, zero, flat_up[1])], axis=0
    )
    up_mine = lax.dynamic_slice_in_dim(up_pair, part * 3 * width, 3 * width, axis=1)
    scale_row = query_scale * HD ** (-0.5)
    scale_mine = jnp.tile(jnp.concatenate([scale_row, jnp.ones((2 * HD,), f32)]), LH)[:, None]

    qkvt = qkv_project(
        bounds, ids, rows_all, gain_attn[None, :], weights_mine, down_pair, up_mine, scale_mine
    )
    mixture, logsum = attn_fwd(bounds, qkvt)
    mixed = exchange(mixture).reshape(D, ROWS)

    rows_in = inputs[0].astype(f32)
    normed, scaling_attn = normalize(rows_in, gain_attn)
    normed_low = normed.astype(bf16)
    inner_pair = (nn(normed_low, down_pair) * chosen2).astype(bf16)

    middle = rows_in + tn(mixed, w_out)
    normed_mlp, scaling_mlp = normalize(middle, gain_mlp)
    normed_mlp_low = normed_mlp.astype(bf16)
    inner_up = (nn(normed_mlp_low, flat_down[2]) * chosen).astype(bf16)
    before = nn(normed_mlp_low, w_up) + nn(inner_up, flat_up[2])
    gate = jax.nn.sigmoid(before)
    hidden_low = (before * gate).astype(bf16)
    inner_down = (nn(hidden_low, flat_down[3]) * chosen).astype(bf16)
    outputs = (middle + (nn(hidden_low, w_down) + nn(inner_down, flat_up[3]))).astype(bf16)

    upstream = cotangent[0].astype(f32)
    grad_after = cotangent[0]
    spread_down = (nt(grad_after, flat_up[3]) * chosen).astype(bf16)
    grad_hidden = nt(grad_after, w_down) + nt(spread_down, flat_down[3])
    grad_before = (grad_hidden * gate * (1.0 + before * (1.0 - gate))).astype(bf16)
    spread_up = (nt(grad_before, flat_up[2]) * chosen).astype(bf16)
    grad_normed_mlp = nt(grad_before, w_up) + nt(spread_up, flat_down[2])
    grad_middle = upstream + normalize_back(middle, scaling_mlp, gain_mlp, grad_normed_mlp)
    grad_branch = grad_middle.astype(bf16)
    grad_mixed = nt(w_out, grad_branch).astype(bf16).reshape(PARTS, width, ROWS)
    grad_heads = exchange(grad_mixed)

    first_mlp = jnp.stack([tn(normed_mlp_low, spread_up), tn(hidden_low, spread_down)]).astype(bf16)
    second_mlp = jnp.stack([tn(inner_up, grad_before), tn(inner_down, grad_after)]).astype(bf16)
    first_mlp, second_mlp = lax.psum((first_mlp, second_mlp), ("heads", "fsdp"))

    grad_qkv = attn_bwd(bounds, scale_row[:, None], qkvt, grad_heads, mixture, logsum)
    grad_rows = exchange(grad_qkv).reshape(3 * D, ROWS)

    spread_pair = (lax.dot_general(grad_rows, up_pair, (((0,), (1,)), ((), ())), preferred_element_type=f32) * chosen2).astype(bf16)
    first_attn = tn(normed_low, spread_pair).astype(bf16)
    grad_split = grad_rows.reshape(HEADS, 3, HD, ROWS)
    second_query = lax.dot_general(inner_pair[:, :AR], grad_split[:, 0], (((0,), (2,)), ((), ())), preferred_element_type=f32)
    second_value = lax.dot_general(inner_pair[:, AR:], grad_split[:, 2], (((0,), (2,)), ((), ())), preferred_element_type=f32)
    second_attn = jnp.stack([second_query.reshape(AR, D), second_value.reshape(AR, D)]).astype(bf16)
    first_attn, second_attn = lax.psum((first_attn, second_attn), ("heads", "fsdp"))
    grad_normed = lax.dot_general(
        grad_rows, weights_all, (((0,), (1,)), ((), ())), preferred_element_type=f32
    ) + nt(spread_pair, down_pair)
    grad_inputs = grad_middle + normalize_back(rows_in, scaling_attn, gain_attn, grad_normed)

    first = jnp.stack([first_attn[:, :AR], first_attn[:, AR:], first_mlp[0], first_mlp[1]]).astype(f32)
    second = jnp.concatenate([second_attn, second_mlp]).astype(f32)
    grad_first = jnp.transpose(first.reshape(4, D, ADAPTERS, RANK), (0, 2, 1, 3))
    grad_second = second.reshape(4, ADAPTERS, RANK, D)
    return (outputs[None], grad_inputs[None], grad_first, grad_second)


def solution(mesh):
    placed = (
        P("fsdp", "heads", None),
        P("fsdp", "heads", None),
        P("fsdp", None),
        P("fsdp", None),
        P("fsdp", None),
        P("fsdp", None),
        P("fsdp", None),
        P("fsdp", None),
        P("fsdp", None),
        P("fsdp", None),
        P(),
        P(),
        P(),
        P(),
        P(),
    )
    return jax.shard_map(
        body,
        mesh=mesh,
        in_specs=placed,
        out_specs=(P("fsdp", "heads", None), P("fsdp", "heads", None), P(), P()),
        check_vma=False,
    )
```

time: 1310 us -> 653 us (0.50)
  matrix products: 603 us -> 78.9 us
  other arithmetic: 252 us -> 24.7 us
  Pallas kernels: 0 us -> 148 us
  local copies, waits for them, and re-layouts: 133 us -> 34.4 us
  waiting for transfers between devices: 256 us -> 330 us
  starting transfers between devices: 35.9 us -> 14.7 us
    dot_general x78 -> x25, matrix products: 603 us -> 78.9 us  [the longest x8 31.9 us: nt(): lax.dot_general(a, b, (((1,), (1,)), ((), ())), preferred_element_type=f32)]
    pallas_call x0 -> x3, Pallas kernels: none -> 148 us  [the longest x1 80.7 us: attn_bwd(): pl.pallas_call(bwd_kernel, out_shape=jax.ShapeDtypeStruct((4, nh * 3 * HD...]
    convert_element_type x13 -> x4, other arithmetic: 139 us -> 3.34 us  [the longest x1 2.95 us: body(): second = jnp.concatenate([second_attn, second_mlp]).astype(f32)]
    reduce_sum x9 -> x0, other arithmetic: 71.4 us -> none  [the longest x6 70.7 us: one_block(): row_total = jnp.sum(exponent, axis=-1, keepdims=True)]
    all_to_all x8 -> x3, waiting for transfers between devices: 51.2 us -> 83.1 us  [exchange(): lax.all_to_all(value, 'heads', split_axis=0, concat_axis=0, tiled=True)]
    all_gather x6, waiting for transfers between devices: 80.9 us -> 112 us  [the longest x1 84 us: body(): rows_all = lax.all_gather(inputs[0], 'heads', axis=0, tiled=True)]
    and x12 -> x0, other arithmetic: 29.6 us -> none  [one_block(): (places[None, :] <= row_places[:, None]) & (prompt_col[None, :] | (segmen...]
    convert_element_type x9 -> x1, local copies, waits for them, and re-layouts: 33.4 us -> 4.02 us  [body(): grad_mixed = nt(w_out, grad_branch).astype(bf16).reshape(PARTS, width, ROWS)]
  transfers between devices with their start and end apart: 15 -> 10, of which waited for: 8 -> 7; matrix products, arithmetic and copies ran while one was open for 31% -> 15% of each run, Pallas kernels for 0% -> 23%
where the time goes in v1:
time: 653 us; the launch traced here: 646 us
  waiting for transfers between devices  330 us (51%)
  Pallas kernels  148 us (23%)
  matrix products  78.9 us (12%)
  local copies, waits for them, and re-layouts  34.4 us (5%)
  other arithmetic  24.7 us (4%)
  between operations  15.1 us (2%)
  starting transfers between devices  14.7 us (2%)
    psum x1, waiting for transfers between devices, body(): first_mlp, second_mlp = lax.psum((first_mlp, second_mlp), ('heads', 'fsdp'))  133 us
    all_gather x1, waiting for transfers between devices, body(): rows_all = lax.all_gather(inputs[0], 'heads', axis=0, tiled=True)  84 us
    all_to_all x3, waiting for transfers between devices, exchange(): lax.all_to_all(value, 'heads', split_axis=0, concat_axis=0, tiled=True)  83.1 us
    pallas_call x1, Pallas kernels, attn_bwd(): pl.pallas_call(bwd_kernel, out_shape=jax.ShapeDtypeStruct((4, nh * 3 * HD...  80.7 us
    pallas_call x1, Pallas kernels, attn_fwd(): pl.pallas_call(fwd_kernel, out_shape=(jax.ShapeDtypeStruct((4, nh * HD, 7...  46 us
    dot_general x8, matrix products, nt(): lax.dot_general(a, b, (((1,), (1,)), ((), ())), preferred_element_type=f32)  31.9 us
    pallas_call x1, Pallas kernels, qkv_project(): pl.pallas_call(qkv_kernel, out_shape=jax.ShapeDtypeStruct((width, TOK), b...  21.4 us
    dot_general x7, matrix products, nn(): lax.dot_general(a, b, (((1,), (0,)), ((), ())), preferred_element_type=f32)  16.9 us
  transfers between devices with their start and end apart: 10, of which 7 were waited for; matrix products, arithmetic and copies ran while one was open for 15% of the time, Pallas kernels for 23%

profile of v1, /device:TPU:9, one launch (start us, length us, event | category | flops | bytes accessed | tf_op | source)
XLA Modules:
  0.0 646.3 jit_solution(18322840231736047463)
XLA Ops:
  17.4 2.1 copy.57
  22.4 2.2 fusion.53
  33.2 13.3 %all-gather.8.cloned.1.call-done.w_ref = bf16[1280,960]{1,0:T(8,128)(2,1)} async-done(((bf16[160,960]{1,0:T(8,128)(2,1)}), bf16[1280,960]{1,0:T(8,128)(2,1)}) %all-gather.8.cloned.1.call-update) | async-done | bytes 2457616 | tf_op jit(solution)/shard_map/all_gather | solution.py:304
  46.5 84.0 %all-gather.18.cloned.1.call-done = bf16[1,3072,1280]{2,1,0:T(8,128)(2,1)} async-done(((bf16[1,768,1280]{2,1,0:T(8,128)(2,1)}), bf16[1,3072,1280]{2,1,0:T(8,128)(2,1)}) %all-gather.18.cloned.1.call-update) | async-done | bytes 7864336 | tf_op jit(solution)/shard_map/all_gather | solution.py:305
  130.5 21.4 %qkv_project.1.qkv_ref = bf16[960,3072]{1,0:T(8,128)(2,1)} custom-call(s32[2]{0:T(128)} %slice_bitcast_fusion.bounds, s32[4]{0:T(128)} %bitcast.153, bf16[3072,1280]{1,0:T(8,128)(2,1)} %bitcast.154, f32[1,1280]{1,0:T(1,128)} %broadcast_in_dim.38.gain_ref, bf16[1280,960]{1,0:T(8,128)(2,1)} %all-gather.8.cloned.1.call-done.w_ref, ...), custom_call_target="tpu_custom_call" | custom-call | flops 7549747200 | bytes 7864320 | tf_op jit(solution)/shard_map/qkv_project/pallas_call | solution.py:54
  151.9 46.0 %attn_fwd.1 = (bf16[4,320,768]{2,1,0:T(8,128)(2,1)}, f32[4,1,3072]{2,1,0:T(1,128)}) custom-call(s32[2]{0:T(128)} %slice_bitcast_fusion.bounds, bf16[960,3072]{1,0:T(8,128)(2,1)} %qkv_project.1.qkv_ref), custom_call_target="tpu_custom_call" | custom-call | tf_op jit(solution)/shard_map/attn_fwd/pallas_call | solution.py:141
  197.9 4.8 all-to-all-start
  204.0 3.7 select_select_fusion
  209.5 7.3 %fusion.27 = f32[768,1280]{1,0:T(8,128)} fusion(bf16[1280,1280]{1,0:T(8,128)(2,1)} %all-gather.14.cloned.1.call-done, bf16[1,768,1280]{2,1,0:T(8,128)(2,1)} %param.16), kind=kOutput, calls=%fused_computation.56 | convolution fusion | flops 2516582400 | bytes 9175040 | tf_op jit(solution)/shard_map/dot_general | solution.py:25
  216.8 8.8 %all-to-all-done = bf16[4,320,768]{2,1,0:T(8,128)(2,1)} async-done(((bf16[4,320,768]{2,1,0:T(8,128)(2,1)}), bf16[4,320,768]{2,1,0:T(8,128)(2,1)}, u32[]{:S(2)}, u32[]{:S(2)}) %all-to-all-start) | async-done | bytes 1966112 | tf_op jit(solution)/shard_map/all_to_all | solution.py:261
  225.5 5.6 multiply_reduce_fusion.1
  236.1 14.6 %all-gather.12.cloned.1.call-done = bf16[1280,1280]{1,0:T(8,128)(2,1)} async-done(((bf16[160,1280]{1,0:T(8,128)(2,1)}), bf16[1280,1280]{1,0:T(8,128)(2,1)}) %all-gather.12.cloned.1.call-update) | async-done | bytes 3276816 | tf_op jit(solution)/shard_map/all_gather | solution.py:307
  250.6 5.3 fusion.58
  255.9 2.6 multiply_convert_fusion
  260.9 12.3 %fusion.60 = f32[768,1280]{1,0:T(8,128)S(1)} fusion(bf16[768,1280]{1,0:T(8,128)(2,1)S(1)} %fusion.13, bf16[1280,1280]{1,0:T(8,128)(2,1)S(1)} %copy-done.34), kind=kOutput, calls=%fused_computation.113 | convolution fusion | flops 2516582400 | bytes 9175040 | tf_op jit(solution)/shard_map/dot_general | solution.py:25
  277.3 4.3 fusion.15
  281.6 4.0 copy.52
  285.6 4.4 all-to-all-start.1
  290.8 22.7 %all-to-all-done.1.do_ref = bf16[4,320,768]{2,1,0:T(8,128)(2,1)} async-done(((bf16[4,320,768]{2,1,0:T(8,128)(2,1)}), bf16[4,320,768]{2,1,0:T(8,128)(2,1)}, u32[]{:S(2)}, u32[]{:S(2)}) %all-to-all-start.1) | async-done | bytes 1966112 | tf_op jit(solution)/shard_map/all_to_all | solution.py:261
  313.5 80.7 %attn_bwd.1 = bf16[4,960,768]{2,1,0:T(8,128)(2,1)} custom-call(s32[2]{0:T(128)} %slice_bitcast_fusion.bounds, f32[80,1]{1,0:T(8,128)} %copy.53.scale_ref, bf16[960,3072]{1,0:T(8,128)(2,1)} %qkv_project.1.qkv_ref, bf16[4,320,768]{2,1,0:T(8,128)(2,1)} %all-to-all-done.1.do_ref, bf16[4,320,768]{2,1,0:T(8,128)(2,1)} %get-tuple-element.6.o_ref, ...), custom_call_target="tpu_custom_call" | custom-call | tf_op jit(solution)/shard_map/attn_bwd/pallas_call | solution.py:224
  394.2 5.2 all-to-all-start.2
  400.3 2.2 fusion.21
  402.6 2.4 fusion.37
  408.2 2.7 fusion.59
  412.9 51.7 %all-to-all-done.2 = bf16[4,960,768]{2,1,0:T(8,128)(2,1)} async-done(((bf16[4,960,768]{2,1,0:T(8,128)(2,1)}), bf16[4,960,768]{2,1,0:T(8,128)(2,1)}, u32[]{:S(2)}, u32[]{:S(2)}) %all-to-all-start.2) | async-done | bytes 5898272 | tf_op jit(solution)/shard_map/all_to_all | solution.py:261
  464.6 5.4 fusion.31
  470.0 12.1 %fusion.61 = f32[768,1280]{1,0:T(8,128)S(1)} fusion(bf16[3840,768]{1,0:T(8,128)(2,1)} %bitcast.28, bf16[1280,3840]{1,0:T(8,128)(2,1)} %all-gather.16.cloned.1.call-done), kind=kOutput, calls=%fused_computation.114 | convolution fusion | flops 7549747200 | bytes 19660800 | tf_op jit(solution)/shard_map/dot_general | solution.py:367
  482.1 3.2 fusion.5
  487.8 2.4 fusion.52
  492.8 7.3 %fusion.9 = f32[1,768,1280]{2,1,0:T(8,128)} fusion(f32[768,1280]{1,0:T(8,128)} %get-tuple-element.44, bf16[1,768,1280]{2,1,0:T(8,128)(2,1)S(1)} %copy-done.3, f32[768]{0:T(1024)S(1)} %broadcast_multiply_fusion, f32[768]{0:T(1024)S(1)} %get-tuple-element.27, f32[768]{0:T(1024)S(1)} %get-tuple-element.26, f32[768]{0:T(1024)S(1)} %broadcast_multiply_fusion.1, ...), kind=kLoop, calls=%fused_computation.19 | loop fusion | flops 11796480 | bytes 19679232 | tf_op jit(solution)/shard_map/broadcast_in_dim | solution.py:376
  500.1 133.0 %all-reduce.6.cloned.1.call-done = (bf16[2,1280,8,16]{1,3,2,0:T(8,128)(2,1)}, bf16[1280,256]{1,0:T(8,128)(2,1)}, bf16[2,8,16,1280]{3,2,1,0:T(8,128)(2,1)}, bf16[2,8,16,1280]{3,2,1,0:T(8,128)(2,1)}) async-done(((bf16[2,1280,8,16]{1,3,2,0:T(8,128)(2,1)}, bf16[1280,256]{1,0:T(8,128)(2,1)}, bf16[2,8,16,1280]{3,2,1,0:T(8,128)(2,1)}, bf16[2,8,16,1280]{3,2,1,0:T(8,128)(2,1)}), (bf16[2,1280,8,16]{1,3,2,0:T(8,128)(2,1)}, ...) | async-done | bytes 2621456 | tf_op jit(solution)/shard_map/psum | solution.py:355
  634.6 2.9 maximum_convert_fusion
  (158 shorter events, 50.7 us)
Async XLA Ops:
  7.2 39.4 %all-gather.8.cloned.1.call-start = ((), (), s32[]{:S(2)}) async-start(), calls=%async_computation.3 | async-start | bytes 2949120 | tf_op jit(solution)/shard_map/all_gather | solution.py:304
  9.7 4.6 copy-start.19
  10.3 4.3 copy-start.20
  10.7 4.1 copy-start.21
  11.6 118.9 %all-gather.18.cloned.1.call-start = ((), (), s32[]{:S(2)}) async-start(), calls=%async_computation.8 | async-start | bytes 9830400 | tf_op jit(solution)/shard_map/all_gather | solution.py:305
  12.4 197.1 %all-gather.14.cloned.1.call-start = ((), (), s32[]{:S(2)}) async-start(), calls=%async_computation.6 | async-start | bytes 3686400 | tf_op jit(solution)/shard_map/all_gather | solution.py:308
  13.1 203.7 %all-gather.10.cloned.1.call-start = ((), (), s32[]{:S(2)}) async-start(), calls=%async_computation.4 | async-start | bytes 3686400 | tf_op jit(solution)/shard_map/all_gather | solution.py:306
  13.7 236.9 %all-gather.12.cloned.1.call-start = ((), (), s32[]{:S(2)}) async-start(), calls=%async_computation.5 | async-start | bytes 3686400 | tf_op jit(solution)/shard_map/all_gather | solution.py:307
  14.3 455.7 %all-gather.16.cloned.1.call-start = ((), (), s32[]{:S(2)}) async-start(), calls=%async_computation.7 | async-start | bytes 11059200 | tf_op jit(solution)/shard_map/all_gather | solution.py:309
  28.6 123.3 %copy-start.10 = (bf16[128,3840]{1,0:T(8,128)(2,1)}, bf16[128,3840]{1,0:T(8,128)(2,1)S(1)}, u32[]{:S(2)}) copy-start(bf16[128,3840]{1,0:T(8,128)(2,1)S(1)} %copy.50) | copy-start | bytes 2949124
  197.9 4.9 copy-start.32
  197.9 5.5 copy-start.31
  197.9 9.9 %copy-start.7 = (bf16[1,768,1280]{2,1,0:T(8,128)(2,1)S(1)}, bf16[1,768,1280]{2,1,0:T(8,128)(2,1)}, u32[]{:S(2)}) copy-start(bf16[1,768,1280]{2,1,0:T(8,128)(2,1)} %param.16) | copy-start | bytes 5898244
  197.9 27.6 %all-to-all-start = ((bf16[4,320,768]{2,1,0:T(8,128)(2,1)}), bf16[4,320,768]{2,1,0:T(8,128)(2,1)}, u32[]{:S(2)}, u32[]{:S(2)}) async-start(bf16[4,320,768]{2,1,0:T(8,128)(2,1)} %get-tuple-element.6.o_ref), calls=%async_computation | async-start | bytes 3932160 | tf_op jit(solution)/shard_map/all_to_all | solution.py:261
  209.4 49.1 %copy-start.26 = (bf16[768,128]{1,0:T(8,128)(2,1)}, bf16[768,128]{1,0:T(8,128)(2,1)S(1)}, u32[]{:S(2)}) copy-start(bf16[768,128]{1,0:T(8,128)(2,1)S(1)} %fusion.39) | copy-start | bytes 589828
  209.5 16.1 %copy-start.3 = (bf16[1,768,1280]{2,1,0:T(8,128)(2,1)S(1)}, bf16[1,768,1280]{2,1,0:T(8,128)(2,1)}, u32[]{:S(2)}) copy-start(bf16[1,768,1280]{2,1,0:T(8,128)(2,1)} %param.15) | copy-start | bytes 5898244
  250.6 5.3 copy-start.25
  250.6 5.3 copy-start.28
  260.2 13.0 %copy-start.14 = (bf16[768,1280]{1,0:T(8,128)(2,1)}, bf16[768,1280]{1,0:T(8,128)(2,1)S(1)}, u32[]{:S(2)}) copy-start(bf16[768,1280]{1,0:T(8,128)(2,1)S(1)} %fusion.13) | copy-start | bytes 5898244
  260.9 12.3 %copy-start.1 = (f32[768,1280]{1,0:T(8,128)S(1)}, f32[768,1280]{1,0:T(8,128)}, u32[]{:S(2)}) copy-start(f32[768,1280]{1,0:T(8,128)} %copy-done) | copy-start | bytes 11796484
  260.9 12.3 %copy-start.17 = (bf16[1,1280,8,16]{1,3,2,0:T(8,128)(2,1)S(1)}, bf16[1,1280,8,16]{1,3,2,0:T(8,128)(2,1)}, u32[]{:S(2)}) copy-start(bf16[1,1280,8,16]{1,3,2,0:T(8,128)(2,1)} %get-tuple-element.21) | copy-start | bytes 983044
  273.3 4.0 copy-start.11
  285.6 27.8 %all-to-all-start.1 = ((bf16[4,320,768]{2,1,0:T(8,128)(2,1)}), bf16[4,320,768]{2,1,0:T(8,128)(2,1)}, u32[]{:S(2)}, u32[]{:S(2)}) async-start(bf16[4,320,768]{2,1,0:T(8,128)(2,1)} %bitcast.127), calls=%async_computation.1 | async-start | bytes 3932160 | tf_op jit(solution)/shard_map/all_to_all | solution.py:261
  394.2 70.4 %all-to-all-start.2 = ((bf16[4,960,768]{2,1,0:T(8,128)(2,1)}), bf16[4,960,768]{2,1,0:T(8,128)(2,1)}, u32[]{:S(2)}, u32[]{:S(2)}) async-start(bf16[4,960,768]{2,1,0:T(8,128)(2,1)} %attn_bwd.1), calls=%async_computation.2 | async-start | bytes 11796480 | tf_op jit(solution)/shard_map/all_to_all | solution.py:261
  399.4 233.6 %all-reduce.6.cloned.1.call-start = ((), (), s32[]{:S(2)}) async-start(), calls=%async_computation.9 | async-start | bytes 5242880 | tf_op jit(solution)/shard_map/psum | solution.py:355
  399.5 5.5 copy-start.9
  400.3 5.1 copy-start.13
  400.3 5.1 copy-start.27
  411.0 53.6 %copy-start.29 = (pred[768,128]{1,0:T(32,128)(4,1)S(1)}, pred[768,128]{1,0:T(32,128)(4,1)}, u32[]{:S(2)}) copy-start(pred[768,128]{1,0:T(32,128)(4,1)} %broadcast_compare_fusion) | copy-start | bytes 294916
  470.0 12.1 %copy-start.12 = (bf16[1280,128]{1,0:T(8,128)(2,1)S(1)}, bf16[1280,128]{1,0:T(8,128)(2,1)}, u32[]{:S(2)}) copy-start(bf16[1280,128]{1,0:T(8,128)(2,1)} %copy.45) | copy-start | bytes 983044
  470.0 12.1 %copy-start.23 = (bf16[768,256]{1,0:T(8,128)(2,1)S(1)}, bf16[768,256]{1,0:T(8,128)(2,1)}, u32[]{:S(2)}) copy-start(bf16[768,256]{1,0:T(8,128)(2,1)} %fusion.31) | copy-start | bytes 1179652
  633.1 4.5 copy-start.22
  (16 other events, 42.0 us)
Sparse Core Ops, SparseCore 0:
  11.7 34.7 all-gather.7
  48.4 82.1 all-gather.17
  132.2 38.9 all-gather.13
  172.7 38.1 all-gather.9
  212.4 38.1 all-gather.11
  252.1 90.9 all-gather.15
  492.9 140.1 all-reduce.5

commit v2 on v1

v2 whole, which is shorter than its diff:
```python
import jax
import jax.numpy as jnp
from jax import lax
from jax.experimental import pallas as pl
from jax.experimental.pallas import tpu as pltpu
from jax.sharding import PartitionSpec as P

D = 1280
HEADS = 16
HD = 80
RANK = 16
ADAPTERS = 8
AR = ADAPTERS * RANK
TOK = 3072
PROMPT = 1536
ROWS = 768
QB = 384
PARTS = TOK // ROWS
LH = HEADS // PARTS
EPSILON = 1e-06
B = 256
f32, bf16 = jnp.float32, jnp.bfloat16


def nt(a, b):
    return lax.dot_general(a, b, (((1,), (1,)), ((), ())), preferred_element_type=f32)


def tn(a, b):
    return lax.dot_general(a, b, (((0,), (0,)), ((), ())), preferred_element_type=f32)


def nn(a, b):
    return lax.dot_general(a, b, (((1,), (0,)), ((), ())), preferred_element_type=f32)

def start_row(qpos, b1, b2):
    return jnp.where(qpos < PROMPT, 0, jnp.where(qpos < b1, PROMPT, jnp.where(qpos < b2, b1, b2)))

def first_block(i, b1, b2):
    q0 = i * B
    return jnp.where(q0 < b1, PROMPT, jnp.where(q0 < b2, b1, b2)) // B


def token_adapter(pos, meta):
    return jnp.where(
        pos < PROMPT, meta[2], jnp.where(pos < meta[0], meta[3], jnp.where(pos < meta[1], meta[4], meta[5]))
    )


def qkv_kernel(meta, first, x_ref, gain_ref, wt_ref, down_ref, up_ref, scale_ref, *refs):
    out_ref, normed_ref, inner_ref = refs[-3:]
    x = x_ref[...].astype(f32)
    q = lax.rsqrt(jnp.mean(x * x, axis=1, keepdims=True) + EPSILON)
    normed = (x * q * gain_ref[...]).astype(bf16)
    normed_ref[...] = normed
    pos = (first[0] + pl.program_id(0)) * QB + lax.broadcasted_iota(jnp.int32, (QB, 1), 0)
    lane = lax.broadcasted_iota(jnp.int32, (QB, 2 * AR), 1)
    chosen = (lane % AR) // RANK == token_adapter(pos, meta)
    inner = jnp.where(chosen, nn(normed, down_ref[...]), 0.0).astype(bf16)
    inner_ref[...] = inner
    out = nt(wt_ref[...], normed) + nt(up_ref[...], inner)
    out_ref[...] = (out * scale_ref[...]).astype(bf16)


def qkv_project(meta, first, x, gain, wt, down, up, scale, done):
    width = wt.shape[0]
    whole = lambda shape: pl.BlockSpec(shape, lambda i, *_: (0, 0))
    return pl.pallas_call(
        qkv_kernel,
        out_shape=(
            jax.ShapeDtypeStruct((width, TOK), bf16),
            jax.ShapeDtypeStruct((TOK, D), bf16),
            jax.ShapeDtypeStruct((TOK, 2 * AR), bf16),
        ),
        grid_spec=pltpu.PrefetchScalarGridSpec(
            num_scalar_prefetch=2,
            grid=(x.shape[0] // QB,),
            in_specs=[
                pl.BlockSpec((QB, D), lambda i, *_: (i, 0)),
                whole((1, D)),
                whole((width, D)),
                whole((D, 2 * AR)),
                whole((width, 2 * AR)),
                whole((width, 1)),
            ]
            + [pl.BlockSpec(memory_space=pl.ANY)] * len(done),
            out_specs=[
                pl.BlockSpec((width, QB), lambda i, m, first: (0, first[0] + i)),
                pl.BlockSpec((QB, D), lambda i, m, first: (first[0] + i, 0)),
                pl.BlockSpec((QB, 2 * AR), lambda i, m, first: (first[0] + i, 0)),
            ],
        ),
        input_output_aliases={8 + i: i for i in range(len(done))},
        compiler_params=pltpu.CompilerParams(dimension_semantics=("arbitrary",), vmem_limit_bytes=60 << 20),
        cost_estimate=pl.CostEstimate(
            flops=2 * x.shape[0] * D * (width + 2 * AR), bytes_accessed=2 * x.shape[0] * D + 2 * D * width, transcendentals=0
        ),
        name="qkv_project",
    )(meta, first, x, gain, wt, down, up, scale, *done)


def adapter_kernel(meta, *refs):
    grad_refs, (normed_ref, inner_ref, up_ref, first_ref, second_ref) = refs[: LH * PARTS], refs[LH * PARTS :]

    @pl.when(pl.program_id(0) == 0)
    def _():
        first_ref[...] = jnp.zeros_like(first_ref)
        second_ref[...] = jnp.zeros_like(second_ref)

    for m in range(PARTS):

        @pl.when(pl.program_id(0) == m)
        def _(m=m):
            grads = [grad_refs[h * PARTS + m][...] for h in range(LH)]
            spread = nn(up_ref[0], grads[0])
            for h in range(1, LH):
                spread += nn(up_ref[h], grads[h])
            pos = (meta[6] ^ m) * ROWS + lax.broadcasted_iota(jnp.int32, (1, ROWS), 1)
            rank = lax.broadcasted_iota(jnp.int32, (2 * AR, ROWS), 0)
            chosen = (rank % AR) // RANK == token_adapter(pos, meta)
            spread = jnp.where(chosen, spread, 0.0).astype(bf16)
            first = nn(spread, normed_ref[...])
            for c in range(D // 128):
                first_ref[c] += first[:, c * 128 : (c + 1) * 128]
            for h in range(LH):
                second_ref[h, 0] += nn(grads[h][:HD], inner_ref[:, :AR])
                second_ref[h, 1] += nn(grads[h][2 * HD :], inner_ref[:, AR:])


def adapter_grads(meta, grads, normed, inner, up):
    return pl.pallas_call(
        adapter_kernel,
        out_shape=(jax.ShapeDtypeStruct((D // 128, 2 * AR, 128), f32), jax.ShapeDtypeStruct((LH, 2, HD, AR), f32)),
        grid_spec=pltpu.PrefetchScalarGridSpec(
            num_scalar_prefetch=1,
            grid=(PARTS,),
            in_specs=[pl.BlockSpec((3 * HD, ROWS), lambda i, m: (0, 0))] * (LH * PARTS)
            + [
                pl.BlockSpec((ROWS, D), lambda i, m: (m[6] ^ i, 0)),
                pl.BlockSpec((ROWS, 2 * AR), lambda i, m: (m[6] ^ i, 0)),
                pl.BlockSpec((LH, 2 * AR, 3 * HD), lambda i, m: (0, 0, 0)),
            ],
            out_specs=[
                pl.BlockSpec((D // 128, 2 * AR, 128), lambda i, m: (0, 0, 0)),
                pl.BlockSpec((LH, 2, HD, AR), lambda i, m: (0, 0, 0, 0)),
            ],
        ),
        compiler_params=pltpu.CompilerParams(dimension_semantics=("arbitrary",), vmem_limit_bytes=60 << 20),
        cost_estimate=pl.CostEstimate(flops=4 * TOK * D * 2 * AR, bytes_accessed=20 << 20, transcendentals=0),
        name="adapter_grads",
    )(meta, *grads, normed, inner, up)


HPB = 4
NEG = -1e30
FW = 512


def fwd_kernel(bounds, qkv_ref, o_ref, lse_ref, kp, qt, vt):
    b1, b2 = bounds[0], bounds[1]
    zpad = jnp.zeros((128 - HD, 128), bf16)
    for h in range(HPB):
        r = h * 3 * HD
        qt[h, 0:HD, :] = qkv_ref[r:r + HD, :]
        qt[h, HD:128, :] = jnp.zeros((128 - HD, TOK), bf16)
        vt[h, 0:HD, :] = qkv_ref[r + 2 * HD:r + 3 * HD, :]
        vt[h, HD:96, :] = (lax.broadcasted_iota(jnp.int32, (16, TOK), 0) == 0).astype(bf16)
        for t in range(TOK // 128):
            kt = qkv_ref[r + HD:r + 2 * HD, t * 128:(t + 1) * 128]
            kp[h, t * 128:(t + 1) * 128, :] = jnp.concatenate([kt, zpad], axis=0).T

    def qblock(i, _):
        q0 = pl.multiple_of(i * B, B)
        qpos = q0 + lax.broadcasted_iota(jnp.int32, (1, B), 1)
        srow = start_row(qpos, b1, b2)

        def step(k0, width, masked, carry):
            ks = pl.ds(k0, width)
            ss = [nn(kp[h, ks, :], qt[h, :, pl.ds(q0, B)]) for h in range(HPB)]
            if masked:
                kpos = k0 + lax.broadcasted_iota(jnp.int32, (width, B), 0)
                ok = (kpos >= srow) & (kpos <= qpos)
                ss = [jnp.where(ok, s, NEG) for s in ss]
            out = []
            for h in range(HPB):
                m, acc = carry[h]
                m_new = jnp.maximum(m, jnp.max(ss[h], axis=0, keepdims=True))
                p = jnp.exp(ss[h] - m_new).astype(bf16)
                a = jnp.exp(m - m_new)
                out.append((m_new, acc * a + nn(vt[h, :, ks], p)))
            return tuple(out)

        full = jnp.minimum(i * B // FW, PROMPT // FW)
        lo = jnp.where(i < PROMPT // B, (FW // B) * (i * B // FW), first_block(i, b1, b2))
        carry = tuple((jnp.full((1, B), NEG, f32), jnp.zeros((96, B), f32)) for _ in range(HPB))
        carry = lax.fori_loop(0, full, lambda j, c: step(pl.multiple_of(j * FW, FW), FW, False, c), carry)
        carry = lax.fori_loop(lo, i + 1, lambda j, c: step(pl.multiple_of(j * B, B), B, True, c), carry)
        for h in range(HPB):
            m, acc = carry[h]
            l = acc[HD:HD + 1, :]
            o_ref[i // 3, h * HD:(h + 1) * HD, pl.ds(pl.multiple_of((i % 3) * B, B), B)] = (acc[0:HD, :] / l).astype(bf16)
            lse_ref[h, :, pl.ds(q0, B)] = m + jnp.log(l)
        return 0
    lax.fori_loop(0, TOK // B, qblock, 0)

def attn_fwd(bounds, qkvt):
    nh = qkvt.shape[0] // (3 * HD)
    return pl.pallas_call(
        fwd_kernel,
        out_shape=(jax.ShapeDtypeStruct((4, nh * HD, 768), bf16), jax.ShapeDtypeStruct((nh, 1, TOK), f32)),
        grid_spec=pltpu.PrefetchScalarGridSpec(
            num_scalar_prefetch=1, grid=(nh // HPB,),
            in_specs=[pl.BlockSpec((HPB * 3 * HD, TOK), lambda h, b: (h, 0))],
            out_specs=[pl.BlockSpec((4, HPB * HD, 768), lambda h, b: (0, h, 0)), pl.BlockSpec((HPB, 1, TOK), lambda h, b: (h, 0, 0))],
            scratch_shapes=[pltpu.VMEM((HPB, TOK, 128), bf16), pltpu.VMEM((HPB, 128, TOK), bf16), pltpu.VMEM((HPB, 96, TOK), bf16)]),
        compiler_params=pltpu.CompilerParams(dimension_semantics=("arbitrary",), vmem_limit_bytes=60 << 20),
        cost_estimate=pl.CostEstimate(flops=40 * 10**9, bytes_accessed=10 << 20, transcendentals=0),
        name="attn_fwd",
    )(bounds, qkvt)

def parts3(x):
    hi = x.astype(bf16)
    r = x - hi.astype(f32)
    mid = r.astype(bf16)
    lo = (r - mid.astype(f32)).astype(bf16)
    return hi, mid, lo

def bwd_kernel(meta, scale_ref, qkv_ref, *refs):
    do_ref, o_ref, lse_ref = refs[:3]
    out_refs = refs[3 : 3 + PARTS]
    kp, vp, qt, dot, qr, dor, dk, dv, dqt = refs[3 + PARTS :]
    b1, b2, part = meta[0], meta[1], meta[6]
    row16 = lax.broadcasted_iota(jnp.int32, (16, 128), 0)
    ones3 = (row16 < 3).astype(bf16)
    pad = jnp.zeros((32, 128), bf16)
    scale = scale_ref[...]

    def tail(x):
        hi, mid, lo = parts3(-x)
        rest = jnp.where(row16 == 1, mid.astype(f32), jnp.where(row16 == 2, lo.astype(f32), 0.0))
        return jnp.where(row16 == 0, hi.astype(f32), rest).astype(bf16)

    for m in range(PARTS):
        chunk = part ^ m

        @pl.loop(0, 2)
        def _(step, m=m, chunk=chunk):
            for t in range(3):
                off = pl.multiple_of(step * 384 + t * 128, 128)
                sl, here = pl.ds(pl.multiple_of(chunk * ROWS + off, 128), 128), pl.ds(off, 128)
                q, k, v = qkv_ref[0:HD, sl], qkv_ref[HD : 2 * HD, sl], qkv_ref[2 * HD : 3 * HD, sl]
                do, o = do_ref[chunk, :, here], o_ref[chunk, :, here]
                delta = jnp.sum(do.astype(f32) * o.astype(f32), axis=0, keepdims=True)
                qa = jnp.concatenate([q, tail(lse_ref[0, :, sl]), pad], axis=0)
                da = jnp.concatenate([do, tail(delta), pad], axis=0)
                qt[:, sl] = qa
                dot[:, sl] = da
                qr[sl, :] = qa.T
                dor[sl, :] = da.T
                kp[sl, :] = jnp.concatenate([k, ones3, pad], axis=0).T
                vp[sl, :] = jnp.concatenate([v, ones3, pad], axis=0).T

    dk[...] = jnp.zeros_like(dk)
    dv[...] = jnp.zeros_like(dv)
    dqt[...] = jnp.zeros_like(dqt)

    def block(k0, q0, width, masked):
        k0, q0 = pl.multiple_of(k0, width), pl.multiple_of(q0, width)
        ks, qs = pl.ds(k0, width), pl.ds(q0, width)
        p = jnp.exp(nn(kp[ks, :], qt[:, qs]))
        if masked:
            qpos = q0 + lax.broadcasted_iota(jnp.int32, (1, width), 1)
            kpos = k0 + lax.broadcasted_iota(jnp.int32, (width, width), 0)
            p = jnp.where((kpos >= start_row(qpos, b1, b2)) & (kpos <= qpos), p, 0.0)
        ds = (p * nn(vp[ks, :], dot[:, qs])).astype(bf16)
        dv[ks, :] += nn(p.astype(bf16), dor[qs, :])
        dk[ks, :] += nn(ds, qr[qs, :])
        dqt[:, qs] += nn(qkv_ref[HD : 2 * HD, ks], ds)

    @pl.loop(0, 12)
    def _(n):
        qb = jnp.where(n < 9, 3 + n // 3, jnp.where(n == 9, 1, 2))
        kb = jnp.where(n < 9, n % 3, jnp.where(n == 11, 1, 0))
        block(kb * FW, qb * FW, FW, False)

    @pl.loop(0, TOK // B)
    def _(i):
        lo = jnp.where(i < PROMPT // B, 2 * (i // 2), first_block(i, b1, b2))

        @pl.loop(lo, i + 1)
        def _(j):
            block(j * B, i * B, B, True)

    for m in range(PARTS):
        chunk = part ^ m

        @pl.loop(0, 2)
        def _(step, m=m, chunk=chunk):
            for t in range(3):
                off = pl.multiple_of(step * 384 + t * 128, 128)
                sl, here = pl.ds(pl.multiple_of(chunk * ROWS + off, 128), 128), pl.ds(off, 128)
                dq = dqt[:, sl].astype(bf16).astype(f32) * scale
                out_refs[m][0:HD, here] = dq.astype(bf16)
                out_refs[m][HD : 2 * HD, here] = dk[sl, :].T[0:HD, :].astype(bf16)
                out_refs[m][2 * HD : 3 * HD, here] = dv[sl, :].T[0:HD, :].astype(bf16)


def attn_bwd(meta, scale, qkvt, grads, slot, mixture, logsum, head):
    whole = lambda rows: pl.BlockSpec((rows, ROWS), lambda i, b: (0, 0))
    return pl.pallas_call(
        bwd_kernel,
        out_shape=[jax.ShapeDtypeStruct((3 * HD, ROWS), bf16)] * PARTS,
        grid_spec=pltpu.PrefetchScalarGridSpec(
            num_scalar_prefetch=1,
            grid=(1,),
            in_specs=[
                pl.BlockSpec((HD, 1), lambda i, b: (0, 0)),
                pl.BlockSpec((3 * HD, TOK), lambda i, b: (head, 0)),
            ]
            + [
                pl.BlockSpec((PARTS, HD, ROWS), lambda i, b: (0, slot, 0)),
                pl.BlockSpec((PARTS, HD, ROWS), lambda i, b: (0, head, 0)),
                pl.BlockSpec((1, 1, TOK), lambda i, b: (head, 0, 0)),
            ],
            out_specs=[whole(3 * HD)] * PARTS,
            scratch_shapes=[pltpu.VMEM((TOK, 128), bf16)] * 2
            + [pltpu.VMEM((128, TOK), bf16)] * 2
            + [pltpu.VMEM((TOK, 128), bf16)] * 2
            + [pltpu.VMEM((TOK, 128), f32)] * 2
            + [pltpu.VMEM((HD, TOK), f32)],
        ),
        compiler_params=pltpu.CompilerParams(dimension_semantics=("arbitrary",), vmem_limit_bytes=60 << 20),
        cost_estimate=pl.CostEstimate(flops=18 * 10**9, bytes_accessed=8 << 20, transcendentals=0),
        name="attn_bwd",
    )(meta, scale, qkvt, grads, mixture, logsum)


def normalize(values, gain_vec):
    scaling = lax.rsqrt(jnp.mean(values * values, axis=-1, keepdims=True) + EPSILON)
    return (values * scaling * gain_vec, scaling)


def normalize_back(values, scaling, gain_vec, upstream):
    weighted = gain_vec * upstream
    return scaling * weighted - values * scaling**3 * jnp.mean(values * weighted, axis=-1, keepdims=True)


def by_head(query, key, value):
    rows, width = query.shape
    split = (rows, width // HD, 1, HD)
    stacked = jnp.concatenate([query.reshape(split), key.reshape(split), value.reshape(split)], axis=2)
    return stacked.reshape(rows, 3 * width)


def by_slot(query, key, value, part):
    rows = query.shape[0]
    stacked = by_head(query, key, value).reshape(rows, PARTS, LH, 3 * HD)
    pieces = [lax.dynamic_index_in_dim(stacked, part ^ m, axis=1, keepdims=False) for m in range(PARTS)]
    return jnp.stack(pieces, axis=2).reshape(rows, 3 * D)


def exchange(value):
    return lax.all_to_all(value, "heads", split_axis=0, concat_axis=0, tiled=True)


def swap(value, axis, mask):
    count = lax.axis_size(axis)
    return lax.ppermute(value, axis, [(i, i ^ mask) for i in range(count)])


def piece(value, index, count):
    rows = value.shape[-2] // count
    return lax.dynamic_slice_in_dim(value, index * rows, rows, axis=value.ndim - 2)


def sum_low(*terms):
    total = terms[0].astype(f32)
    for term in terms[1:]:
        total = total + term.astype(f32)
    return total.astype(bf16)


def far_bits():
    bits = [2]
    while bits[-1] * 2 < lax.axis_size("fsdp"):
        bits.append(bits[-1] * 2)
    return bits


def sum_far(value):
    bits = far_bits()
    for bit, twice in zip(bits[0::2], bits[1::2]):
        value = sum_low(value, *[swap(value, "fsdp", m) for m in (bit, twice, bit | twice)])
    if len(bits) % 2:
        value = sum_low(value, swap(value, "fsdp", bits[-1]))
    return value


def scatter_near(value):
    core = lax.axis_index("fsdp") & 1
    return sum_low(piece(value, core, 2), swap(piece(value, 1 - core, 2), "fsdp", 1))


def paired(value, axis, mask, high):
    other = swap(value, axis, mask)
    return jnp.where(
        high, jnp.concatenate([other, value], axis=-2), jnp.concatenate([value, other], axis=-2)
    )


def gather_near(value):
    return paired(value, "fsdp", 1, lax.axis_index("fsdp") % 2 == 1)


def scatter_heads(value):
    part = lax.axis_index("heads")
    terms = [swap(piece(value, part ^ m, PARTS), "heads", m) for m in (1, 2, 3)]
    return sum_low(piece(value, part, PARTS), *terms)


def gather_heads(value):
    part = lax.axis_index("heads")
    near, far, both = [swap(value, "heads", m) for m in (1, 2, 3)]
    odd, high = part % 2 == 1, part >= 2
    low_pair = [jnp.where(odd, near, value), jnp.where(odd, value, near)]
    high_pair = [jnp.where(odd, both, far), jnp.where(odd, far, both)]
    pieces = [jnp.where(high, b, a) for a, b in zip(low_pair, high_pair)]
    pieces += [jnp.where(high, a, b) for a, b in zip(low_pair, high_pair)]
    return jnp.concatenate(pieces, axis=-2)


def body(
    inputs,
    cotangent,
    lengths,
    adapter_ids,
    query_weight,
    key_weight,
    value_weight,
    out_weight,
    up_weight,
    down_weight,
    attn_gain,
    mlp_gain,
    query_scale,
    adapter_in,
    adapter_out,
):
    part = lax.axis_index("heads")
    rows = inputs[0]
    near = swap(rows, "heads", 1)
    far = swap(rows, "heads", 2)
    half = ROWS // 2
    both_low = swap(far[:half], "heads", 1)
    both_high = swap(near[half:], "heads", 2)

    offset = part * ROWS
    ends = PROMPT + jnp.cumsum(lengths[0])
    bounds = ends[:2].astype(jnp.int32)
    ids = adapter_ids[0]
    meta = jnp.concatenate([bounds, ids, part[None].astype(jnp.int32)])
    places = offset + jnp.arange(ROWS, dtype=jnp.int32)
    token = token_adapter(places, meta)
    chosen = (token[:, None] == (jnp.arange(AR, dtype=jnp.int32) // RANK)[None, :]).astype(f32)
    chosen2 = jnp.concatenate([chosen, chosen], axis=1)
    flat_down = jnp.transpose(adapter_in, (0, 2, 1, 3)).reshape(4, D, AR)
    flat_up = adapter_out.reshape(4, AR, D)
    gain_attn = attn_gain.astype(f32)
    gain_mlp = mlp_gain.astype(f32)
    width = LH * HD

    def mine(weight):
        return lax.dynamic_slice_in_dim(weight, part * width, width, axis=1)

    weights_mine = by_head(mine(query_weight), mine(key_weight), mine(value_weight))
    weights_mine = lax.all_gather(weights_mine, "fsdp", axis=0, tiled=True)
    w_out = lax.all_gather(out_weight, "fsdp", axis=0, tiled=True)
    w_up = lax.all_gather(up_weight, "fsdp", axis=0, tiled=True)
    w_down = lax.all_gather(down_weight, "fsdp", axis=0, tiled=True)
    weights_all = lax.all_gather(by_slot(query_weight, key_weight, value_weight, part), "fsdp", axis=0, tiled=True)

    down_pair = jnp.concatenate([flat_down[0], flat_down[1]], axis=1)
    zero = jnp.zeros((AR, D), bf16)
    up_slots = jnp.concatenate([by_slot(flat_up[0], zero, zero, part), by_slot(zero, zero, flat_up[1], part)], axis=0)
    up_mine = jnp.concatenate(
        [by_head(mine(flat_up[0]), zero[:, :width], zero[:, :width]), by_head(zero[:, :width], zero[:, :width], mine(flat_up[1]))], axis=0
    )
    up_heads = jnp.transpose(up_mine.reshape(2 * AR, LH, 3 * HD), (1, 0, 2))
    scale_row = query_scale * HD ** (-0.5)
    scale_mine = jnp.tile(jnp.concatenate([scale_row, jnp.ones((2 * HD,), f32)]), LH)[:, None]

    wt, ut = weights_mine.T, up_mine.T
    per = ROWS // QB
    done = ()
    for source, first in ((rows, part * per), (near, (part ^ 1) * per), (far, (part ^ 2) * per),
                          (both_low, (part ^ 3) * per), (both_high, (part ^ 3) * per + per // 2)):
        done = qkv_project(
            meta, first[None].astype(jnp.int32), source, gain_attn[None, :], wt, down_pair, ut, scale_mine, done
        )
    qkvt, normed_all, inner_all = done
    mixture, logsum = attn_fwd(bounds, qkvt)
    mixed = exchange(mixture).reshape(D, ROWS)

    rows_in = inputs[0].astype(f32)
    scaling_attn = lax.rsqrt(jnp.mean(rows_in * rows_in, axis=-1, keepdims=True) + EPSILON)

    middle = rows_in + tn(mixed, w_out)
    normed_mlp, scaling_mlp = normalize(middle, gain_mlp)
    normed_mlp_low = normed_mlp.astype(bf16)
    inner_up = (nn(normed_mlp_low, flat_down[2]) * chosen).astype(bf16)
    before = nn(normed_mlp_low, w_up) + nn(inner_up, flat_up[2])
    gate = jax.nn.sigmoid(before)
    hidden_low = (before * gate).astype(bf16)
    inner_down = (nn(hidden_low, flat_down[3]) * chosen).astype(bf16)
    outputs = (middle + (nn(hidden_low, w_down) + nn(inner_down, flat_up[3]))).astype(bf16)

    upstream = cotangent[0].astype(f32)
    grad_after = cotangent[0]
    spread_down = (nt(grad_after, flat_up[3]) * chosen).astype(bf16)
    grad_hidden = nt(grad_after, w_down) + nt(spread_down, flat_down[3])
    grad_before = (grad_hidden * gate * (1.0 + before * (1.0 - gate))).astype(bf16)
    spread_up = (nt(grad_before, flat_up[2]) * chosen).astype(bf16)
    grad_normed_mlp = nt(grad_before, w_up) + nt(spread_up, flat_down[2])
    grad_middle = upstream + normalize_back(middle, scaling_mlp, gain_mlp, grad_normed_mlp)
    grad_branch = grad_middle.astype(bf16)
    grad_mixed = nt(w_out, grad_branch).astype(bf16).reshape(PARTS, LH, HD, ROWS)
    grad_first_head = exchange(grad_mixed[:, 0])
    grad_rest = exchange(grad_mixed[:, 1:].reshape(PARTS, (LH - 1) * HD, ROWS))

    terms = [tn(spread_up, normed_mlp_low), tn(spread_down, hidden_low), tn(inner_up, grad_before), tn(inner_down, grad_after)]
    mlp_total = jnp.concatenate(terms).astype(bf16)
    bits = far_bits()

    def add_far(value, chosen_bits):
        for bit in chosen_bits:
            value = sum_low(value, swap(value, "fsdp", bit))
        return value

    stages = [
        lambda v: scatter_heads(scatter_near(v)),
        lambda v: add_far(v, bits[:1]),
        lambda v: add_far(v, bits[1:]),
        lambda v: paired(v, "heads", 1, part % 2 == 1),
    ]

    grads, arrived = [], []
    for h in range(LH):
        if h >= 2:
            meta, _ = lax.optimization_barrier((meta, arrived[h - 2]))
        if h >= 1:
            mlp_total = stages[h - 1](mlp_total)
            meta, _ = lax.optimization_barrier((meta, mlp_total))
        source, slot = (grad_first_head, 0) if h == 0 else (grad_rest, h - 1)
        grad = attn_bwd(meta, scale_row[:, None], qkvt, source, slot, mixture, logsum, h)
        grads += grad
        arrived.append([grad[0]] + [swap(grad[m], "heads", m) for m in (1, 2, 3)])
    mlp_total = stages[3](mlp_total)
    meta, _ = lax.optimization_barrier((meta, (mlp_total, arrived[2])))

    first_attn, second_attn = adapter_grads(meta, grads, normed_all, inner_all, up_heads)
    tiles = D // 128
    first_half = scatter_heads(scatter_near(first_attn.astype(bf16)))
    second_half = scatter_near(second_attn.astype(bf16).reshape(tiles, -1, 128))
    total = sum_far(jnp.concatenate([first_half, second_half]))
    total = gather_near(gather_heads(total))
    mlp_total = gather_near(paired(mlp_total, "heads", 2, part >= 2))
    first_total = total[:tiles]
    second_total = total[tiles:].reshape(tiles, 2, PARTS, -1, 128)
    second_total = jnp.transpose(second_total, (2, 0, 1, 3, 4))

    slot = PARTS * 3 * HD
    grad_normed, spread = 0.0, 0.0
    for h in range(LH):
        cut = slice(h * slot, (h + 1) * slot)
        both = jnp.concatenate(arrived[h])
        grad_normed = grad_normed + lax.dot_general(
            both, weights_all[:, cut], (((0,), (1,)), ((), ())), preferred_element_type=f32
        )
        spread = spread + lax.dot_general(
            both, up_slots[:, cut], (((0,), (1,)), ((), ())), preferred_element_type=f32
        )
    grad_normed = grad_normed + nt((spread * chosen2).astype(bf16), down_pair)
    grad_inputs = grad_middle + normalize_back(rows_in, scaling_attn, gain_attn, grad_normed)

    first_pair = jnp.transpose(first_total.reshape(tiles, 2, ADAPTERS, RANK, 128), (1, 2, 0, 4, 3))
    first_rest = jnp.transpose(mlp_total[: 2 * AR].reshape(2, ADAPTERS, RANK, D), (0, 1, 3, 2))
    grad_first = jnp.concatenate([first_pair.reshape(2, ADAPTERS, D, RANK), first_rest]).astype(f32)
    second_pair = jnp.transpose(second_total.reshape(PARTS, LH, 2, HD, AR), (2, 4, 0, 1, 3)).reshape(2 * AR, D)
    grad_second = jnp.concatenate([second_pair, mlp_total[2 * AR :]]).astype(f32).reshape(4, ADAPTERS, RANK, D)
    return (outputs[None], grad_inputs[None], grad_first, grad_second)


def solution(mesh):
    placed = (
        P("fsdp", "heads", None),
        P("fsdp", "heads", None),
        P("fsdp", None),
        P("fsdp", None),
        P("fsdp", None),
        P("fsdp", None),
        P("fsdp", None),
        P("fsdp", None),
        P("fsdp", None),
        P("fsdp", None),
        P(),
        P(),
        P(),
        P(),
        P(),
    )
    return jax.shard_map(
        body,
        mesh=mesh,
        in_specs=placed,
        out_specs=(P("fsdp", "heads", None), P("fsdp", "heads", None), P(), P()),
        check_vma=False,
    )
```

time: 653 us -> 540 us (0.83)
  waiting for transfers between devices: 330 us -> 81.2 us
  Pallas kernels: 148 us -> 196 us
  starting transfers between devices: 14.7 us -> 59.8 us
  local copies, waits for them, and re-layouts: 34.4 us -> 67 us
  other arithmetic: 24.7 us -> 32.1 us
    psum x1 -> x0, waiting for transfers between devices: 133 us -> none  [body(): first_mlp, second_mlp = lax.psum((first_mlp, second_mlp), ('heads', 'fsdp'))]
    all_gather x2 -> x1, waiting for transfers between devices: 84 us -> 0.01 us  [body(): lax.all_gather(by_slot(query_weight, key_weight, value_weight, part), 'fs...]
    all_to_all x3, waiting for transfers between devices: 83.1 us -> 11.2 us  [exchange(): lax.all_to_all(value, 'heads', split_axis=0, concat_axis=0, tiled=True)]
    ppermute x0 -> x37, waiting for transfers between devices: none -> 68 us  [swap(): return lax.ppermute(value, axis, [(i, i ^ mask) for i in range(count)])]
    pallas_call x2 -> x10, Pallas kernels: 102 us -> 150 us  [the longest x4 95 us: attn_bwd(): pl.pallas_call(bwd_kernel, out_shape=[jax.ShapeDtypeStruct((3 * HD, ROWS)...]
    ppermute x0 -> x37, starting transfers between devices: none -> 47.1 us  [swap(): return lax.ppermute(value, axis, [(i, i ^ mask) for i in range(count)])]
    all_gather x1, waiting for transfers between devices: 14.6 us -> 0.01 us  [body(): w_up = lax.all_gather(up_weight, 'fsdp', axis=0, tiled=True)]
    all_gather x1, waiting for transfers between devices: 13.3 us -> 0.02 us  [body(): weights_mine = lax.all_gather(weights_mine, 'fsdp', axis=0, tiled=True)]
  transfers between devices with their start and end apart: 10 -> 45, of which waited for: 7 -> 13; matrix products, arithmetic and copies ran while one was open for 15% -> 26% of each run, Pallas kernels for 23% -> 37%
where the time goes in v2:
time: 540 us; the launch traced here: 531 us
  Pallas kernels  196 us (36%)
  waiting for transfers between devices  81.2 us (15%)
  matrix products  79.3 us (15%)
  local copies, waits for them, and re-layouts  67 us (12%)
  starting transfers between devices  59.8 us (11%)
  other arithmetic  32.1 us (6%)
  between operations  15.4 us (3%)
    pallas_call x4, Pallas kernels, attn_bwd(): pl.pallas_call(bwd_kernel, out_shape=[jax.ShapeDtypeStruct((3 * HD, ROWS)...  95 us
    ppermute x37, waiting for transfers between devices, swap(): return lax.ppermute(value, axis, [(i, i ^ mask) for i in range(count)])  68 us
    ppermute x37, starting transfers between devices, swap(): return lax.ppermute(value, axis, [(i, i ^ mask) for i in range(count)])  47.1 us
    pallas_call x1, Pallas kernels, attn_fwd(): pl.pallas_call(fwd_kernel, out_shape=(jax.ShapeDtypeStruct((4, nh * HD, 7...  46 us
    pallas_call x5, Pallas kernels, qkv_project(): pl.pallas_call(qkv_kernel, out_shape=(jax.ShapeDtypeStruct((width, TOK),...  42.7 us
    dot_general x4, matrix products, body(): lax.dot_general(both, weights_all[:, cut], (((0,), (1,)), ((), ())), pref...  24.8 us
    dot_general x8, matrix products, nt(): lax.dot_general(a, b, (((1,), (1,)), ((), ())), preferred_element_type=f32)  24.7 us
    unnamed x147, local copies, waits for them, and re-layouts  16.5 us
  transfers between devices with their start and end apart: 45, of which 13 were waited for; matrix products, arithmetic and copies ran while one was open for 26% of the time, Pallas kernels for 37%

profile of v2, /device:TPU:9, one launch (start us, length us, event | category | flops | bytes accessed | tf_op | source)
XLA Modules:
  0.0 530.9 jit_solution(13513989993622656141)
XLA Ops:
  44.7 13.8 %collective-permute-done.2.x_ref = bf16[768,1280]{1,0:T(8,128)(2,1)} collective-permute-done((bf16[768,1280]{1,0:T(8,128)(2,1)S(1)}, bf16[768,1280]{1,0:T(8,128)(2,1)}, u32[]{:S(2)}, u32[]{:S(2)}) %collective-permute-start.2) | collective-permute-done | bytes 1966112 | tf_op jit(solution)/shard_map/ppermute | solution.py:368
  73.4 4.4 copy.134
  77.8 9.6 %qkv_project.5 = (bf16[960,3072]{1,0:T(8,128)(2,1)}, bf16[3072,1280]{1,0:T(8,128)(2,1)}, bf16[3072,256]{1,0:T(8,128)(2,1)}) custom-call(s32[7]{0:T(128)} %pad_add_fusion.meta, s32[1]{0:T(128)} %bitcast.21.first, bf16[768,1280]{1,0:T(8,128)(2,1)} %bitcast.169, f32[1,1280]{1,0:T(1,128)} %broadcast_in_dim.64.gain_ref, bf16[960,1280]{1,0:T(8,128)(2,1)} %bitcast.164, ...), custom_call_target="tpu_custom_call" | custom-call | flops 2390753280 | bytes 4423680 | tf_op jit(solution)/shard_map/qkv_project/pallas_call | solution.py:68
  87.4 9.6 %qkv_project.6 = (bf16[960,3072]{1,0:T(8,128)(2,1)}, bf16[3072,1280]{1,0:T(8,128)(2,1)}, bf16[3072,256]{1,0:T(8,128)(2,1)}) custom-call(s32[7]{0:T(128)} %pad_add_fusion.meta, s32[1]{0:T(128)} %bitcast.20.first, bf16[768,1280]{1,0:T(8,128)(2,1)} %collective-permute-done.x_ref, ...), custom_call_target="tpu_custom_call", output_to_operand_aliasing={{0}: (8, {}), {1}: (9, {}), {2}: (10, {})} | custom-call | flops 2390753280 | bytes 4423680 | tf_op jit(solution)/shard_map/qkv_project/pallas_call | solution.py:68
  97.0 9.7 %qkv_project.7 = (bf16[960,3072]{1,0:T(8,128)(2,1)}, bf16[3072,1280]{1,0:T(8,128)(2,1)}, bf16[3072,256]{1,0:T(8,128)(2,1)}) custom-call(s32[7]{0:T(128)} %pad_add_fusion.meta, s32[1]{0:T(128)} %bitcast.19.first, bf16[768,1280]{1,0:T(8,128)(2,1)} %collective-permute-done.2.x_ref, ...), custom_call_target="tpu_custom_call", output_to_operand_aliasing={{0}: (8, {}), {1}: (9, {}), {2}: (10, {})} | custom-call | flops 2390753280 | bytes 4423680 | tf_op jit(solution)/shard_map/qkv_project/pallas_call | solution.py:68
  106.8 6.9 %qkv_project.8 = (bf16[960,3072]{1,0:T(8,128)(2,1)}, bf16[3072,1280]{1,0:T(8,128)(2,1)}, bf16[3072,256]{1,0:T(8,128)(2,1)}) custom-call(s32[7]{0:T(128)} %pad_add_fusion.meta, s32[1]{0:T(128)} %bitcast.18.first, bf16[384,1280]{1,0:T(8,128)(2,1)} %collective-permute-done.3.x_ref, ...), custom_call_target="tpu_custom_call", output_to_operand_aliasing={{0}: (8, {}), {1}: (9, {}), {2}: (10, {})} | custom-call | flops 1195376640 | bytes 3440640 | tf_op jit(solution)/shard_map/qkv_project/pallas_call | solution.py:68
  113.7 6.8 %qkv_project.9 = (bf16[960,3072]{1,0:T(8,128)(2,1)}, bf16[3072,1280]{1,0:T(8,128)(2,1)}, bf16[3072,256]{1,0:T(8,128)(2,1)}) custom-call(s32[7]{0:T(128)} %pad_add_fusion.meta, s32[1]{0:T(128)} %bitcast.5.first, bf16[384,1280]{1,0:T(8,128)(2,1)} %collective-permute-done.1.x_ref, ...), custom_call_target="tpu_custom_call", output_to_operand_aliasing={{0}: (8, {}), {1}: (9, {}), {2}: (10, {})} | custom-call | flops 1195376640 | bytes 3440640 | tf_op jit(solution)/shard_map/qkv_project/pallas_call | solution.py:68
  120.5 46.0 %attn_fwd.1 = (bf16[4,320,768]{2,1,0:T(8,128)(2,1)}, f32[4,1,3072]{2,1,0:T(1,128)}) custom-call(s32[2]{0:T(128)} %copy-done.60, bf16[960,3072]{1,0:T(8,128)(2,1)} %get-tuple-element.57.qkv_ref), custom_call_target="tpu_custom_call" | custom-call | flops 40000000000 | bytes 10485760 | tf_op jit(solution)/shard_map/attn_fwd/pallas_call | solution.py:208
  166.5 4.6 all-to-all-start
  175.2 8.2 %fusion.27 = f32[768,1280]{1,0:T(8,128)} fusion(bf16[1280,1280]{1,0:T(8,128)(2,1)} %all-gather.12.cloned.1.call-done, bf16[1,768,1280]{2,1,0:T(8,128)(2,1)} %param.16), kind=kOutput, calls=%fused_computation.52 | convolution fusion | flops 2516582400 | bytes 9175040 | tf_op jit(solution)/shard_map/dot_general | solution.py:26
  183.4 10.7 %all-to-all-done = bf16[4,320,768]{2,1,0:T(8,128)(2,1)} async-done(((bf16[4,320,768]{2,1,0:T(8,128)(2,1)}), bf16[4,320,768]{2,1,0:T(8,128)(2,1)}, u32[]{:S(2)}, u32[]{:S(2)}) %all-to-all-start) | async-done | bytes 1966112 | tf_op jit(solution)/shard_map/all_to_all | solution.py:363
  194.1 5.5 %multiply_reduce_fusion.1 = (f32[768]{0:T(1024)S(1)}, f32[768,1280]{1,0:T(8,128)S(1)}) fusion(bf16[1280,768]{1,0:T(8,128)(2,1)} %bitcast.22, bf16[1280,1280]{1,0:T(8,128)(2,1)} %all-gather.8.cloned.1.call-done, bf16[1,768,1280]{2,1,0:T(8,128)(2,1)S(1)} %copy-done.5), kind=kOutput, calls=%fused_computation.24 | convolution fusion | flops 2520513792 | bytes 11144192 | tf_op jit(solution)/shard_map/dot_general | solution.py:30
  202.9 4.8 fusion.76
  223.8 4.3 fusion.12
  240.1 5.4 %fusion.77 = f32[768,1280]{1,0:T(8,128)S(1)} fusion(bf16[768,1280]{1,0:T(8,128)(2,1)} %copy-done.22, bf16[1280,1280]{1,0:T(8,128)(2,1)} %all-gather.12.cloned.1.call-done), kind=kOutput, calls=%fused_computation.201 | convolution fusion | flops 2516582400 | bytes 9175040 | tf_op jit(solution)/shard_map/dot_general | solution.py:34
  247.9 4.5 all-to-all-start.2
  252.5 23.8 %attn_bwd.4 = (bf16[240,768]{1,0:T(8,128)(2,1)}, bf16[240,768]{1,0:T(8,128)(2,1)}, bf16[240,768]{1,0:T(8,128)(2,1)}, bf16[240,768]{1,0:T(8,128)(2,1)}) custom-call(s32[7]{0:T(128)} %pad_add_fusion.meta, f32[80,1]{1,0:T(8,128)} %copy.146.scale_ref, bf16[960,3072]{1,0:T(8,128)(2,1)} %get-tuple-element.57.qkv_ref, bf16[4,80,768]{2,1,0:T(8,128)(2,1)} %copy-done.36, ...), custom_call_target="tpu_custom_call" | custom-call | flops 17999998976 | bytes 8388608 | tf_op jit(solution)/shard_map/attn_bwd/pallas_call | solution.py:310
  294.8 6.9 %collective-permute-done.6 = bf16[240,768]{1,0:T(8,128)(2,1)S(1)} collective-permute-done((bf16[240,768]{1,0:T(8,128)(2,1)S(1)}, bf16[240,768]{1,0:T(8,128)(2,1)S(1)}, u32[]{:S(2)}, u32[]{:S(2)}) %collective-permute-start.6) | collective-permute-done | bytes 368672 | tf_op jit(solution)/shard_map/ppermute | solution.py:368
  302.5 6.5 %collective-permute-start.18 = (bf16[64,1280]{1,0:T(8,128)(2,1)S(1)}, bf16[64,1280]{1,0:T(8,128)(2,1)S(1)}, u32[]{:S(2)}, u32[]{:S(2)}) collective-permute-start(bf16[64,1280]{1,0:T(8,128)(2,1)S(1)} %add_convert_fusion.4), channel_id=1, source_target_pairs={{0,4},{1,5},{2,6},{3,7},{4,0},{5,1},{6,2},{7,3},{8,12},{9,13},{10,... | collective-permute-start | bytes 491528 | tf_op jit(solution)/shard_map/ppermute | solution.py:368
  309.0 23.7 %attn_bwd.5 = (bf16[240,768]{1,0:T(8,128)(2,1)}, bf16[240,768]{1,0:T(8,128)(2,1)}, bf16[240,768]{1,0:T(8,128)(2,1)}, bf16[240,768]{1,0:T(8,128)(2,1)}) custom-call(s32[7]{0:T(128)} %pad_add_fusion.meta, f32[80,1]{1,0:T(8,128)} %copy.146.scale_ref, bf16[960,3072]{1,0:T(8,128)(2,1)} %get-tuple-element.57.qkv_ref, bf16[4,240,768]{2,1,0:T(8,128)(2,1)} %all-to-all-done.2.refs_0_, ...), custom_call_target="tpu_custom_call" | custom-call | flops 17999998976 | bytes 8388608 | tf_op jit(solution)/shard_map/attn_bwd/pallas_call | solution.py:310
  334.3 23.7 %attn_bwd.6 = (bf16[240,768]{1,0:T(8,128)(2,1)}, bf16[240,768]{1,0:T(8,128)(2,1)}, bf16[240,768]{1,0:T(8,128)(2,1)}, bf16[240,768]{1,0:T(8,128)(2,1)}) custom-call(s32[7]{0:T(128)} %pad_add_fusion.meta, f32[80,1]{1,0:T(8,128)} %copy.146.scale_ref, bf16[960,3072]{1,0:T(8,128)(2,1)} %get-tuple-element.57.qkv_ref, bf16[4,240,768]{2,1,0:T(8,128)(2,1)} %all-to-all-done.2.refs_0_, ...), custom_call_target="tpu_custom_call" | custom-call | flops 17999998976 | bytes 8388608 | tf_op jit(solution)/shard_map/attn_bwd/pallas_call | solution.py:310
  365.6 25.2 %collective-permute-done.12 = bf16[240,768]{1,0:T(8,128)(2,1)S(1)} collective-permute-done((bf16[240,768]{1,0:T(8,128)(2,1)}, bf16[240,768]{1,0:T(8,128)(2,1)S(1)}, u32[]{:S(2)}, u32[]{:S(2)}) %collective-permute-start.12) | collective-permute-done | bytes 368672 | tf_op jit(solution)/shard_map/ppermute | solution.py:368
  390.9 23.8 %attn_bwd.7 = (bf16[240,768]{1,0:T(8,128)(2,1)}, bf16[240,768]{1,0:T(8,128)(2,1)}, bf16[240,768]{1,0:T(8,128)(2,1)}, bf16[240,768]{1,0:T(8,128)(2,1)}) custom-call(s32[7]{0:T(128)} %pad_add_fusion.meta, f32[80,1]{1,0:T(8,128)} %copy.146.scale_ref, bf16[960,3072]{1,0:T(8,128)(2,1)} %get-tuple-element.57.qkv_ref, bf16[4,240,768]{2,1,0:T(8,128)(2,1)} %all-to-all-done.2.refs_0_, ...), custom_call_target="tpu_custom_call" | custom-call | flops 17999998976 | bytes 8388608 | tf_op jit(solution)/shard_map/attn_bwd/pallas_call | solution.py:310
  417.4 12.4 %adapter_grads.1 = (f32[10,256,128]{2,1,0:T(8,128)}, f32[4,2,80,128]{3,2,1,0:T(8,128)}) custom-call(s32[7]{0:T(128)} %pad_add_fusion.meta, bf16[240,768]{1,0:T(8,128)(2,1)} %get-tuple-element.60.refs_0_, bf16[240,768]{1,0:T(8,128)(2,1)} %get-tuple-element.61.refs_1_, bf16[240,768]{1,0:T(8,128)(2,1)} %get-tuple-element.62.refs_2_, ...), custom_call_target="tpu_custom_call" | custom-call | flops 4026531840 | bytes 20971520 | tf_op jit(solution)/shard_map/adapter_grads/pallas_call | solution.py:131
  431.5 5.3 collective-permute-start.27
  451.7 4.5 collective-permute-start.29
  457.8 8.4 %collective-permute-done.29 = bf16[20,32,128]{2,1,0:T(8,128)(2,1)S(1)} collective-permute-done((bf16[20,32,128]{2,1,0:T(8,128)(2,1)S(1)}, bf16[20,32,128]{2,1,0:T(8,128)(2,1)S(1)}, u32[]{:S(2)}, u32[]{:S(2)}) %collective-permute-start.29) | collective-permute-done | bytes 163872 | tf_op jit(solution)/shard_map/ppermute | solution.py:368
  472.5 5.7 %fusion.37 = f32[768,1280]{1,0:T(8,128)} fusion(f32[768,256]{1,0:T(8,128)} %fusion.56, f32[768,256]{1,0:T(8,128)} %fusion.48, f32[768,256]{1,0:T(8,128)} %fusion.54, bf16[960,768]{1,0:T(8,128)(2,1)} %constant_dynamic-update-slice_fusion, pred[768,128]{1,0:T(32,128)(4,1)S(1)} %copy-done.37, bf16[128,3840]{0,1:T(8,128)(2,1)S(1)} %bitcast.180, ...), kind=kOutput, calls=%fused_computation.71 | convolution fusion | flops 884277248 | bytes 10485760 | tf_op jit(solution)/shard_map/dot_general | solution.py:26
  496.0 5.6 %fusion.20 = f32[768,1280]{1,0:T(8,128)S(1)} fusion(bf16[960,768]{1,0:T(8,128)(2,1)} %copy-done.55, bf16[1280,3840]{1,0:T(8,128)(2,1)} %all-gather.14.cloned.1.call-done), kind=kOutput, calls=%fused_computation.34 | convolution fusion | flops 1887436800 | bytes 8028160 | tf_op jit(solution)/shard_map/dot_general | solution.py:576
  501.6 5.7 %fusion.22 = f32[768,1280]{1,0:T(8,128)} fusion(bf16[960,768]{1,0:T(8,128)(2,1)} %constant_dynamic-update-slice_fusion, bf16[1280,3840]{1,0:T(8,128)(2,1)S(1)} %copy-done.34), kind=kOutput, calls=%fused_computation.36 | convolution fusion | flops 1887436800 | bytes 8028160 | tf_op jit(solution)/shard_map/dot_general | solution.py:576
  507.3 4.2 fusion.18
  511.6 9.3 %fusion.4 = (f32[768]{0:T(1024)S(1)}, f32[768]{0:T(1024)S(1)}, f32[768,1280]{1,0:T(8,128)S(1)}) fusion(bf16[1,768,1280]{2,1,0:T(8,128)(2,1)S(1)} %copy-done.6, f32[768,1280]{1,0:T(8,128)S(1)} %copy-done.9, bf16[960,768]{1,0:T(8,128)(2,1)} %copy-done.21, bf16[1280,3840]{1,0:T(8,128)(2,1)} %all-gather.14.cloned.1.call-done, f32[768,1280]{1,0:T(8,128)} %fusion.18, ...), kind=kOutput, calls=%fused_computation.12 | convolution fusion | flops 1897265664 | bytes 25734144 | tf_op jit(solution)/shard_map/dot_general | solution.py:576
  (359 shorter events, 166.2 us)
Async XLA Ops:
  7.2 66.3 %all-gather.6.cloned.1.call-start = ((), (), s32[]{:S(2)}) async-start(), calls=%async_computation.3 | async-start | bytes 2949120 | tf_op jit(solution)/shard_map/all_gather | solution.py:476
  11.6 163.6 %all-gather.12.cloned.1.call-start = ((), (), s32[]{:S(2)}) async-start(), calls=%async_computation.6 | async-start | bytes 3686400 | tf_op jit(solution)/shard_map/all_gather | solution.py:479
  12.4 171.0 %all-gather.8.cloned.1.call-start = ((), (), s32[]{:S(2)}) async-start(), calls=%async_computation.4 | async-start | bytes 3686400 | tf_op jit(solution)/shard_map/all_gather | solution.py:477
  13.1 189.8 %all-gather.10.cloned.1.call-start = ((), (), s32[]{:S(2)}) async-start(), calls=%async_computation.5 | async-start | bytes 3686400 | tf_op jit(solution)/shard_map/all_gather | solution.py:478
  13.7 482.3 %all-gather.14.cloned.1.call-start = ((), (), s32[]{:S(2)}) async-start(), calls=%async_computation.7 | async-start | bytes 11059200 | tf_op jit(solution)/shard_map/all_gather | solution.py:480
  13.7 51.0 %collective-permute-start = (bf16[768,1280]{1,0:T(8,128)(2,1)S(1)}, bf16[768,1280]{1,0:T(8,128)(2,1)}, u32[]{:S(2)}, u32[]{:S(2)}) collective-permute-start(bf16[768,1280]{1,0:T(8,128)(2,1)S(1)} %bitcast.170), channel_id=1, source_target_pairs={{0,8},{8,0},{16,24},{24,16},{1,9},{9,1},{17,25},{25,17},{2,10},{10... | collective-permute-start | bytes 5898248 | tf_op jit(solution)/shard_map/ppermute | solution.py:368
  15.0 43.5 %collective-permute-start.2 = (bf16[768,1280]{1,0:T(8,128)(2,1)S(1)}, bf16[768,1280]{1,0:T(8,128)(2,1)}, u32[]{:S(2)}, u32[]{:S(2)}) collective-permute-start(bf16[768,1280]{1,0:T(8,128)(2,1)S(1)} %bitcast.171), channel_id=1, source_target_pairs={{0,16},{8,24},{16,0},{24,8},{1,17},{9,25},{17,1},{25,9},{2,18},{10... | collective-permute-start | bytes 5898248 | tf_op jit(solution)/shard_map/ppermute | solution.py:368
  60.7 46.0 %collective-permute-start.3 = (bf16[384,1280]{1,0:T(8,128)(2,1)}, bf16[384,1280]{1,0:T(8,128)(2,1)}, u32[]{:S(2)}, u32[]{:S(2)}) collective-permute-start(bf16[384,1280]{1,0:T(8,128)(2,1)} %slice.153), channel_id=1, source_target_pairs={{0,8},{8,0},{16,24},{24,16},{1,9},{9,1},{17,25},{25,17},{2,10},{10... | collective-permute-start | bytes 2949128 | tf_op jit(solution)/shard_map/ppermute | solution.py:368
  67.0 46.7 %collective-permute-start.1 = (bf16[384,1280]{1,0:T(8,128)(2,1)}, bf16[384,1280]{1,0:T(8,128)(2,1)}, u32[]{:S(2)}, u32[]{:S(2)}) collective-permute-start(bf16[384,1280]{1,0:T(8,128)(2,1)} %slice.150), channel_id=1, source_target_pairs={{0,16},{8,24},{16,0},{24,8},{1,17},{9,25},{17,1},{25,9},{2,18},{10... | collective-permute-start | bytes 2949128 | tf_op jit(solution)/shard_map/ppermute | solution.py:368
  166.5 27.6 %all-to-all-start = ((bf16[4,320,768]{2,1,0:T(8,128)(2,1)}), bf16[4,320,768]{2,1,0:T(8,128)(2,1)}, u32[]{:S(2)}, u32[]{:S(2)}) async-start(bf16[4,320,768]{2,1,0:T(8,128)(2,1)} %get-tuple-element.58.refs_1_), calls=%async_computation | async-start | bytes 3932160 | tf_op jit(solution)/shard_map/all_to_all | solution.py:363
  235.0 43.9 %collective-permute-start.7 = (bf16[256,1280]{1,0:T(8,128)(2,1)}, bf16[256,1280]{1,0:T(8,128)(2,1)}, u32[]{:S(2)}, u32[]{:S(2)}) collective-permute-start(bf16[256,1280]{1,0:T(8,128)(2,1)} %constant_dynamic-slice_fusion.8), channel_id=1, source_target_pairs={{0,1},{1,0},{2,3},{3,2},{4,5},{5,4},{6,7},{7,6},{8,9},{9,8},{10,11... | collective-permute-start | bytes 1966088 | tf_op jit(solution)/shard_map/ppermute | solution.py:368
  236.6 11.3 %all-to-all-start.1 = ((bf16[4,80,768]{2,1,0:T(8,128)(2,1)}), bf16[4,80,768]{2,1,0:T(8,128)(2,1)S(1)}, u32[]{:S(2)}, u32[]{:S(2)}) async-start(bf16[4,80,768]{2,1,0:T(8,128)(2,1)} %slice_bitcast_fusion), calls=%async_computation.1 | async-start | bytes 983040 | tf_op jit(solution)/shard_map/all_to_all | solution.py:363
  247.9 61.1 %all-to-all-start.2 = ((bf16[4,240,768]{2,1,0:T(8,128)(2,1)}), bf16[4,240,768]{2,1,0:T(8,128)(2,1)}, u32[]{:S(2)}, u32[]{:S(2)}) async-start(bf16[4,240,768]{2,1,0:T(8,128)(2,1)} %bitcast.47), calls=%async_computation.2 | async-start | bytes 2949120 | tf_op jit(solution)/shard_map/all_to_all | solution.py:363
  277.7 16.4 %collective-permute-start.5 = (bf16[240,768]{1,0:T(8,128)(2,1)}, bf16[240,768]{1,0:T(8,128)(2,1)S(1)}, u32[]{:S(2)}, u32[]{:S(2)}) collective-permute-start(bf16[240,768]{1,0:T(8,128)(2,1)} %get-tuple-element.62.refs_2_), channel_id=1, source_target_pairs={{0,16},{8,24},{16,0},{24,8},{1,17},{9,25},{17,1},{25,9},{2,18},{10... | collective-permute-start | bytes 1105928 | tf_op jit(solution)/shard_map/ppermute | solution.py:368
  280.3 12.6 %collective-permute-start.8 = (bf16[64,1280]{1,0:T(8,128)(2,1)S(1)}, bf16[64,1280]{1,0:T(8,128)(2,1)S(1)}, u32[]{:S(2)}, u32[]{:S(2)}) collective-permute-start(bf16[64,1280]{1,0:T(8,128)(2,1)S(1)} %get-tuple-element.122), channel_id=1, source_target_pairs={{0,8},{8,0},{16,24},{24,16},{1,9},{9,1},{17,25},{25,17},{2,10},{10... | collective-permute-start | bytes 491528 | tf_op jit(solution)/shard_map/ppermute | solution.py:368
  281.7 12.1 %collective-permute-start.9 = (bf16[64,1280]{1,0:T(8,128)(2,1)S(1)}, bf16[64,1280]{1,0:T(8,128)(2,1)S(1)}, u32[]{:S(2)}, u32[]{:S(2)}) collective-permute-start(bf16[64,1280]{1,0:T(8,128)(2,1)S(1)} %get-tuple-element.124), channel_id=1, source_target_pairs={{0,16},{8,24},{16,0},{24,8},{1,17},{9,25},{17,1},{25,9},{2,18},{10... | collective-permute-start | bytes 491528 | tf_op jit(solution)/shard_map/ppermute | solution.py:368
  285.9 15.8 %collective-permute-start.6 = (bf16[240,768]{1,0:T(8,128)(2,1)S(1)}, bf16[240,768]{1,0:T(8,128)(2,1)S(1)}, u32[]{:S(2)}, u32[]{:S(2)}) collective-permute-start(bf16[240,768]{1,0:T(8,128)(2,1)S(1)} %copy-done.44), channel_id=1, source_target_pairs={{0,24},{8,16},{16,8},{24,0},{1,25},{9,17},{17,9},{25,1},{2,26},{10... | collective-permute-start | bytes 1105928 | tf_op jit(solution)/shard_map/ppermute | solution.py:368
  302.5 31.3 %collective-permute-start.18 = (bf16[64,1280]{1,0:T(8,128)(2,1)S(1)}, bf16[64,1280]{1,0:T(8,128)(2,1)S(1)}, u32[]{:S(2)}, u32[]{:S(2)}) collective-permute-start(bf16[64,1280]{1,0:T(8,128)(2,1)S(1)} %add_convert_fusion.4), channel_id=1, source_target_pairs={{0,4},{1,5},{2,6},{3,7},{4,0},{5,1},{6,2},{7,3},{8,12},{9,13},{10,... | collective-permute-start | bytes 491528 | tf_op jit(solution)/shard_map/ppermute | solution.py:368
  332.7 28.2 %collective-permute-start.11 = (bf16[240,768]{1,0:T(8,128)(2,1)}, bf16[240,768]{1,0:T(8,128)(2,1)S(1)}, u32[]{:S(2)}, u32[]{:S(2)}) collective-permute-start(bf16[240,768]{1,0:T(8,128)(2,1)} %get-tuple-element.66.refs_5_), channel_id=1, source_target_pairs={{0,8},{8,0},{16,24},{24,16},{1,9},{9,1},{17,25},{25,17},{2,10},{10... | collective-permute-start | bytes 1105928 | tf_op jit(solution)/shard_map/ppermute | solution.py:368
  333.9 26.8 %collective-permute-start.22 = (bf16[64,1280]{1,0:T(8,128)(2,1)S(1)}, bf16[64,1280]{1,0:T(8,128)(2,1)S(1)}, u32[]{:S(2)}, u32[]{:S(2)}) collective-permute-start(bf16[64,1280]{1,0:T(8,128)(2,1)S(1)} %add_convert_fusion.3), channel_id=1, source_target_pairs={{0,8},{8,0},{16,24},{24,16},{1,9},{9,1},{17,25},{25,17},{2,10},{10... | collective-permute-start | bytes 491528 | tf_op jit(solution)/shard_map/ppermute | solution.py:368
  358.1 32.8 %collective-permute-start.15 = (bf16[240,768]{1,0:T(8,128)(2,1)}, bf16[240,768]{1,0:T(8,128)(2,1)S(1)}, u32[]{:S(2)}, u32[]{:S(2)}) collective-permute-start(bf16[240,768]{1,0:T(8,128)(2,1)} %get-tuple-element.72.refs_9_), channel_id=1, source_target_pairs={{0,8},{8,0},{16,24},{24,16},{1,9},{9,1},{17,25},{25,17},{2,10},{10... | collective-permute-start | bytes 1105928 | tf_op jit(solution)/shard_map/ppermute | solution.py:368
  359.2 31.7 %collective-permute-start.16 = (bf16[240,768]{1,0:T(8,128)(2,1)}, bf16[240,768]{1,0:T(8,128)(2,1)S(1)}, u32[]{:S(2)}, u32[]{:S(2)}) collective-permute-start(bf16[240,768]{1,0:T(8,128)(2,1)} %get-tuple-element.73.refs_10_), channel_id=1, source_target_pairs={{0,16},{8,24},{16,0},{24,8},{1,17},{9,25},{17,1},{25,9},{2,18},{10... | collective-permute-start | bytes 1105928 | tf_op jit(solution)/shard_map/ppermute | solution.py:368
  359.5 31.3 %collective-permute-start.17 = (bf16[240,768]{1,0:T(8,128)(2,1)}, bf16[240,768]{1,0:T(8,128)(2,1)S(1)}, u32[]{:S(2)}, u32[]{:S(2)}) collective-permute-start(bf16[240,768]{1,0:T(8,128)(2,1)} %get-tuple-element.74.refs_11_), channel_id=1, source_target_pairs={{0,24},{8,16},{16,8},{24,0},{1,25},{9,17},{17,9},{25,1},{2,26},{10... | collective-permute-start | bytes 1105928 | tf_op jit(solution)/shard_map/ppermute | solution.py:368
  360.7 30.1 %collective-permute-start.12 = (bf16[240,768]{1,0:T(8,128)(2,1)}, bf16[240,768]{1,0:T(8,128)(2,1)S(1)}, u32[]{:S(2)}, u32[]{:S(2)}) collective-permute-start(bf16[240,768]{1,0:T(8,128)(2,1)} %get-tuple-element.67.refs_6_), channel_id=1, source_target_pairs={{0,16},{8,24},{16,0},{24,8},{1,17},{9,25},{17,1},{25,9},{2,18},{10... | collective-permute-start | bytes 1105928 | tf_op jit(solution)/shard_map/ppermute | solution.py:368
  361.0 29.9 %collective-permute-start.13 = (bf16[240,768]{1,0:T(8,128)(2,1)}, bf16[240,768]{1,0:T(8,128)(2,1)S(1)}, u32[]{:S(2)}, u32[]{:S(2)}) collective-permute-start(bf16[240,768]{1,0:T(8,128)(2,1)} %get-tuple-element.68.refs_7_), channel_id=1, source_target_pairs={{0,24},{8,16},{16,8},{24,0},{1,25},{9,17},{17,9},{25,1},{2,26},{10... | collective-permute-start | bytes 1105928 | tf_op jit(solution)/shard_map/ppermute | solution.py:368
  390.8 51.0 %collective-permute-start.35 = (bf16[128,1280]{1,0:T(8,128)(2,1)S(1)}, bf16[128,1280]{1,0:T(8,128)(2,1)}, u32[]{:S(2)}, u32[]{:S(2)}) collective-permute-start(bf16[128,1280]{1,0:T(8,128)(2,1)S(1)} %maximum_select_fusion.2), channel_id=1, source_target_pairs={{0,16},{8,24},{16,0},{24,8},{1,17},{9,25},{17,1},{25,9},{2,18},{10... | collective-permute-start | bytes 983048 | tf_op jit(solution)/shard_map/ppermute | solution.py:368
  414.7 30.4 %collective-permute-start.19 = (bf16[240,768]{1,0:T(8,128)(2,1)}, bf16[240,768]{1,0:T(8,128)(2,1)}, u32[]{:S(2)}, u32[]{:S(2)}) collective-permute-start(bf16[240,768]{1,0:T(8,128)(2,1)} %get-tuple-element.78.refs_13_), channel_id=1, source_target_pairs={{0,8},{8,0},{16,24},{24,16},{1,9},{9,1},{17,25},{25,17},{2,10},{10... | collective-permute-start | bytes 1105928 | tf_op jit(solution)/shard_map/ppermute | solution.py:368
  414.7 32.3 %collective-permute-start.20 = (bf16[240,768]{1,0:T(8,128)(2,1)}, bf16[240,768]{1,0:T(8,128)(2,1)}, u32[]{:S(2)}, u32[]{:S(2)}) collective-permute-start(bf16[240,768]{1,0:T(8,128)(2,1)} %get-tuple-element.79.refs_14_), channel_id=1, source_target_pairs={{0,16},{8,24},{16,0},{24,8},{1,17},{9,25},{17,1},{25,9},{2,18},{10... | collective-permute-start | bytes 1105928 | tf_op jit(solution)/shard_map/ppermute | solution.py:368
  416.2 32.3 %collective-permute-start.21 = (bf16[240,768]{1,0:T(8,128)(2,1)}, bf16[240,768]{1,0:T(8,128)(2,1)}, u32[]{:S(2)}, u32[]{:S(2)}) collective-permute-start(bf16[240,768]{1,0:T(8,128)(2,1)} %get-tuple-element.80.refs_15_), channel_id=1, source_target_pairs={{0,24},{8,16},{16,8},{24,0},{1,25},{9,17},{17,9},{25,1},{2,26},{10... | collective-permute-start | bytes 1105928 | tf_op jit(solution)/shard_map/ppermute | solution.py:368
  443.1 42.8 %collective-permute-start.36 = (bf16[256,1280]{1,0:T(8,128)(2,1)S(1)}, bf16[256,1280]{1,0:T(8,128)(2,1)}, u32[]{:S(2)}, u32[]{:S(2)}) collective-permute-start(bf16[256,1280]{1,0:T(8,128)(2,1)S(1)} %maximum_select_fusion.1), channel_id=1, source_target_pairs={{0,1},{1,0},{2,3},{3,2},{4,5},{5,4},{6,7},{7,6},{8,9},{9,8},{10,11... | collective-permute-start | bytes 1966088 | tf_op jit(solution)/shard_map/ppermute | solution.py:368
  451.7 14.5 %collective-permute-start.29 = (bf16[20,32,128]{2,1,0:T(8,128)(2,1)S(1)}, bf16[20,32,128]{2,1,0:T(8,128)(2,1)S(1)}, u32[]{:S(2)}, u32[]{:S(2)}) collective-permute-start(bf16[20,32,128]{2,1,0:T(8,128)(2,1)S(1)} %pad_maximum_fusion.11), channel_id=1, source_target_pairs={{0,4},{1,5},{2,6},{3,7},{4,0},{5,1},{6,2},{7,3},{8,12},{9,13},{10,... | collective-permute-start | bytes 491528 | tf_op jit(solution)/shard_map/ppermute | solution.py:368
  456.2 13.5 %collective-permute-start.30 = (bf16[20,32,128]{2,1,0:T(8,128)(2,1)S(1)}, bf16[20,32,128]{2,1,0:T(8,128)(2,1)S(1)}, u32[]{:S(2)}, u32[]{:S(2)}) collective-permute-start(bf16[20,32,128]{2,1,0:T(8,128)(2,1)S(1)} %pad_maximum_fusion.11), channel_id=1, source_target_pairs={{0,6},{1,7},{2,4},{3,5},{4,2},{5,3},{6,0},{7,1},{8,14},{9,15},{10,... | collective-permute-start | bytes 491528 | tf_op jit(solution)/shard_map/ppermute | solution.py:368
  (78 other events, 593.7 us)
Sparse Core Ops, SparseCore 0:
  11.7 34.7 all-gather.5
  48.2 37.9 all-gather.11
  87.8 38.1 all-gather.7
  127.5 38.1 all-gather.9
  167.2 90.9 all-gather.13

commit v3 on v2

v3 whole, which is shorter than its diff:
```python
import jax
import jax.numpy as jnp
from jax import lax
from jax.experimental import pallas as pl
from jax.experimental.pallas import tpu as pltpu
from jax.sharding import PartitionSpec as P

D = 1280
HEADS = 16
HD = 80
RANK = 16
ADAPTERS = 8
AR = ADAPTERS * RANK
TOK = 3072
PROMPT = 1536
ROWS = 768
QB = 256
PARTS = TOK // ROWS
LH = HEADS // PARTS
HALF = ROWS // 2
PH = LH // 2
PW = PH * HD
WIDTH = LH * HD
EPSILON = 1e-06
B = 256
f32, bf16 = jnp.float32, jnp.bfloat16


def nt(a, b):
    return lax.dot_general(a, b, (((1,), (1,)), ((), ())), preferred_element_type=f32)


def tn(a, b):
    return lax.dot_general(a, b, (((0,), (0,)), ((), ())), preferred_element_type=f32)


def nn(a, b):
    return lax.dot_general(a, b, (((1,), (0,)), ((), ())), preferred_element_type=f32)

def start_row(qpos, b1, b2):
    return jnp.where(qpos < PROMPT, 0, jnp.where(qpos < b1, PROMPT, jnp.where(qpos < b2, b1, b2)))

def first_block(i, b1, b2):
    q0 = i * B
    return jnp.where(q0 < b1, PROMPT, jnp.where(q0 < b2, b1, b2)) // B


def token_adapter(pos, meta):
    return jnp.where(
        pos < PROMPT, meta[2], jnp.where(pos < meta[0], meta[3], jnp.where(pos < meta[1], meta[4], meta[5]))
    )


def qkv_kernel(meta, first, low_ref, high_ref, gain_ref, wt_ref, down_ref, up_ref, scale_ref, *refs):
    out_ref, normed_ref, inner_ref, rows = refs[-4:]
    step = pl.program_id(0)

    @pl.when(step == 0)
    def _():
        rows[0:HALF, :] = low_ref[...]
        rows[HALF:ROWS, :] = high_ref[...]

    x = rows[pl.ds(pl.multiple_of(step * QB, QB), QB), :].astype(f32)
    q = lax.rsqrt(jnp.mean(x * x, axis=1, keepdims=True) + EPSILON)
    normed = (x * q * gain_ref[...]).astype(bf16)
    normed_ref[...] = normed
    pos = (first[0] + step) * QB + lax.broadcasted_iota(jnp.int32, (QB, 1), 0)
    lane = lax.broadcasted_iota(jnp.int32, (QB, 2 * AR), 1)
    chosen = (lane % AR) // RANK == token_adapter(pos, meta)
    inner = jnp.where(chosen, nn(normed, down_ref[...]), 0.0).astype(bf16)
    inner_ref[...] = inner
    out = nt(wt_ref[...], normed) + nt(up_ref[...], inner)
    out_ref[...] = (out * scale_ref[...]).astype(bf16)


def qkv_project(meta, chunk, low, high, gain, wt, down, up, scale, done):
    whole = lambda shape: pl.BlockSpec(shape, lambda i, *_: (0, 0))
    second = 1 if high is None else 0
    first = (chunk * (ROWS // QB))[None].astype(jnp.int32)
    return pl.pallas_call(
        qkv_kernel,
        out_shape=(
            jax.ShapeDtypeStruct((3 * WIDTH, TOK), bf16),
            jax.ShapeDtypeStruct((TOK, D), bf16),
            jax.ShapeDtypeStruct((TOK, 2 * AR), bf16),
        ),
        grid_spec=pltpu.PrefetchScalarGridSpec(
            num_scalar_prefetch=2,
            grid=(ROWS // QB,),
            in_specs=[
                whole((HALF, D)),
                pl.BlockSpec((HALF, D), lambda i, *_: (second, 0)),
                whole((1, D)),
                whole((3 * WIDTH, D)),
                whole((D, 2 * AR)),
                whole((3 * WIDTH, 2 * AR)),
                whole((3 * WIDTH, 1)),
            ]
            + [pl.BlockSpec(memory_space=pl.ANY)] * len(done),
            out_specs=[
                pl.BlockSpec((3 * WIDTH, QB), lambda i, m, first: (0, first[0] + i)),
                pl.BlockSpec((QB, D), lambda i, m, first: (first[0] + i, 0)),
                pl.BlockSpec((QB, 2 * AR), lambda i, m, first: (first[0] + i, 0)),
            ],
            scratch_shapes=[pltpu.VMEM((ROWS, D), bf16)],
        ),
        input_output_aliases={9 + i: i for i in range(len(done))},
        compiler_params=pltpu.CompilerParams(dimension_semantics=("arbitrary",), vmem_limit_bytes=60 << 20),
        cost_estimate=pl.CostEstimate(flops=2 * ROWS * D * (3 * WIDTH + 2 * AR), bytes_accessed=8 << 20, transcendentals=0),
        name="qkv_project",
    )(meta, first, low, low if high is None else high, gain, wt, down, up, scale, *done)


def adapter_kernel(meta, g0_ref, g1_ref, normed_ref, inner_ref, up_ref, first_ref, second_ref, facc, sacc):
    step = pl.program_id(0)

    @pl.when(step == 0)
    def _():
        facc[...] = jnp.zeros_like(facc)
        sacc[...] = jnp.zeros_like(sacc)

    grads = [g0_ref[0], g1_ref[0]]
    spread = nn(up_ref[0], grads[0]) + nn(up_ref[1], grads[1])
    pos = step * ROWS + lax.broadcasted_iota(jnp.int32, (1, ROWS), 1)
    rank = lax.broadcasted_iota(jnp.int32, (2 * AR, ROWS), 0)
    chosen = (rank % AR) // RANK == token_adapter(pos, meta)
    spread = jnp.where(chosen, spread, 0.0).astype(bf16)
    facc[...] += nn(spread, normed_ref[...])
    for p in range(2):
        sacc[p, 0] += nn(grads[p][0:PW], inner_ref[:, :AR])
        sacc[p, 1] += nn(grads[p][2 * PW :], inner_ref[:, AR:])

    @pl.when(step == PARTS - 1)
    def _():
        for c in range(D // 128):
            first_ref[c] = facc[:, c * 128 : (c + 1) * 128].astype(bf16)
        second_ref[...] = sacc[...].astype(bf16)


def adapter_grads(meta, grads, normed, inner, up):
    return pl.pallas_call(
        adapter_kernel,
        out_shape=(jax.ShapeDtypeStruct((D // 128, 2 * AR, 128), bf16), jax.ShapeDtypeStruct((2, 2, PW, AR), bf16)),
        grid_spec=pltpu.PrefetchScalarGridSpec(
            num_scalar_prefetch=1,
            grid=(PARTS,),
            in_specs=[pl.BlockSpec((1, 3 * PW, ROWS), lambda i, m: (i, 0, 0))] * 2
            + [
                pl.BlockSpec((ROWS, D), lambda i, m: (i, 0)),
                pl.BlockSpec((ROWS, 2 * AR), lambda i, m: (i, 0)),
                pl.BlockSpec((2, 2 * AR, 3 * PW), lambda i, m: (0, 0, 0)),
            ],
            out_specs=[
                pl.BlockSpec((D // 128, 2 * AR, 128), lambda i, m: (0, 0, 0)),
                pl.BlockSpec((2, 2, PW, AR), lambda i, m: (0, 0, 0, 0)),
            ],
            scratch_shapes=[pltpu.VMEM((2 * AR, D), f32), pltpu.VMEM((2, 2, PW, AR), f32)],
        ),
        compiler_params=pltpu.CompilerParams(dimension_semantics=("arbitrary",), vmem_limit_bytes=60 << 20),
        cost_estimate=pl.CostEstimate(flops=4 * TOK * D * 2 * AR, bytes_accessed=20 << 20, transcendentals=0),
        name="adapter_grads",
    )(meta, *grads, normed, inner, up)


HPB = PH
NEG = -1e30
FW = 512


def fwd_kernel(bounds, q_ref, k_ref, v_ref, o_ref, lse_ref, kp, qt, vt):
    b1, b2 = bounds[0], bounds[1]
    zpad = jnp.zeros((128 - HD, 128), bf16)
    for h in range(HPB):
        own = slice(h * HD, (h + 1) * HD)
        qt[h, 0:HD, :] = q_ref[own, :]
        qt[h, HD:128, :] = jnp.zeros((128 - HD, TOK), bf16)
        vt[h, 0:HD, :] = v_ref[own, :]
        vt[h, HD:96, :] = (lax.broadcasted_iota(jnp.int32, (16, TOK), 0) == 0).astype(bf16)
        for t in range(TOK // 128):
            kt = k_ref[own, t * 128:(t + 1) * 128]
            kp[h, t * 128:(t + 1) * 128, :] = jnp.concatenate([kt, zpad], axis=0).T

    def qblock(i, _):
        q0 = pl.multiple_of(i * B, B)
        qpos = q0 + lax.broadcasted_iota(jnp.int32, (1, B), 1)
        srow = start_row(qpos, b1, b2)

        def step(k0, width, masked, carry):
            ks = pl.ds(k0, width)
            ss = [nn(kp[h, ks, :], qt[h, :, pl.ds(q0, B)]) for h in range(HPB)]
            if masked:
                kpos = k0 + lax.broadcasted_iota(jnp.int32, (width, B), 0)
                ok = (kpos >= srow) & (kpos <= qpos)
                ss = [jnp.where(ok, s, NEG) for s in ss]
            out = []
            for h in range(HPB):
                m, acc = carry[h]
                m_new = jnp.maximum(m, jnp.max(ss[h], axis=0, keepdims=True))
                p = jnp.exp(ss[h] - m_new).astype(bf16)
                a = jnp.exp(m - m_new)
                out.append((m_new, acc * a + nn(vt[h, :, ks], p)))
            return tuple(out)

        full = jnp.minimum(i * B // FW, PROMPT // FW)
        lo = jnp.where(i < PROMPT // B, (FW // B) * (i * B // FW), first_block(i, b1, b2))
        carry = tuple((jnp.full((1, B), NEG, f32), jnp.zeros((96, B), f32)) for _ in range(HPB))
        carry = lax.fori_loop(0, full, lambda j, c: step(pl.multiple_of(j * FW, FW), FW, False, c), carry)
        carry = lax.fori_loop(lo, i + 1, lambda j, c: step(pl.multiple_of(j * B, B), B, True, c), carry)
        for h in range(HPB):
            m, acc = carry[h]
            l = acc[HD:HD + 1, :]
            o_ref[i // 3, h * HD:(h + 1) * HD, pl.ds(pl.multiple_of((i % 3) * B, B), B)] = (acc[0:HD, :] / l).astype(bf16)
            lse_ref[h, :, pl.ds(q0, B)] = m + jnp.log(l)
        return 0
    lax.fori_loop(0, TOK // B, qblock, 0)

def attn_fwd(bounds, qkvt, pair):
    rows = lambda a: pl.BlockSpec((PW, TOK), lambda i, b: (2 * a + pair, 0))
    return pl.pallas_call(
        fwd_kernel,
        out_shape=(jax.ShapeDtypeStruct((PARTS, PW, ROWS), bf16), jax.ShapeDtypeStruct((PH, 1, TOK), f32)),
        grid_spec=pltpu.PrefetchScalarGridSpec(
            num_scalar_prefetch=1,
            grid=(1,),
            in_specs=[rows(0), rows(1), rows(2)],
            out_specs=[pl.BlockSpec((PARTS, PW, ROWS), lambda i, b: (0, 0, 0)), pl.BlockSpec((PH, 1, TOK), lambda i, b: (0, 0, 0))],
            scratch_shapes=[pltpu.VMEM((HPB, TOK, 128), bf16), pltpu.VMEM((HPB, 128, TOK), bf16), pltpu.VMEM((HPB, 96, TOK), bf16)],
        ),
        compiler_params=pltpu.CompilerParams(dimension_semantics=("arbitrary",), vmem_limit_bytes=60 << 20),
        cost_estimate=pl.CostEstimate(flops=20 * 10**9, bytes_accessed=5 << 20, transcendentals=0),
        name="attn_fwd",
    )(bounds, qkvt, qkvt, qkvt)


def parts3(x):
    hi = x.astype(bf16)
    r = x - hi.astype(f32)
    mid = r.astype(bf16)
    lo = (r - mid.astype(f32)).astype(bf16)
    return hi, mid, lo

def bwd_kernel(meta, scale_ref, q_ref, k_ref, v_ref, do_ref, o_ref, lse_ref, out_ref, kp, vp, qt, dot, qr, dor, dk, dv, dqt):
    b1, b2 = meta[0], meta[1]
    row16 = lax.broadcasted_iota(jnp.int32, (16, 128), 0)
    ones3 = (row16 < 3).astype(bf16)
    pad = jnp.zeros((32, 128), bf16)
    scale = scale_ref[...]

    def tail(x):
        hi, mid, lo = parts3(-x)
        rest = jnp.where(row16 == 1, mid.astype(f32), jnp.where(row16 == 2, lo.astype(f32), 0.0))
        return jnp.where(row16 == 0, hi.astype(f32), rest).astype(bf16)

    @pl.loop(0, 2 * PARTS)
    def _(step):
        chunk = step // 2
        for t in range(3):
            off = pl.multiple_of((step % 2) * HALF + t * 128, 128)
            sl, here = pl.ds(pl.multiple_of(chunk * ROWS + off, 128), 128), pl.ds(off, 128)
            q, k, v = q_ref[:, sl], k_ref[:, sl], v_ref[:, sl]
            do, o = do_ref[chunk, :, here], o_ref[chunk, :, here]
            delta = jnp.sum(do.astype(f32) * o.astype(f32), axis=0, keepdims=True)
            qa = jnp.concatenate([q, tail(lse_ref[0, :, sl]), pad], axis=0)
            da = jnp.concatenate([do, tail(delta), pad], axis=0)
            qt[:, sl] = qa
            dot[:, sl] = da
            qr[sl, :] = qa.T
            dor[sl, :] = da.T
            kp[sl, :] = jnp.concatenate([k, ones3, pad], axis=0).T
            vp[sl, :] = jnp.concatenate([v, ones3, pad], axis=0).T

    dk[...] = jnp.zeros_like(dk)
    dv[...] = jnp.zeros_like(dv)
    dqt[...] = jnp.zeros_like(dqt)

    def block(k0, q0, width, masked):
        k0, q0 = pl.multiple_of(k0, width), pl.multiple_of(q0, width)
        ks, qs = pl.ds(k0, width), pl.ds(q0, width)
        p = jnp.exp(nn(kp[ks, :], qt[:, qs]))
        if masked:
            qpos = q0 + lax.broadcasted_iota(jnp.int32, (1, width), 1)
            kpos = k0 + lax.broadcasted_iota(jnp.int32, (width, width), 0)
            p = jnp.where((kpos >= start_row(qpos, b1, b2)) & (kpos <= qpos), p, 0.0)
        ds = (p * nn(vp[ks, :], dot[:, qs])).astype(bf16)
        dv[ks, :] += nn(p.astype(bf16), dor[qs, :])
        dk[ks, :] += nn(ds, qr[qs, :])
        dqt[:, qs] += nn(k_ref[:, ks], ds)

    @pl.loop(0, 12)
    def _(n):
        qb = jnp.where(n < 9, 3 + n // 3, jnp.where(n == 9, 1, 2))
        kb = jnp.where(n < 9, n % 3, jnp.where(n == 11, 1, 0))
        block(kb * FW, qb * FW, FW, False)

    @pl.loop(0, TOK // B)
    def _(i):
        lo = jnp.where(i < PROMPT // B, 2 * (i // 2), first_block(i, b1, b2))

        @pl.loop(lo, i + 1)
        def _(j):
            block(j * B, i * B, B, True)

    @pl.loop(0, 2 * PARTS)
    def _(step):
        chunk = step // 2
        for t in range(3):
            off = pl.multiple_of((step % 2) * HALF + t * 128, 128)
            sl, here = pl.ds(pl.multiple_of(chunk * ROWS + off, 128), 128), pl.ds(off, 128)
            dq = dqt[:, sl].astype(bf16).astype(f32) * scale
            out_ref[chunk, 0, :, here] = dq.astype(bf16)
            out_ref[chunk, 1, :, here] = dk[sl, :].T[0:HD, :].astype(bf16)
            out_ref[chunk, 2, :, here] = dv[sl, :].T[0:HD, :].astype(bf16)


def attn_bwd(meta, scale, qkvt, grad, mixture, logsum, pair):
    rows = lambda a: pl.BlockSpec((HD, TOK), lambda i, b: (LH * a + PH * pair + i, 0))
    chunks = pl.BlockSpec((PARTS, HD, ROWS), lambda i, b: (0, i, 0))
    return pl.pallas_call(
        bwd_kernel,
        out_shape=jax.ShapeDtypeStruct((PARTS, 3, PW, ROWS), bf16),
        grid_spec=pltpu.PrefetchScalarGridSpec(
            num_scalar_prefetch=1,
            grid=(PH,),
            in_specs=[
                pl.BlockSpec((HD, 1), lambda i, b: (0, 0)),
                rows(0),
                rows(1),
                rows(2),
                chunks,
                chunks,
                pl.BlockSpec((1, 1, TOK), lambda i, b: (i, 0, 0)),
            ],
            out_specs=pl.BlockSpec((PARTS, 3, HD, ROWS), lambda i, b: (0, 0, i, 0)),
            scratch_shapes=[pltpu.VMEM((TOK, 128), bf16)] * 2
            + [pltpu.VMEM((128, TOK), bf16)] * 2
            + [pltpu.VMEM((TOK, 128), bf16)] * 2
            + [pltpu.VMEM((TOK, 128), f32)] * 2
            + [pltpu.VMEM((HD, TOK), f32)],
        ),
        compiler_params=pltpu.CompilerParams(dimension_semantics=("arbitrary",), vmem_limit_bytes=60 << 20),
        cost_estimate=pl.CostEstimate(flops=36 * 10**9, bytes_accessed=16 << 20, transcendentals=0),
        name="attn_bwd",
    )(meta, scale, qkvt, qkvt, qkvt, grad, mixture, logsum)


def normalize(values, gain_vec):
    scaling = lax.rsqrt(jnp.mean(values * values, axis=-1, keepdims=True) + EPSILON)
    return (values * scaling * gain_vec, scaling)


def normalize_back(values, scaling, gain_vec, upstream):
    weighted = gain_vec * upstream
    return scaling * weighted - values * scaling**3 * jnp.mean(values * weighted, axis=-1, keepdims=True)


def by_pair(query, key, value):
    rows = query.shape[0]
    split = jnp.stack([query, key, value], axis=1).reshape(rows, 3, PARTS, 2, PW)
    return jnp.transpose(split, (0, 3, 2, 1, 4)).reshape(rows, 3 * D)


def exchange(value):
    return lax.all_to_all(value, "heads", split_axis=0, concat_axis=0, tiled=True)


def swap(value, axis, mask):
    count = lax.axis_size(axis)
    return lax.ppermute(value, axis, [(i, i ^ mask) for i in range(count)])


def piece(value, index, count):
    rows = value.shape[-2] // count
    return lax.dynamic_slice_in_dim(value, index * rows, rows, axis=value.ndim - 2)


def sum_low(*terms):
    total = terms[0].astype(f32)
    for term in terms[1:]:
        total = total + term.astype(f32)
    return total.astype(bf16)


def far_bits():
    bits = [2]
    while bits[-1] * 2 < lax.axis_size("fsdp"):
        bits.append(bits[-1] * 2)
    return bits


def sum_far(value):
    bits = far_bits()
    for bit, twice in zip(bits[0::2], bits[1::2]):
        value = sum_low(value, *[swap(value, "fsdp", m) for m in (bit, twice, bit | twice)])
    if len(bits) % 2:
        value = sum_low(value, swap(value, "fsdp", bits[-1]))
    return value


def scatter_near(value):
    core = lax.axis_index("fsdp") & 1
    return sum_low(piece(value, core, 2), swap(piece(value, 1 - core, 2), "fsdp", 1))


def paired(value, axis, mask, high):
    other = swap(value, axis, mask)
    return jnp.where(
        high, jnp.concatenate([other, value], axis=-2), jnp.concatenate([value, other], axis=-2)
    )


def gather_near(value):
    return paired(value, "fsdp", 1, lax.axis_index("fsdp") % 2 == 1)


def scatter_heads(value):
    part = lax.axis_index("heads")
    terms = [swap(piece(value, part ^ m, PARTS), "heads", m) for m in (1, 2, 3)]
    return sum_low(piece(value, part, PARTS), *terms)


def gather_heads(value):
    part = lax.axis_index("heads")
    near, far, both = [swap(value, "heads", m) for m in (1, 2, 3)]
    odd, high = part % 2 == 1, part >= 2
    low_pair = [jnp.where(odd, near, value), jnp.where(odd, value, near)]
    high_pair = [jnp.where(odd, both, far), jnp.where(odd, far, both)]
    pieces = [jnp.where(high, b, a) for a, b in zip(low_pair, high_pair)]
    pieces += [jnp.where(high, a, b) for a, b in zip(low_pair, high_pair)]
    return jnp.concatenate(pieces, axis=-2)


def body(
    inputs,
    cotangent,
    lengths,
    adapter_ids,
    query_weight,
    key_weight,
    value_weight,
    out_weight,
    up_weight,
    down_weight,
    attn_gain,
    mlp_gain,
    query_scale,
    adapter_in,
    adapter_out,
):
    part = lax.axis_index("heads")
    rows = inputs[0]
    near_high = swap(rows[HALF:], "heads", 1)
    far_low = swap(rows[:HALF], "heads", 2)
    near_low = swap(rows[:HALF], "heads", 1)
    far_high = swap(rows[HALF:], "heads", 2)
    both_low = swap(far_low, "heads", 1)
    both_high = swap(near_high, "heads", 2)

    offset = part * ROWS
    ends = PROMPT + jnp.cumsum(lengths[0])
    bounds = ends[:2].astype(jnp.int32)
    ids = adapter_ids[0]
    meta = jnp.concatenate([bounds, ids, part[None].astype(jnp.int32)])
    places = offset + jnp.arange(ROWS, dtype=jnp.int32)
    token = token_adapter(places, meta)
    chosen = (token[:, None] == (jnp.arange(AR, dtype=jnp.int32) // RANK)[None, :]).astype(f32)
    chosen2 = jnp.concatenate([chosen, chosen], axis=1)
    flat_down = jnp.transpose(adapter_in, (0, 2, 1, 3)).reshape(4, D, AR)
    flat_up = adapter_out.reshape(4, AR, D)
    gain_attn = attn_gain.astype(f32)
    gain_mlp = mlp_gain.astype(f32)

    def mine(weight):
        return lax.dynamic_slice_in_dim(weight, part * WIDTH, WIDTH, axis=1)

    weights_mine = jnp.concatenate([mine(query_weight), mine(key_weight), mine(value_weight)], axis=1)
    weights_mine = lax.all_gather(weights_mine, "fsdp", axis=0, tiled=True)
    w_out = lax.all_gather(out_weight, "fsdp", axis=0, tiled=True)
    w_up = lax.all_gather(up_weight, "fsdp", axis=0, tiled=True)
    w_down = lax.all_gather(down_weight, "fsdp", axis=0, tiled=True)
    weights_all = lax.all_gather(by_pair(query_weight, key_weight, value_weight), "fsdp", axis=0, tiled=True)

    down_pair = jnp.concatenate([flat_down[0], flat_down[1]], axis=1)
    zero = jnp.zeros((AR, D), bf16)
    up_query = jnp.concatenate([flat_up[0], zero])
    up_value = jnp.concatenate([zero, flat_up[1]])
    up_pairs = by_pair(up_query, jnp.zeros_like(up_query), up_value)
    up_mine = jnp.concatenate([mine(up_query), jnp.zeros((2 * AR, WIDTH), bf16), mine(up_value)], axis=1)
    up_heads = jnp.transpose(up_mine.reshape(2 * AR, 3, 2, PW), (2, 0, 1, 3)).reshape(2, 2 * AR, 3 * PW)
    scale_row = query_scale * HD ** (-0.5)
    scale_mine = jnp.concatenate([jnp.tile(scale_row, LH), jnp.ones((2 * WIDTH,), f32)])[:, None]

    wt, ut = weights_mine.T, up_mine.T
    done = ()
    for m, low, high in ((0, rows, None), (1, near_low, near_high), (2, far_low, far_high), (3, both_low, both_high)):
        done = qkv_project(meta, part ^ m, low, high, gain_attn[None, :], wt, down_pair, ut, scale_mine, done)
    qkvt, normed_all, inner_all = done
    out_pairs = w_out.reshape(PARTS, 2, PW, D)
    pair_weight = [out_pairs[:, p].reshape(PARTS * PW, D) for p in range(2)]
    forward = [attn_fwd(bounds, qkvt, 0)]
    mixed_first = exchange(forward[0][0])
    forward.append(attn_fwd(bounds, qkvt, 1))
    mixed_second = exchange(forward[1][0])

    rows_in = inputs[0].astype(f32)
    scaling_attn = lax.rsqrt(jnp.mean(rows_in * rows_in, axis=-1, keepdims=True) + EPSILON)

    middle = rows_in + tn(mixed_first.reshape(PARTS * PW, ROWS), pair_weight[0])
    middle = middle + tn(mixed_second.reshape(PARTS * PW, ROWS), pair_weight[1])
    normed_mlp, scaling_mlp = normalize(middle, gain_mlp)
    normed_mlp_low = normed_mlp.astype(bf16)
    inner_up = (nn(normed_mlp_low, flat_down[2]) * chosen).astype(bf16)
    before = nn(normed_mlp_low, w_up) + nn(inner_up, flat_up[2])
    gate = jax.nn.sigmoid(before)
    hidden_low = (before * gate).astype(bf16)
    inner_down = (nn(hidden_low, flat_down[3]) * chosen).astype(bf16)
    outputs = (middle + (nn(hidden_low, w_down) + nn(inner_down, flat_up[3]))).astype(bf16)

    upstream = cotangent[0].astype(f32)
    grad_after = cotangent[0]
    spread_down = (nt(grad_after, flat_up[3]) * chosen).astype(bf16)
    grad_hidden = nt(grad_after, w_down) + nt(spread_down, flat_down[3])
    grad_before = (grad_hidden * gate * (1.0 + before * (1.0 - gate))).astype(bf16)
    spread_up = (nt(grad_before, flat_up[2]) * chosen).astype(bf16)
    grad_normed_mlp = nt(grad_before, w_up) + nt(spread_up, flat_down[2])
    grad_middle = upstream + normalize_back(middle, scaling_mlp, gain_mlp, grad_normed_mlp)
    grad_branch = grad_middle.astype(bf16)
    grad_heads = [exchange(nt(w, grad_branch).astype(bf16).reshape(PARTS, PW, ROWS)) for w in pair_weight]

    terms = [tn(spread_up, normed_mlp_low), tn(spread_down, hidden_low), tn(inner_up, grad_before), tn(inner_down, grad_after)]
    mlp_total = scatter_near(jnp.concatenate(terms).astype(bf16))
    mlp_total, grad_heads[0] = lax.optimization_barrier((mlp_total, grad_heads[0]))
    mlp_total = scatter_heads(mlp_total)
    grad_first_pair = attn_bwd(meta, scale_row[:, None], qkvt, grad_heads[0], forward[0][0], forward[0][1], 0)
    arrived = [exchange(grad_first_pair.reshape(PARTS, 3 * PW, ROWS))]
    mlp_total, grad_heads[1] = lax.optimization_barrier((mlp_total, grad_heads[1]))
    mlp_total = sum_far(mlp_total)
    grad_second_pair = attn_bwd(meta, scale_row[:, None], qkvt, grad_heads[1], forward[1][0], forward[1][1], 1)
    arrived.append(exchange(grad_second_pair.reshape(PARTS, 3 * PW, ROWS)))

    grads = [g.reshape(PARTS, 3 * PW, ROWS) for g in (grad_first_pair, grad_second_pair)]
    meta, arrived[0] = lax.optimization_barrier((meta, arrived[0]))
    first_attn, second_attn = adapter_grads(meta, grads, normed_all, inner_all, up_heads)

    slot = PARTS * 3 * PW

    def back(p):
        both, cut = arrived[p].reshape(slot, ROWS), slice(p * slot, (p + 1) * slot)
        contract = (((0,), (1,)), ((), ()))
        return (
            lax.dot_general(both, weights_all[:, cut], contract, preferred_element_type=f32),
            lax.dot_general(both, up_pairs[:, cut], contract, preferred_element_type=f32),
        )

    tiles = D // 128
    mlp_total = gather_heads(mlp_total)
    near_first = scatter_near(first_attn)
    near_second = scatter_near(second_attn.reshape(tiles, -1, 128))
    grad_normed, spread = back(0)
    near_first, grad_normed = lax.optimization_barrier((near_first, grad_normed))
    total = sum_far(jnp.concatenate([scatter_heads(near_first), near_second]))
    grad_second_part, spread_second = back(1)
    total, grad_second_part = lax.optimization_barrier((total, grad_second_part))
    total = gather_near(gather_heads(total))
    mlp_total = gather_near(mlp_total)
    grad_normed, spread = grad_normed + grad_second_part, spread + spread_second
    first_total = total[:tiles]
    second_total = total[tiles:].reshape(tiles, 2, PARTS, -1, 128)
    second_total = jnp.transpose(second_total, (2, 0, 1, 3, 4))
    grad_normed = grad_normed + nt((spread * chosen2).astype(bf16), down_pair)
    grad_inputs = grad_middle + normalize_back(rows_in, scaling_attn, gain_attn, grad_normed)

    first_pair = jnp.transpose(first_total.reshape(tiles, 2, ADAPTERS, RANK, 128), (1, 2, 0, 4, 3))
    first_rest = jnp.transpose(mlp_total[: 2 * AR].reshape(2, ADAPTERS, RANK, D), (0, 1, 3, 2))
    grad_first = jnp.concatenate([first_pair.reshape(2, ADAPTERS, D, RANK), first_rest]).astype(f32)
    second_pair = jnp.transpose(second_total.reshape(PARTS, 2, 2, PW, AR), (2, 4, 0, 1, 3)).reshape(2 * AR, D)
    grad_second = jnp.concatenate([second_pair, mlp_total[2 * AR :]]).astype(f32).reshape(4, ADAPTERS, RANK, D)
    return (outputs[None], grad_inputs[None], grad_first, grad_second)


def solution(mesh):
    placed = (
        P("fsdp", "heads", None),
        P("fsdp", "heads", None),
        P("fsdp", None),
        P("fsdp", None),
        P("fsdp", None),
        P("fsdp", None),
        P("fsdp", None),
        P("fsdp", None),
        P("fsdp", None),
        P("fsdp", None),
        P(),
        P(),
        P(),
        P(),
        P(),
    )
    return jax.shard_map(
        body,
        mesh=mesh,
        in_specs=placed,
        out_specs=(P("fsdp", "heads", None), P("fsdp", "heads", None), P(), P()),
        check_vma=False,
    )
```

time: 540 us -> 500 us (0.926)
  waiting for transfers between devices: 81.2 us -> 55.3 us
  local copies, waits for them, and re-layouts: 67 us -> 54.1 us
    ppermute x37 -> x29, waiting for transfers between devices: 68 us -> 42.9 us  [swap(): return lax.ppermute(value, axis, [(i, i ^ mask) for i in range(count)])]
    ppermute x37 -> x29, starting transfers between devices: 47.1 us -> 32.6 us  [swap(): return lax.ppermute(value, axis, [(i, i ^ mask) for i in range(count)])]
    all_to_all x3 -> x6, starting transfers between devices: 12.6 us -> 23.7 us  [exchange(): lax.all_to_all(value, 'heads', split_axis=0, concat_axis=0, tiled=True)]
    dot_general x6, matrix products: 15.8 us -> 22.5 us  [nn(): lax.dot_general(a, b, (((1,), (0,)), ((), ())), preferred_element_type=f32)]
    dot_general x7 -> x3, matrix products: 29.3 us -> 23.2 us  [the longest x2 19.1 us: back(): lax.dot_general(both, weights_all[:, cut], contract, preferred_element_ty...]
    dot_general x8 -> x9, matrix products: 24.7 us -> 28.8 us  [nt(): lax.dot_general(a, b, (((1,), (1,)), ((), ())), preferred_element_type=f32)]
    unnamed x147 -> x114, local copies, waits for them, and re-layouts: 16.5 us -> 12.6 us
    all_to_all x3 -> x6, waiting for transfers between devices: 11.2 us -> 10.4 us  [exchange(): lax.all_to_all(value, 'heads', split_axis=0, concat_axis=0, tiled=True)]
  transfers between devices with their start and end apart: 45 -> 40, of which waited for: 13 -> 10; matrix products, arithmetic and copies ran while one was open for 26% -> 29% of each run, Pallas kernels for 37% -> 40%
where the time goes in v3:
time: 500 us; the launch traced here: 492 us
  Pallas kernels  196 us (39%)
  matrix products  84.4 us (17%)
  starting transfers between devices  56.5 us (11%)
  waiting for transfers between devices  55.3 us (11%)
  local copies, waits for them, and re-layouts  54.1 us (11%)
  other arithmetic  30.5 us (6%)
  between operations  15 us (3%)
    pallas_call x2, Pallas kernels, attn_bwd(): pl.pallas_call(bwd_kernel, out_shape=jax.ShapeDtypeStruct((PARTS, 3, PW,...  88.9 us
    pallas_call x2, Pallas kernels, attn_fwd(): pl.pallas_call(fwd_kernel, out_shape=(jax.ShapeDtypeStruct((PARTS, PW, RO...  60.5 us
    ppermute x29, waiting for transfers between devices, swap(): return lax.ppermute(value, axis, [(i, i ^ mask) for i in range(count)])  42.9 us
    pallas_call x4, Pallas kernels, qkv_project(): pl.pallas_call(qkv_kernel, out_shape=(jax.ShapeDtypeStruct((3 * WIDTH, TO...  35 us
    ppermute x29, starting transfers between devices, swap(): return lax.ppermute(value, axis, [(i, i ^ mask) for i in range(count)])  32.6 us
    dot_general x9, matrix products, nt(): lax.dot_general(a, b, (((1,), (1,)), ((), ())), preferred_element_type=f32)  28.8 us
    all_to_all x6, starting transfers between devices, exchange(): lax.all_to_all(value, 'heads', split_axis=0, concat_axis=0, tiled=True)  23.7 us
    dot_general x6, matrix products, nn(): lax.dot_general(a, b, (((1,), (0,)), ((), ())), preferred_element_type=f32)  22.5 us
  transfers between devices with their start and end apart: 40, of which 10 were waited for; matrix products, arithmetic and copies ran while one was open for 29% of the time, Pallas kernels for 40%

profile of v3, /device:TPU:9, one launch (start us, length us, event | category | flops | bytes accessed | tf_op | source)
XLA Modules:
  0.0 491.7 jit_solution(8833607896830711520)
XLA Ops:
  43.2 14.8 %collective-permute-done.2.high_ref = bf16[384,1280]{1,0:T(8,128)(2,1)} collective-permute-done((bf16[384,1280]{1,0:T(8,128)(2,1)}, bf16[384,1280]{1,0:T(8,128)(2,1)}, u32[]{:S(2)}, u32[]{:S(2)}) %collective-permute-start.2) | collective-permute-done | bytes 983072 | tf_op jit(solution)/shard_map/ppermute | solution.py:368
  69.1 4.3 copy.63
  73.4 8.7 %qkv_project.4 = (bf16[960,3072]{1,0:T(8,128)(2,1)}, bf16[3072,1280]{1,0:T(8,128)(2,1)}, bf16[3072,256]{1,0:T(8,128)(2,1)}) custom-call(s32[7]{0:T(128)} %pad_add_fusion.meta, s32[1]{0:T(128)} %bitcast.18.first, bf16[768,1280]{1,0:T(8,128)(2,1)} %bitcast.144, bf16[768,1280]{1,0:T(8,128)(2,1)} %bitcast.145, f32[1,1280]{1,0:T(1,128)} %broadcast_in_dim.65.gain_ref, ...), custom_call_target="tpu_custom_call" | custom-call | flops 2390753280 | bytes 8388608 | tf_op jit(solution)/shard_map/qkv_project/pallas_call | solution.py:80
  82.1 8.7 %qkv_project.5 = (bf16[960,3072]{1,0:T(8,128)(2,1)}, bf16[3072,1280]{1,0:T(8,128)(2,1)}, bf16[3072,256]{1,0:T(8,128)(2,1)}) custom-call(s32[7]{0:T(128)} %pad_add_fusion.meta, s32[1]{0:T(128)} %bitcast.17.first, bf16[384,1280]{1,0:T(8,128)(2,1)} %collective-permute-done.5.low_ref, ...), custom_call_target="tpu_custom_call", output_to_operand_aliasing={{0}: (9, {}), {1}: (10, {}), {2}: (11, {})} | custom-call | flops 2390753280 | bytes 8388608 | tf_op jit(solution)/shard_map/qkv_project/pallas_call | solution.py:80
  90.8 8.9 %qkv_project.6 = (bf16[960,3072]{1,0:T(8,128)(2,1)}, bf16[3072,1280]{1,0:T(8,128)(2,1)}, bf16[3072,256]{1,0:T(8,128)(2,1)}) custom-call(s32[7]{0:T(128)} %pad_add_fusion.meta, s32[1]{0:T(128)} %bitcast.16.first, bf16[384,1280]{1,0:T(8,128)(2,1)} %collective-permute-done.low_ref, ...), custom_call_target="tpu_custom_call", output_to_operand_aliasing={{0}: (9, {}), {1}: (10, {}), {2}: (11, {})} | custom-call | flops 2390753280 | bytes 8388608 | tf_op jit(solution)/shard_map/qkv_project/pallas_call | solution.py:80
  99.6 8.8 %qkv_project.7 = (bf16[960,3072]{1,0:T(8,128)(2,1)}, bf16[3072,1280]{1,0:T(8,128)(2,1)}, bf16[3072,256]{1,0:T(8,128)(2,1)}) custom-call(s32[7]{0:T(128)} %pad_add_fusion.meta, s32[1]{0:T(128)} %bitcast.5.first, bf16[384,1280]{1,0:T(8,128)(2,1)} %collective-permute-done.1.low_ref, ...), custom_call_target="tpu_custom_call", output_to_operand_aliasing={{0}: (9, {}), {1}: (10, {}), {2}: (11, {})} | custom-call | flops 2390753280 | bytes 8388608 | tf_op jit(solution)/shard_map/qkv_project/pallas_call | solution.py:80
  108.4 30.3 %attn_fwd.2 = (bf16[4,160,768]{2,1,0:T(8,128)(2,1)}, f32[2,1,3072]{2,1,0:T(1,128)}) custom-call(s32[2]{0:T(128)} %copy-done.49, bf16[960,3072]{1,0:T(8,128)(2,1)} %get-tuple-element.41.q_ref.k_ref.v_ref, bf16[960,3072]{1,0:T(8,128)(2,1)} %get-tuple-element.41.q_ref.k_ref.v_ref, bf16[960,3072]{1,0:T(8,128)(2,1)} %get-tuple-element.41.q_ref.k_ref.v_ref), custom_call_target="tpu_custom_call" | custom-call | flops 20000000000 | bytes 5242880 | tf_op jit(solution)/shard_map/attn_fwd/pallas_call | solution.py:219
  142.2 30.3 %attn_fwd.3 = (bf16[4,160,768]{2,1,0:T(8,128)(2,1)}, f32[2,1,3072]{2,1,0:T(1,128)}) custom-call(s32[2]{0:T(128)} %copy-done.49, bf16[960,3072]{1,0:T(8,128)(2,1)} %get-tuple-element.41.q_ref.k_ref.v_ref, bf16[960,3072]{1,0:T(8,128)(2,1)} %get-tuple-element.41.q_ref.k_ref.v_ref, bf16[960,3072]{1,0:T(8,128)(2,1)} %get-tuple-element.41.q_ref.k_ref.v_ref), custom_call_target="tpu_custom_call" | custom-call | flops 20000000000 | bytes 5242880 | tf_op jit(solution)/shard_map/attn_fwd/pallas_call | solution.py:219
  173.4 3.8 all-to-all-start.1
  189.4 4.5 multiply_reduce_fusion.1
  197.8 5.3 %fusion.61 = f32[768,1280]{1,0:T(8,128)S(1)} fusion(bf16[768,1280]{1,0:T(8,128)(2,1)} %copy-done.9, bf16[1280,1280]{1,0:T(8,128)(2,1)} %all-gather.10.cloned.1.call-done), kind=kOutput, calls=%fused_computation.169 | convolution fusion | flops 2516582400 | bytes 9175040 | tf_op jit(solution)/shard_map/dot_general | solution.py:38
  203.1 3.7 multiply_convert_fusion
  206.8 4.9 fusion.21
  227.5 4.4 all-to-all-start.2
  231.9 4.6 convolution_convert_fusion.4
  237.7 6.7 %all-to-all-done.2.do_ref = bf16[4,160,768]{2,1,0:T(8,128)(2,1)} async-done(((bf16[4,160,768]{2,1,0:T(8,128)(2,1)}), bf16[4,160,768]{2,1,0:T(8,128)(2,1)}, u32[]{:S(2)}, u32[]{:S(2)}) %all-to-all-start.2) | async-done | bytes 983072 | tf_op jit(solution)/shard_map/all_to_all | solution.py:363
  244.4 4.4 all-to-all-start.4
  251.7 6.5 %fusion.62 = f32[768,1280]{1,0:T(8,128)} fusion(bf16[768,1280]{1,0:T(8,128)(2,1)S(1)} %copy-done.21, bf16[1280,1280]{1,0:T(8,128)(2,1)} %all-gather.12.cloned.1.call-done), kind=kOutput, calls=%fused_computation.170 | convolution fusion | flops 2516582400 | bytes 9175040 | tf_op jit(solution)/shard_map/dot_general | solution.py:38
  258.2 5.9 %collective-permute-done.7 = bf16[64,1280]{1,0:T(8,128)(2,1)S(1)} collective-permute-done((bf16[64,1280]{1,0:T(8,128)(2,1)S(1)}, bf16[64,1280]{1,0:T(8,128)(2,1)S(1)}, u32[]{:S(2)}, u32[]{:S(2)}) %collective-permute-start.7) | collective-permute-done | bytes 163872 | tf_op jit(solution)/shard_map/ppermute | solution.py:368
  268.2 4.3 collective-permute-start.22
  273.7 5.2 %fusion.17 = bf16[1,768,1280]{2,1,0:T(8,128)(2,1)} fusion(f32[768,1280]{1,0:T(8,128)} %copy-done, f32[768,1280]{1,0:T(8,128)} %fusion.62, bf16[768,128]{1,0:T(8,128)(2,1)S(1)} %fusion.29, bf16[128,1280]{1,0:T(8,128)(2,1)S(1)} %bitcast.174), kind=kOutput, calls=%fused_computation.33 | convolution fusion | flops 254607360 | bytes 10354688 | tf_op jit(solution)/shard_map/dot_general | solution.py:38
  279.0 8.4 %collective-permute-done.24 = bf16[64,1280]{1,0:T(8,128)(2,1)S(1)} collective-permute-done((bf16[64,1280]{1,0:T(8,128)(2,1)S(1)}, bf16[64,1280]{1,0:T(8,128)(2,1)S(1)}, u32[]{:S(2)}, u32[]{:S(2)}) %collective-permute-start.24) | collective-permute-done | bytes 163872 | tf_op jit(solution)/shard_map/ppermute | solution.py:368
  290.2 44.5 %attn_bwd.2 = bf16[4,3,160,768]{3,2,1,0:T(8,128)(2,1)} custom-call(s32[7]{0:T(128)} %pad_add_fusion.meta, f32[80,1]{1,0:T(8,128)} %copy.72.scale_ref, bf16[960,3072]{1,0:T(8,128)(2,1)} %get-tuple-element.41.q_ref.k_ref.v_ref, bf16[960,3072]{1,0:T(8,128)(2,1)} %get-tuple-element.41.q_ref.k_ref.v_ref, bf16[960,3072]{1,0:T(8,128)(2,1)} %get-tuple-element.41.q_ref.k_ref.v_ref, ...), custom_call_target="tpu_custom_call" | custom-call | flops 35999997952 | bytes 16777216 | tf_op jit(solution)/shard_map/attn_bwd/pallas_call | solution.py:318
  346.1 44.5 %attn_bwd.3 = bf16[4,3,160,768]{3,2,1,0:T(8,128)(2,1)} custom-call(s32[7]{0:T(128)} %pad_add_fusion.meta, f32[80,1]{1,0:T(8,128)} %copy.72.scale_ref, bf16[960,3072]{1,0:T(8,128)(2,1)} %get-tuple-element.41.q_ref.k_ref.v_ref, bf16[960,3072]{1,0:T(8,128)(2,1)} %get-tuple-element.41.q_ref.k_ref.v_ref, bf16[960,3072]{1,0:T(8,128)(2,1)} %get-tuple-element.41.q_ref.k_ref.v_ref, ...), custom_call_target="tpu_custom_call" | custom-call | flops 35999997952 | bytes 16777216 | tf_op jit(solution)/shard_map/attn_bwd/pallas_call | solution.py:318
  396.9 3.9 all-to-all-start.5
  400.8 11.3 %adapter_grads.1 = (bf16[10,256,128]{2,1,0:T(8,128)(2,1)}, bf16[2,2,160,128]{3,2,1,0:T(8,128)(2,1)}) custom-call(s32[7]{0:T(128)} %pad_add_fusion.meta, bf16[4,480,768]{2,1,0:T(8,128)(2,1)} %bitcast.151, bf16[4,480,768]{2,1,0:T(8,128)(2,1)} %bitcast.149, bf16[3072,1280]{1,0:T(8,128)(2,1)} %get-tuple-element.50.normed_ref, ...), custom_call_target="tpu_custom_call" | custom-call | flops 4026531840 | bytes 20971520 | tf_op jit(solution)/shard_map/adapter_grads/pallas_call | solution.py:141
  414.6 4.0 fusion.35
  418.8 9.5 %fusion.2 = f32[768,1280]{1,0:T(8,128)} fusion(bf16[1920,768]{1,0:T(8,128)(2,1)} %bitcast.162, bf16[1280,3840]{1,0:T(8,128)(2,1)} %all-gather.14.cloned.1.call-done), kind=kOutput, calls=%fused_computation.6 | convolution fusion | flops 3774873600 | bytes 11796480 | tf_op jit(solution)/shard_map/dot_general | solution.py:550
  432.1 4.3 collective-permute-done.11
  443.5 9.6 %fusion = f32[768,1280]{1,0:T(8,128)} fusion(bf16[1920,768]{1,0:T(8,128)(2,1)} %bitcast.146, bf16[1280,3840]{1,0:T(8,128)(2,1)} %all-gather.14.cloned.1.call-done), kind=kOutput, calls=%fused_computation.4 | convolution fusion | flops 3774873600 | bytes 11796480 | tf_op jit(solution)/shard_map/dot_general | solution.py:550
  459.8 9.5 %fusion.9 = (f32[768]{0:T(1024)S(1)}, f32[768]{0:T(1024)S(1)}, f32[768,1280]{1,0:T(8,128)}) fusion(bf16[1,768,1280]{2,1,0:T(8,128)(2,1)S(1)} %copy-done.4, bf16[1280,128]{1,0:T(8,128)(2,1)S(1)} %copy-done.16, bf16[1280,128]{1,0:T(8,128)(2,1)S(1)} %copy-done.14, f32[768,256]{1,0:T(8,128)} %fusion.35, bf16[1920,768]{1,0:T(8,128)(2,1)} %bitcast.147, ...), kind=kOutput, calls=%fused_computation.19 | convolution fusion | flops 1268251136 | bytes 19246080 | tf_op jit(solution)/shard_map/dot_general | solution.py:30
  472.5 4.9 fusion.13
  (296 shorter events, 143.5 us)
Async XLA Ops:
  7.2 61.9 %all-gather.6.cloned.1.call-start = ((), (), s32[]{:S(2)}) async-start(), calls=%async_computation.6 | async-start | bytes 2949120 | tf_op jit(solution)/shard_map/all_gather | solution.py:476
  10.4 166.9 %all-gather.8.cloned.1.call-start = ((), (), s32[]{:S(2)}) async-start(), calls=%async_computation.7 | async-start | bytes 3686400 | tf_op jit(solution)/shard_map/all_gather | solution.py:477
  11.2 186.6 %all-gather.10.cloned.1.call-start = ((), (), s32[]{:S(2)}) async-start(), calls=%async_computation.8 | async-start | bytes 3686400 | tf_op jit(solution)/shard_map/all_gather | solution.py:478
  11.9 194.9 %all-gather.12.cloned.1.call-start = ((), (), s32[]{:S(2)}) async-start(), calls=%async_computation.9 | async-start | bytes 3686400 | tf_op jit(solution)/shard_map/all_gather | solution.py:479
  12.5 406.3 %all-gather.14.cloned.1.call-start = ((), (), s32[]{:S(2)}) async-start(), calls=%async_computation.10 | async-start | bytes 11059200 | tf_op jit(solution)/shard_map/all_gather | solution.py:480
  14.0 68.1 %collective-permute-start.5 = (bf16[384,1280]{1,0:T(8,128)(2,1)}, bf16[384,1280]{1,0:T(8,128)(2,1)}, u32[]{:S(2)}, u32[]{:S(2)}) collective-permute-start(bf16[384,1280]{1,0:T(8,128)(2,1)} %get-tuple-element.81), channel_id=1, source_target_pairs={{0,8},{8,0},{16,24},{24,16},{1,9},{9,1},{17,25},{25,17},{2,10},{10... | collective-permute-start | bytes 2949128 | tf_op jit(solution)/shard_map/ppermute | solution.py:368
  15.2 26.8 %collective-permute-start = (bf16[384,1280]{1,0:T(8,128)(2,1)}, bf16[384,1280]{1,0:T(8,128)(2,1)}, u32[]{:S(2)}, u32[]{:S(2)}) collective-permute-start(bf16[384,1280]{1,0:T(8,128)(2,1)} %get-tuple-element.81), channel_id=1, source_target_pairs={{0,16},{8,24},{16,0},{24,8},{1,17},{9,25},{17,1},{25,9},{2,18},{10... | collective-permute-start | bytes 2949128 | tf_op jit(solution)/shard_map/ppermute | solution.py:368
  16.4 41.6 %collective-permute-start.2 = (bf16[384,1280]{1,0:T(8,128)(2,1)}, bf16[384,1280]{1,0:T(8,128)(2,1)}, u32[]{:S(2)}, u32[]{:S(2)}) collective-permute-start(bf16[384,1280]{1,0:T(8,128)(2,1)} %get-tuple-element.80), channel_id=1, source_target_pairs={{0,8},{8,0},{16,24},{24,16},{1,9},{9,1},{17,25},{25,17},{2,10},{10... | collective-permute-start | bytes 2949128 | tf_op jit(solution)/shard_map/ppermute | solution.py:368
  16.7 74.1 %collective-permute-start.4 = (bf16[384,1280]{1,0:T(8,128)(2,1)}, bf16[384,1280]{1,0:T(8,128)(2,1)}, u32[]{:S(2)}, u32[]{:S(2)}) collective-permute-start(bf16[384,1280]{1,0:T(8,128)(2,1)} %get-tuple-element.80), channel_id=1, source_target_pairs={{0,16},{8,24},{16,0},{24,8},{1,17},{9,25},{17,1},{25,9},{2,18},{10... | collective-permute-start | bytes 2949128 | tf_op jit(solution)/shard_map/ppermute | solution.py:368
  41.9 57.7 %collective-permute-start.1 = (bf16[384,1280]{1,0:T(8,128)(2,1)}, bf16[384,1280]{1,0:T(8,128)(2,1)}, u32[]{:S(2)}, u32[]{:S(2)}) collective-permute-start(bf16[384,1280]{1,0:T(8,128)(2,1)} %collective-permute-done.low_ref), channel_id=1, source_target_pairs={{0,8},{8,0},{16,24},{24,16},{1,9},{9,1},{17,25},{25,17},{2,10},{10... | collective-permute-start | bytes 2949128 | tf_op jit(solution)/shard_map/ppermute | solution.py:368
  58.0 41.7 %collective-permute-start.3 = (bf16[384,1280]{1,0:T(8,128)(2,1)}, bf16[384,1280]{1,0:T(8,128)(2,1)}, u32[]{:S(2)}, u32[]{:S(2)}) collective-permute-start(bf16[384,1280]{1,0:T(8,128)(2,1)} %collective-permute-done.2.high_ref), channel_id=1, source_target_pairs={{0,16},{8,24},{16,0},{24,8},{1,17},{9,25},{17,1},{25,9},{2,18},{10... | collective-permute-start | bytes 2949128 | tf_op jit(solution)/shard_map/ppermute | solution.py:368
  138.7 33.8 %all-to-all-start = ((bf16[4,160,768]{2,1,0:T(8,128)(2,1)}), bf16[4,160,768]{2,1,0:T(8,128)(2,1)S(1)}, u32[]{:S(2)}, u32[]{:S(2)}) async-start(bf16[4,160,768]{2,1,0:T(8,128)(2,1)} %get-tuple-element.42.o_ref), calls=%async_computation | async-start | bytes 1966080 | tf_op jit(solution)/shard_map/all_to_all | solution.py:363
  173.4 16.0 %all-to-all-start.1 = ((bf16[4,160,768]{2,1,0:T(8,128)(2,1)}), bf16[4,160,768]{2,1,0:T(8,128)(2,1)S(1)}, u32[]{:S(2)}, u32[]{:S(2)}) async-start(bf16[4,160,768]{2,1,0:T(8,128)(2,1)} %get-tuple-element.43.o_ref), calls=%async_computation.1 | async-start | bytes 1966080 | tf_op jit(solution)/shard_map/all_to_all | solution.py:363
  218.4 18.1 %collective-permute-start.6 = (bf16[256,1280]{1,0:T(8,128)(2,1)}, bf16[256,1280]{1,0:T(8,128)(2,1)}, u32[]{:S(2)}, u32[]{:S(2)}) collective-permute-start(bf16[256,1280]{1,0:T(8,128)(2,1)} %constant_dynamic-slice_fusion.8), channel_id=1, source_target_pairs={{0,1},{1,0},{2,3},{3,2},{4,5},{5,4},{6,7},{7,6},{8,9},{9,8},{10,11... | collective-permute-start | bytes 1966088 | tf_op jit(solution)/shard_map/ppermute | solution.py:368
  227.5 16.9 %all-to-all-start.2 = ((bf16[4,160,768]{2,1,0:T(8,128)(2,1)}), bf16[4,160,768]{2,1,0:T(8,128)(2,1)}, u32[]{:S(2)}, u32[]{:S(2)}) async-start(bf16[4,160,768]{2,1,0:T(8,128)(2,1)} %bitcast.184), calls=%async_computation.2 | async-start | bytes 1966080 | tf_op jit(solution)/shard_map/all_to_all | solution.py:363
  244.4 23.7 %all-to-all-start.4 = ((bf16[4,160,768]{2,1,0:T(8,128)(2,1)}), bf16[4,160,768]{2,1,0:T(8,128)(2,1)}, u32[]{:S(2)}, u32[]{:S(2)}) async-start(bf16[4,160,768]{2,1,0:T(8,128)(2,1)} %bitcast.182), calls=%async_computation.4 | async-start | bytes 1966080 | tf_op jit(solution)/shard_map/all_to_all | solution.py:363
  248.9 15.1 %collective-permute-start.7 = (bf16[64,1280]{1,0:T(8,128)(2,1)S(1)}, bf16[64,1280]{1,0:T(8,128)(2,1)S(1)}, u32[]{:S(2)}, u32[]{:S(2)}) collective-permute-start(bf16[64,1280]{1,0:T(8,128)(2,1)S(1)} %get-tuple-element.98), channel_id=1, source_target_pairs={{0,8},{8,0},{16,24},{24,16},{1,9},{9,1},{17,25},{25,17},{2,10},{10... | collective-permute-start | bytes 491528 | tf_op jit(solution)/shard_map/ppermute | solution.py:368
  250.4 14.4 %collective-permute-start.8 = (bf16[64,1280]{1,0:T(8,128)(2,1)S(1)}, bf16[64,1280]{1,0:T(8,128)(2,1)S(1)}, u32[]{:S(2)}, u32[]{:S(2)}) collective-permute-start(bf16[64,1280]{1,0:T(8,128)(2,1)S(1)} %get-tuple-element.100), channel_id=1, source_target_pairs={{0,16},{8,24},{16,0},{24,8},{1,17},{9,25},{17,1},{25,9},{2,18},{10... | collective-permute-start | bytes 491528 | tf_op jit(solution)/shard_map/ppermute | solution.py:368
  251.6 16.5 %collective-permute-start.9 = (bf16[64,1280]{1,0:T(8,128)(2,1)S(1)}, bf16[64,1280]{1,0:T(8,128)(2,1)S(1)}, u32[]{:S(2)}, u32[]{:S(2)}) collective-permute-start(bf16[64,1280]{1,0:T(8,128)(2,1)S(1)} %get-tuple-element.99), channel_id=1, source_target_pairs={{0,24},{8,16},{16,8},{24,0},{1,25},{9,17},{17,9},{25,1},{2,26},{10... | collective-permute-start | bytes 491528 | tf_op jit(solution)/shard_map/ppermute | solution.py:368
  272.8 14.6 %collective-permute-start.24 = (bf16[64,1280]{1,0:T(8,128)(2,1)S(1)}, bf16[64,1280]{1,0:T(8,128)(2,1)S(1)}, u32[]{:S(2)}, u32[]{:S(2)}) collective-permute-start(bf16[64,1280]{1,0:T(8,128)(2,1)S(1)} %add_convert_fusion.4), channel_id=1, source_target_pairs={{0,6},{1,7},{2,4},{3,5},{4,2},{5,3},{6,0},{7,1},{8,14},{9,15},{10,... | collective-permute-start | bytes 491528 | tf_op jit(solution)/shard_map/ppermute | solution.py:368
  287.5 50.9 %collective-permute-start.25 = (bf16[64,1280]{1,0:T(8,128)(2,1)S(1)}, bf16[64,1280]{1,0:T(8,128)(2,1)S(1)}, u32[]{:S(2)}, u32[]{:S(2)}) collective-permute-start(bf16[64,1280]{1,0:T(8,128)(2,1)S(1)} %add_convert_fusion.2), channel_id=1, source_target_pairs={{0,24},{8,16},{16,8},{24,0},{1,25},{9,17},{17,9},{25,1},{2,26},{10... | collective-permute-start | bytes 491528 | tf_op jit(solution)/shard_map/ppermute | solution.py:368
  288.1 50.3 %collective-permute-start.26 = (bf16[64,1280]{1,0:T(8,128)(2,1)S(1)}, bf16[64,1280]{1,0:T(8,128)(2,1)S(1)}, u32[]{:S(2)}, u32[]{:S(2)}) collective-permute-start(bf16[64,1280]{1,0:T(8,128)(2,1)S(1)} %add_convert_fusion.2), channel_id=1, source_target_pairs={{0,16},{8,24},{16,0},{24,8},{1,17},{9,25},{17,1},{25,9},{2,18},{10... | collective-permute-start | bytes 491528 | tf_op jit(solution)/shard_map/ppermute | solution.py:368
  288.9 49.4 %collective-permute-start.27 = (bf16[64,1280]{1,0:T(8,128)(2,1)S(1)}, bf16[64,1280]{1,0:T(8,128)(2,1)}, u32[]{:S(2)}, u32[]{:S(2)}) collective-permute-start(bf16[64,1280]{1,0:T(8,128)(2,1)S(1)} %add_convert_fusion.2), channel_id=1, source_target_pairs={{0,8},{8,0},{16,24},{24,16},{1,9},{9,1},{17,25},{25,17},{2,10},{10... | collective-permute-start | bytes 491528 | tf_op jit(solution)/shard_map/ppermute | solution.py:368
  334.6 60.6 %all-to-all-start.3 = ((bf16[4,480,768]{2,1,0:T(8,128)(2,1)}), bf16[4,480,768]{2,1,0:T(8,128)(2,1)S(1)}, u32[]{:S(2)}, u32[]{:S(2)}) async-start(bf16[4,480,768]{2,1,0:T(8,128)(2,1)} %bitcast.150), calls=%async_computation.3 | async-start | bytes 5898240 | tf_op jit(solution)/shard_map/all_to_all | solution.py:363
  343.2 47.4 %collective-permute-start.28 = (bf16[256,1280]{1,0:T(8,128)(2,1)}, bf16[256,1280]{1,0:T(8,128)(2,1)}, u32[]{:S(2)}, u32[]{:S(2)}) collective-permute-start(bf16[256,1280]{1,0:T(8,128)(2,1)} %pad_maximum_fusion.6), channel_id=1, source_target_pairs={{0,1},{1,0},{2,3},{3,2},{4,5},{5,4},{6,7},{7,6},{8,9},{9,8},{10,11... | collective-permute-start | bytes 1966088 | tf_op jit(solution)/shard_map/ppermute | solution.py:368
  396.9 45.0 %all-to-all-start.5 = ((bf16[4,480,768]{2,1,0:T(8,128)(2,1)}), bf16[4,480,768]{2,1,0:T(8,128)(2,1)S(1)}, u32[]{:S(2)}, u32[]{:S(2)}) async-start(bf16[4,480,768]{2,1,0:T(8,128)(2,1)} %bitcast.148), calls=%async_computation.5 | async-start | bytes 5898240 | tf_op jit(solution)/shard_map/all_to_all | solution.py:363
  414.4 16.8 %collective-permute-start.14 = (bf16[10,32,128]{2,1,0:T(8,128)(2,1)S(1)}, bf16[10,32,128]{2,1,0:T(8,128)(2,1)}, u32[]{:S(2)}, u32[]{:S(2)}) collective-permute-start(bf16[10,32,128]{2,1,0:T(8,128)(2,1)S(1)} %constant_dynamic-slice_fusion), channel_id=1, source_target_pairs={{0,1},{1,0},{2,3},{3,2},{4,5},{5,4},{6,7},{7,6},{8,9},{9,8},{10,11... | collective-permute-start | bytes 245768 | tf_op jit(solution)/shard_map/ppermute | solution.py:368
  439.2 14.0 %collective-permute-start.15 = (bf16[20,32,128]{2,1,0:T(8,128)(2,1)S(1)}, bf16[20,32,128]{2,1,0:T(8,128)(2,1)S(1)}, u32[]{:S(2)}, u32[]{:S(2)}) collective-permute-start(bf16[20,32,128]{2,1,0:T(8,128)(2,1)S(1)} %pad_maximum_fusion.9), channel_id=1, source_target_pairs={{0,2},{1,3},{2,0},{3,1},{4,6},{5,7},{6,4},{7,5},{8,10},{9,11},{10,... | collective-permute-start | bytes 491528 | tf_op jit(solution)/shard_map/ppermute | solution.py:368
  440.0 13.2 %collective-permute-start.16 = (bf16[20,32,128]{2,1,0:T(8,128)(2,1)S(1)}, bf16[20,32,128]{2,1,0:T(8,128)(2,1)}, u32[]{:S(2)}, u32[]{:S(2)}) collective-permute-start(bf16[20,32,128]{2,1,0:T(8,128)(2,1)S(1)} %pad_maximum_fusion.9), channel_id=1, source_target_pairs={{0,4},{1,5},{2,6},{3,7},{4,0},{5,1},{6,2},{7,3},{8,12},{9,13},{10,... | collective-permute-start | bytes 491528 | tf_op jit(solution)/shard_map/ppermute | solution.py:368
  441.3 14.7 %collective-permute-start.17 = (bf16[20,32,128]{2,1,0:T(8,128)(2,1)S(1)}, bf16[20,32,128]{2,1,0:T(8,128)(2,1)}, u32[]{:S(2)}, u32[]{:S(2)}) collective-permute-start(bf16[20,32,128]{2,1,0:T(8,128)(2,1)S(1)} %pad_maximum_fusion.9), channel_id=1, source_target_pairs={{0,6},{1,7},{2,4},{3,5},{4,2},{5,3},{6,0},{7,1},{8,14},{9,15},{10,... | collective-permute-start | bytes 491528 | tf_op jit(solution)/shard_map/ppermute | solution.py:368
  457.1 12.2 %collective-permute-start.18 = (bf16[20,32,128]{2,1,0:T(8,128)(2,1)S(1)}, bf16[20,32,128]{2,1,0:T(8,128)(2,1)S(1)}, u32[]{:S(2)}, u32[]{:S(2)}) collective-permute-start(bf16[20,32,128]{2,1,0:T(8,128)(2,1)S(1)} %add_convert_fusion.3), channel_id=1, source_target_pairs={{0,24},{8,16},{16,8},{24,0},{1,25},{9,17},{17,9},{25,1},{2,26},{10... | collective-permute-start | bytes 491528 | tf_op jit(solution)/shard_map/ppermute | solution.py:368
  457.2 12.1 %collective-permute-start.19 = (bf16[20,32,128]{2,1,0:T(8,128)(2,1)S(1)}, bf16[20,32,128]{2,1,0:T(8,128)(2,1)S(1)}, u32[]{:S(2)}, u32[]{:S(2)}) collective-permute-start(bf16[20,32,128]{2,1,0:T(8,128)(2,1)S(1)} %add_convert_fusion.3), channel_id=1, source_target_pairs={{0,16},{8,24},{16,0},{24,8},{1,17},{9,25},{17,1},{25,9},{2,18},{10... | collective-permute-start | bytes 491528 | tf_op jit(solution)/shard_map/ppermute | solution.py:368
  (62 other events, 554.5 us)
Sparse Core Ops, SparseCore 0:
  10.5 34.7 all-gather.5
  47.0 37.9 all-gather.7
  86.6 38.1 all-gather.9
  126.3 38.1 all-gather.11
  166.1 90.9 all-gather.13

commit v4 on v3

--- a/solution.py
+++ b/solution.py
@@ -162,7 +162,8 @@
     )(meta, *grads, normed, inner, up)
 
 
-HPB = PH
+HPB = LH
+BLOCKS = ROWS // B
 NEG = -1e30
 FW = 512
 
@@ -180,8 +181,14 @@
             kt = k_ref[own, t * 128:(t + 1) * 128]
             kp[h, t * 128:(t + 1) * 128, :] = jnp.concatenate([kt, zpad], axis=0).T
 
-    def qblock(i, _):
+    subs = o_ref.shape[2] // B
+    base = 0 if subs > 1 else BLOCKS - 1
+
+    def qblock(n, _):
+        chunk, sub = n // subs, n % subs
+        i = chunk * BLOCKS + base + sub
         q0 = pl.multiple_of(i * B, B)
+        here = pl.ds(pl.multiple_of(sub * B, B), B)
         qpos = q0 + lax.broadcasted_iota(jnp.int32, (1, B), 1)
         srow = start_row(qpos, b1, b2)
 
@@ -209,25 +216,29 @@
         for h in range(HPB):
             m, acc = carry[h]
             l = acc[HD:HD + 1, :]
-            o_ref[i // 3, h * HD:(h + 1) * HD, pl.ds(pl.multiple_of((i % 3) * B, B), B)] = (acc[0:HD, :] / l).astype(bf16)
-            lse_ref[h, :, pl.ds(q0, B)] = m + jnp.log(l)
+            o_ref[chunk, h * HD:(h + 1) * HD, here] = (acc[0:HD, :] / l).astype(bf16)
+            lse_ref[h, chunk, :, here] = m + jnp.log(l)
         return 0
-    lax.fori_loop(0, TOK // B, qblock, 0)
-
-def attn_fwd(bounds, qkvt, pair):
-    rows = lambda a: pl.BlockSpec((PW, TOK), lambda i, b: (2 * a + pair, 0))
+    lax.fori_loop(0, PARTS * subs, qblock, 0)
+
+def attn_fwd(bounds, qkvt, subs):
+    rows = lambda a: pl.BlockSpec((WIDTH, TOK), lambda i, b: (a, 0))
+    width = subs * B
     return pl.pallas_call(
         fwd_kernel,
-        out_shape=(jax.ShapeDtypeStruct((PARTS, PW, ROWS), bf16), jax.ShapeDtypeStruct((PH, 1, TOK), f32)),
+        out_shape=(jax.ShapeDtypeStruct((PARTS, WIDTH, width), bf16), jax.ShapeDtypeStruct((LH, PARTS, 1, width), f32)),
         grid_spec=pltpu.PrefetchScalarGridSpec(
             num_scalar_prefetch=1,
             grid=(1,),
             in_specs=[rows(0), rows(1), rows(2)],
-            out_specs=[pl.BlockSpec((PARTS, PW, ROWS), lambda i, b: (0, 0, 0)), pl.BlockSpec((PH, 1, TOK), lambda i, b: (0, 0, 0))],
+            out_specs=[
+                pl.BlockSpec((PARTS, WIDTH, width), lambda i, b: (0, 0, 0)),
+                pl.BlockSpec((LH, PARTS, 1, width), lambda i, b: (0, 0, 0, 0)),
+            ],
             scratch_shapes=[pltpu.VMEM((HPB, TOK, 128), bf16), pltpu.VMEM((HPB, 128, TOK), bf16), pltpu.VMEM((HPB, 96, TOK), bf16)],
         ),
         compiler_params=pltpu.CompilerParams(dimension_semantics=("arbitrary",), vmem_limit_bytes=60 << 20),
-        cost_estimate=pl.CostEstimate(flops=20 * 10**9, bytes_accessed=5 << 20, transcendentals=0),
+        cost_estimate=pl.CostEstimate(flops=subs * 13 * 10**9, bytes_accessed=5 << 20, transcendentals=0),
         name="attn_fwd",
     )(bounds, qkvt, qkvt, qkvt)
 
@@ -260,7 +271,7 @@
             q, k, v = q_ref[:, sl], k_ref[:, sl], v_ref[:, sl]
             do, o = do_ref[chunk, :, here], o_ref[chunk, :, here]
             delta = jnp.sum(do.astype(f32) * o.astype(f32), axis=0, keepdims=True)
-            qa = jnp.concatenate([q, tail(lse_ref[0, :, sl]), pad], axis=0)
+            qa = jnp.concatenate([q, tail(lse_ref[0, chunk, :, here]), pad], axis=0)
             da = jnp.concatenate([do, tail(delta), pad], axis=0)
             qt[:, sl] = qa
             dot[:, sl] = da
@@ -314,7 +325,6 @@
 
 def attn_bwd(meta, scale, qkvt, grad, mixture, logsum, pair):
     rows = lambda a: pl.BlockSpec((HD, TOK), lambda i, b: (LH * a + PH * pair + i, 0))
-    chunks = pl.BlockSpec((PARTS, HD, ROWS), lambda i, b: (0, i, 0))
     return pl.pallas_call(
         bwd_kernel,
         out_shape=jax.ShapeDtypeStruct((PARTS, 3, PW, ROWS), bf16),
@@ -326,9 +336,9 @@
                 rows(0),
                 rows(1),
                 rows(2),
-                chunks,
-                chunks,
-                pl.BlockSpec((1, 1, TOK), lambda i, b: (i, 0, 0)),
+                pl.BlockSpec((PARTS, HD, ROWS), lambda i, b: (0, i, 0)),
+                pl.BlockSpec((PARTS, HD, ROWS), lambda i, b: (0, PH * pair + i, 0)),
+                pl.BlockSpec((1, PARTS, 1, ROWS), lambda i, b: (PH * pair + i, 0, 0, 0)),
             ],
             out_specs=pl.BlockSpec((PARTS, 3, HD, ROWS), lambda i, b: (0, 0, i, 0)),
             scratch_shapes=[pltpu.VMEM((TOK, 128), bf16)] * 2
@@ -448,13 +458,9 @@
 ):
     part = lax.axis_index("heads")
     rows = inputs[0]
-    near_high = swap(rows[HALF:], "heads", 1)
-    far_low = swap(rows[:HALF], "heads", 2)
-    near_low = swap(rows[:HALF], "heads", 1)
-    far_high = swap(rows[HALF:], "heads", 2)
-    both_low = swap(far_low, "heads", 1)
-    both_high = swap(near_high, "heads", 2)
-
+    low, high = rows[:HALF], rows[HALF:]
+    near_high = swap(high, "heads", 1)
+    far_low = swap(low, "heads", 2)
     offset = part * ROWS
     ends = PROMPT + jnp.cumsum(lengths[0])
     bounds = ends[:2].astype(jnp.int32)
@@ -486,6 +492,11 @@
     up_pairs = by_pair(up_query, jnp.zeros_like(up_query), up_value)
     up_mine = jnp.concatenate([mine(up_query), jnp.zeros((2 * AR, WIDTH), bf16), mine(up_value)], axis=1)
     up_heads = jnp.transpose(up_mine.reshape(2 * AR, 3, 2, PW), (2, 0, 1, 3)).reshape(2, 2 * AR, 3 * PW)
+    low_late, high_late, up_heads, up_mine = lax.optimization_barrier((low, high, up_heads, up_mine))
+    near_low = swap(low_late, "heads", 1)
+    far_high = swap(high_late, "heads", 2)
+    both_low = swap(far_low, "heads", 1)
+    both_high = swap(near_high, "heads", 2)
     scale_row = query_scale * HD ** (-0.5)
     scale_mine = jnp.concatenate([jnp.tile(scale_row, LH), jnp.ones((2 * WIDTH,), f32)])[:, None]
 
@@ -496,16 +507,20 @@
     qkvt, normed_all, inner_all = done
     out_pairs = w_out.reshape(PARTS, 2, PW, D)
     pair_weight = [out_pairs[:, p].reshape(PARTS * PW, D) for p in range(2)]
-    forward = [attn_fwd(bounds, qkvt, 0)]
-    mixed_first = exchange(forward[0][0])
-    forward.append(attn_fwd(bounds, qkvt, 1))
-    mixed_second = exchange(forward[1][0])
+    head_mix, head_log = attn_fwd(bounds, qkvt, 2)
+    mixed_head = exchange(head_mix)
+    later, head_log = lax.optimization_barrier((bounds, head_log))
+    tail_mix, tail_log = attn_fwd(later, qkvt, 1)
+    tail_sent, mixed_head = lax.optimization_barrier((tail_mix, mixed_head))
+    mixed_tail = exchange(tail_sent)
+    mixture = jnp.concatenate([head_mix, tail_mix], axis=2)
+    logsum = jnp.concatenate([head_log, tail_log], axis=3)
 
     rows_in = inputs[0].astype(f32)
     scaling_attn = lax.rsqrt(jnp.mean(rows_in * rows_in, axis=-1, keepdims=True) + EPSILON)
 
-    middle = rows_in + tn(mixed_first.reshape(PARTS * PW, ROWS), pair_weight[0])
-    middle = middle + tn(mixed_second.reshape(PARTS * PW, ROWS), pair_weight[1])
+    branch = [tn(m.reshape(D, m.shape[2]), w_out) for m in (mixed_head, mixed_tail)]
+    middle = rows_in + jnp.concatenate(branch)
     normed_mlp, scaling_mlp = normalize(middle, gain_mlp)
     normed_mlp_low = normed_mlp.astype(bf16)
     inner_up = (nn(normed_mlp_low, flat_down[2]) * chosen).astype(bf16)
@@ -530,11 +545,13 @@
     mlp_total = scatter_near(jnp.concatenate(terms).astype(bf16))
     mlp_total, grad_heads[0] = lax.optimization_barrier((mlp_total, grad_heads[0]))
     mlp_total = scatter_heads(mlp_total)
-    grad_first_pair = attn_bwd(meta, scale_row[:, None], qkvt, grad_heads[0], forward[0][0], forward[0][1], 0)
+    grad_first_pair = attn_bwd(meta, scale_row[:, None], qkvt, grad_heads[0], mixture, logsum, 0)
+    mlp_total, grad_first_pair = lax.optimization_barrier((mlp_total, grad_first_pair))
     arrived = [exchange(grad_first_pair.reshape(PARTS, 3 * PW, ROWS))]
-    mlp_total, grad_heads[1] = lax.optimization_barrier((mlp_total, grad_heads[1]))
     mlp_total = sum_far(mlp_total)
-    grad_second_pair = attn_bwd(meta, scale_row[:, None], qkvt, grad_heads[1], forward[1][0], forward[1][1], 1)
+    meta, _ = lax.optimization_barrier((meta, grad_first_pair))
+    grad_second_pair = attn_bwd(meta, scale_row[:, None], qkvt, grad_heads[1], mixture, logsum, 1)
+    mlp_total, grad_second_pair = lax.optimization_barrier((mlp_total, grad_second_pair))
     arrived.append(exchange(grad_second_pair.reshape(PARTS, 3 * PW, ROWS)))
 
     grads = [g.reshape(PARTS, 3 * PW, ROWS) for g in (grad_first_pair, grad_second_pair)]
@@ -552,6 +569,7 @@
         )
 
     tiles = D // 128
+    mlp_total, first_attn = lax.optimization_barrier((mlp_total, first_attn))
     mlp_total = gather_heads(mlp_total)
     near_first = scatter_near(first_attn)
     near_second = scatter_near(second_attn.reshape(tiles, -1, 128))

time: 500 us -> 460 us (0.920)
  waiting for transfers between devices: 55.3 us -> 34.6 us
  matrix products: 84.4 us -> 75.3 us
  starting transfers between devices: 56.5 us -> 47.7 us
    ppermute x29, waiting for transfers between devices: 42.9 us -> 30.6 us  [swap(): return lax.ppermute(value, axis, [(i, i ^ mask) for i in range(count)])]
    all_to_all x6, waiting for transfers between devices: 10.4 us -> 2.05 us  [exchange(): lax.all_to_all(value, 'heads', split_axis=0, concat_axis=0, tiled=True)]
    ppermute x29, starting transfers between devices: 32.6 us -> 24.4 us  [swap(): return lax.ppermute(value, axis, [(i, i ^ mask) for i in range(count)])]
    dot_general x6, matrix products: 22.5 us -> 15.5 us  [nn(): lax.dot_general(a, b, (((1,), (0,)), ((), ())), preferred_element_type=f32)]
    pallas_call x2, Pallas kernels: 88.9 us -> 94.8 us  [attn_bwd(): pl.pallas_call(bwd_kernel, out_shape=jax.ShapeDtypeStruct((PARTS, 3, PW,...]
    pallas_call x2, Pallas kernels: 60.5 us -> 54.7 us  [attn_fwd(): pl.pallas_call(fwd_kernel, out_shape=(jax.ShapeDtypeStruct((PARTS, WIDTH,...]
    unnamed x114 -> x122, local copies, waits for them, and re-layouts: 12.6 us -> 12.4 us
  transfers between devices with their start and end apart: 40 -> 40, of which waited for: 10 -> 6; matrix products, arithmetic and copies ran while one was open for 29% -> 31% of each run, Pallas kernels for 40% -> 43%
where the time goes in v4:
time: 460 us; the launch traced here: 456 us
  Pallas kernels  195 us (42%)
  matrix products  75.3 us (16%)
  local copies, waits for them, and re-layouts  57.8 us (13%)
  starting transfers between devices  47.7 us (10%)
  waiting for transfers between devices  34.6 us (8%)
  other arithmetic  29.5 us (6%)
  between operations  15.3 us (3%)
    pallas_call x2, Pallas kernels, attn_bwd(): pl.pallas_call(bwd_kernel, out_shape=jax.ShapeDtypeStruct((PARTS, 3, PW,...  94.8 us
    pallas_call x2, Pallas kernels, attn_fwd(): pl.pallas_call(fwd_kernel, out_shape=(jax.ShapeDtypeStruct((PARTS, WIDTH,...  54.7 us
    pallas_call x4, Pallas kernels, qkv_project(): pl.pallas_call(qkv_kernel, out_shape=(jax.ShapeDtypeStruct((3 * WIDTH, TO...  34.7 us
    ppermute x29, waiting for transfers between devices, swap(): return lax.ppermute(value, axis, [(i, i ^ mask) for i in range(count)])  30.6 us
    dot_general x9, matrix products, nt(): lax.dot_general(a, b, (((1,), (1,)), ((), ())), preferred_element_type=f32)  28.5 us
    ppermute x29, starting transfers between devices, swap(): return lax.ppermute(value, axis, [(i, i ^ mask) for i in range(count)])  24.4 us
    all_to_all x6, starting transfers between devices, exchange(): lax.all_to_all(value, 'heads', split_axis=0, concat_axis=0, tiled=True)  23.1 us
    dot_general x2, matrix products, back(): lax.dot_general(both, weights_all[:, cut], contract, preferred_element_ty...  19.2 us
  transfers between devices with their start and end apart: 40, of which 6 were waited for; matrix products, arithmetic and copies ran while one was open for 31% of the time, Pallas kernels for 43%

profile of v4, /device:TPU:9, one launch (start us, length us, event | category | flops | bytes accessed | tf_op | source)
XLA Modules:
  0.0 455.6 jit_solution(6385245563971849650)
XLA Ops:
  39.0 3.8 select_select_fusion
  56.8 4.3 copy.63
  61.1 8.7 %qkv_project.4 = (bf16[960,3072]{1,0:T(8,128)(2,1)}, bf16[3072,1280]{1,0:T(8,128)(2,1)}, bf16[3072,256]{1,0:T(8,128)(2,1)}) custom-call(s32[7]{0:T(128)} %pad_add_fusion.meta, s32[1]{0:T(128)} %bitcast.21.first, bf16[768,1280]{1,0:T(8,128)(2,1)} %bitcast.150, bf16[768,1280]{1,0:T(8,128)(2,1)} %bitcast.151, f32[1,1280]{1,0:T(1,128)} %broadcast_in_dim.65.gain_ref, ...), custom_call_target="tpu_custom_call" | custom-call | flops 2390753280 | bytes 8388608 | tf_op jit(solution)/shard_map/qkv_project/pallas_call | solution.py:80
  69.8 8.7 %qkv_project.5 = (bf16[960,3072]{1,0:T(8,128)(2,1)}, bf16[3072,1280]{1,0:T(8,128)(2,1)}, bf16[3072,256]{1,0:T(8,128)(2,1)}) custom-call(s32[7]{0:T(128)} %pad_add_fusion.meta, s32[1]{0:T(128)} %bitcast.20.first, bf16[384,1280]{1,0:T(8,128)(2,1)} %collective-permute-done.5.low_ref, ...), custom_call_target="tpu_custom_call", output_to_operand_aliasing={{0}: (9, {}), {1}: (10, {}), {2}: (11, {})} | custom-call | flops 2390753280 | bytes 8388608 | tf_op jit(solution)/shard_map/qkv_project/pallas_call | solution.py:80
  78.5 8.7 %qkv_project.6 = (bf16[960,3072]{1,0:T(8,128)(2,1)}, bf16[3072,1280]{1,0:T(8,128)(2,1)}, bf16[3072,256]{1,0:T(8,128)(2,1)}) custom-call(s32[7]{0:T(128)} %pad_add_fusion.meta, s32[1]{0:T(128)} %bitcast.19.first, bf16[384,1280]{1,0:T(8,128)(2,1)} %collective-permute-done.low_ref, ...), custom_call_target="tpu_custom_call", output_to_operand_aliasing={{0}: (9, {}), {1}: (10, {}), {2}: (11, {})} | custom-call | flops 2390753280 | bytes 8388608 | tf_op jit(solution)/shard_map/qkv_project/pallas_call | solution.py:80
  87.2 8.6 %qkv_project.7 = (bf16[960,3072]{1,0:T(8,128)(2,1)}, bf16[3072,1280]{1,0:T(8,128)(2,1)}, bf16[3072,256]{1,0:T(8,128)(2,1)}) custom-call(s32[7]{0:T(128)} %pad_add_fusion.meta, s32[1]{0:T(128)} %bitcast.5.first, bf16[384,1280]{1,0:T(8,128)(2,1)} %collective-permute-done.1.low_ref, ...), custom_call_target="tpu_custom_call", output_to_operand_aliasing={{0}: (9, {}), {1}: (10, {}), {2}: (11, {})} | custom-call | flops 2390753280 | bytes 8388608 | tf_op jit(solution)/shard_map/qkv_project/pallas_call | solution.py:80
  95.8 32.7 %attn_fwd.2 = (bf16[4,320,512]{2,1,0:T(8,128)(2,1)}, f32[4,4,1,512]{3,2,1,0:T(1,128)}) custom-call(s32[2]{0:T(128)} %copy-done.52, bf16[960,3072]{1,0:T(8,128)(2,1)} %get-tuple-element.57.q_ref.k_ref.v_ref, bf16[960,3072]{1,0:T(8,128)(2,1)} %get-tuple-element.57.q_ref.k_ref.v_ref, bf16[960,3072]{1,0:T(8,128)(2,1)} %get-tuple-element.57.q_ref.k_ref.v_ref), custom_call_target="tpu_custom_call" | custom-call | flops 25999998976 | bytes 5242880 | tf_op jit(solution)/shard_map/attn_fwd/pallas_call | solution.py:227
  128.6 4.3 all-to-all-start
  132.9 22.0 %attn_fwd.3 = (bf16[4,320,256]{2,1,0:T(8,128)(2,1)}, f32[4,4,1,256]{3,2,1,0:T(1,128)}) custom-call(s32[2]{0:T(128)} %copy-done.52, bf16[960,3072]{1,0:T(8,128)(2,1)} %get-tuple-element.57.q_ref.k_ref.v_ref, bf16[960,3072]{1,0:T(8,128)(2,1)} %get-tuple-element.57.q_ref.k_ref.v_ref, bf16[960,3072]{1,0:T(8,128)(2,1)} %get-tuple-element.57.q_ref.k_ref.v_ref), custom_call_target="tpu_custom_call" | custom-call | flops 12999999488 | bytes 5242880 | tf_op jit(solution)/shard_map/attn_fwd/pallas_call | solution.py:227
  157.7 3.6 all-to-all-start.1
  161.3 3.8 fusion.64
  165.1 6.7 %fusion.25 = f32[768,1280]{1,0:T(8,128)} fusion(bf16[1280,1280]{1,0:T(8,128)(2,1)} %all-gather.12.cloned.1.call-done, bf16[1,768,1280]{2,1,0:T(8,128)(2,1)S(1)} %copy-done.10), kind=kOutput, calls=%fused_computation.47 | convolution fusion | flops 2516582400 | bytes 9175040 | tf_op jit(solution)/shard_map/dot_general | solution.py:30
  171.9 4.9 %fusion.73 = f32[512,1280]{1,0:T(8,128)} fusion(bf16[1280,512]{1,0:T(8,128)(2,1)} %bitcast.22, bf16[1280,1280]{1,0:T(8,128)(2,1)S(1)} %copy-done.14), kind=kOutput, calls=%fused_computation.179 | convolution fusion | flops 1677721600 | bytes 7208960 | tf_op jit(solution)/shard_map/dot_general | solution.py:34
  176.8 3.1 fusion.74
  183.5 5.9 %fusion.63 = f32[768,1280]{1,0:T(8,128)S(1)} fusion(bf16[1280,1280]{1,0:T(8,128)(2,1)} %all-gather.10.cloned.1.call-done, f32[768,1280]{1,0:T(8,128)} %get-tuple-element.105, f32[1280]{0:T(1024)S(1)} %convert_element_type.163, f32[768]{0:T(1024)S(1)} %get-tuple-element.135), kind=kOutput, calls=%fused_computation.171 | convolution fusion | flops 2519531520 | bytes 11149312 | tf_op jit(solution)/shard_map/dot_general | solution.py:38
  200.2 2.7 fusion.76
  207.6 4.4 all-to-all-start.2
  212.0 4.8 %fusion.75 = f32[768,1280]{1,0:T(8,128)S(1)} fusion(bf16[768,1280]{1,0:T(8,128)(2,1)S(1)} %copy-done.28, bf16[1280,1280]{1,0:T(8,128)(2,1)} %all-gather.12.cloned.1.call-done), kind=kOutput, calls=%fused_computation.181 | convolution fusion | flops 2516582400 | bytes 9175040 | tf_op jit(solution)/shard_map/dot_general | solution.py:38
  224.6 3.5 all-to-all-start.3
  230.9 47.4 %attn_bwd.2 = bf16[4,3,160,768]{3,2,1,0:T(8,128)(2,1)} custom-call(s32[7]{0:T(128)} %pad_add_fusion.meta, f32[80,1]{1,0:T(8,128)} %copy.73.scale_ref, bf16[960,3072]{1,0:T(8,128)(2,1)} %get-tuple-element.57.q_ref.k_ref.v_ref, bf16[960,3072]{1,0:T(8,128)(2,1)} %get-tuple-element.57.q_ref.k_ref.v_ref, bf16[960,3072]{1,0:T(8,128)(2,1)} %get-tuple-element.57.q_ref.k_ref.v_ref, ...), custom_call_target="tpu_custom_call" | custom-call | flops 35999997952 | bytes 16777216 | tf_op jit(solution)/shard_map/attn_bwd/pallas_call | solution.py:328
  278.5 2.6 collective-permute-start.12
  282.1 3.7 all-to-all-start.4
  285.7 47.4 %attn_bwd.3 = bf16[4,3,160,768]{3,2,1,0:T(8,128)(2,1)} custom-call(s32[7]{0:T(128)} %pad_add_fusion.meta, f32[80,1]{1,0:T(8,128)} %copy.73.scale_ref, bf16[960,3072]{1,0:T(8,128)(2,1)} %get-tuple-element.57.q_ref.k_ref.v_ref, bf16[960,3072]{1,0:T(8,128)(2,1)} %get-tuple-element.57.q_ref.k_ref.v_ref, bf16[960,3072]{1,0:T(8,128)(2,1)} %get-tuple-element.57.q_ref.k_ref.v_ref, ...), custom_call_target="tpu_custom_call" | custom-call | flops 35999997952 | bytes 16777216 | tf_op jit(solution)/shard_map/attn_bwd/pallas_call | solution.py:328
  336.6 3.7 all-to-all-start.5
  340.3 11.2 %adapter_grads.1 = (bf16[10,256,128]{2,1,0:T(8,128)(2,1)}, bf16[2,2,160,128]{3,2,1,0:T(8,128)(2,1)}) custom-call(s32[7]{0:T(128)} %pad_add_fusion.meta, bf16[4,480,768]{2,1,0:T(8,128)(2,1)} %bitcast.162, bf16[4,480,768]{2,1,0:T(8,128)(2,1)} %bitcast.160, bf16[3072,1280]{1,0:T(8,128)(2,1)} %get-tuple-element.74.normed_ref, ...), custom_call_target="tpu_custom_call" | custom-call | flops 4026531840 | bytes 20971520 | tf_op jit(solution)/shard_map/adapter_grads/pallas_call | solution.py:141
  356.7 22.2 %collective-permute-done.25 = bf16[64,1280]{1,0:T(8,128)(2,1)S(1)} collective-permute-done((bf16[64,1280]{1,0:T(8,128)(2,1)S(1)}, bf16[64,1280]{1,0:T(8,128)(2,1)S(1)}, u32[]{:S(2)}, u32[]{:S(2)}) %collective-permute-start.25) | collective-permute-done | bytes 163872 | tf_op jit(solution)/shard_map/ppermute | solution.py:378
  386.0 9.6 %fusion.2 = f32[768,1280]{1,0:T(8,128)} fusion(bf16[1920,768]{1,0:T(8,128)(2,1)} %bitcast.169, bf16[1280,3840]{1,0:T(8,128)(2,1)} %all-gather.14.cloned.1.call-done), kind=kOutput, calls=%fused_computation.6 | convolution fusion | flops 3774873600 | bytes 11796480 | tf_op jit(solution)/shard_map/dot_general | solution.py:567
  400.0 2.9 collective-permute-done.15
  407.3 9.6 %fusion = f32[768,1280]{1,0:T(8,128)} fusion(bf16[1920,768]{1,0:T(8,128)(2,1)} %bitcast.157, bf16[1280,3840]{1,0:T(8,128)(2,1)} %all-gather.14.cloned.1.call-done), kind=kOutput, calls=%fused_computation.4 | convolution fusion | flops 3774873600 | bytes 11796480 | tf_op jit(solution)/shard_map/dot_general | solution.py:567
  417.0 3.8 collective-permute-done.20
  424.5 9.5 %fusion.9 = (f32[768]{0:T(1024)S(1)}, f32[768]{0:T(1024)S(1)}, f32[768,1280]{1,0:T(8,128)}) fusion(bf16[1,768,1280]{2,1,0:T(8,128)(2,1)S(1)} %copy-done.4, bf16[1280,128]{1,0:T(8,128)(2,1)S(1)} %copy-done.20, bf16[1280,128]{1,0:T(8,128)(2,1)S(1)} %copy-done.18, f32[768,256]{1,0:T(8,128)} %fusion.46, bf16[1920,768]{1,0:T(8,128)(2,1)} %bitcast.158, ...), kind=kOutput, calls=%fused_computation.18 | convolution fusion | flops 1268251136 | bytes 19246080 | tf_op jit(solution)/shard_map/dot_general | solution.py:30
  436.3 4.9 %fusion.13 = f32[1,768,1280]{2,1,0:T(8,128)} fusion(f32[768,1280]{1,0:T(8,128)S(1)} %copy-done.7, f32[768,1280]{1,0:T(8,128)} %get-tuple-element.148, f32[768]{0:T(1024)S(1)} %broadcast_multiply_fusion, f32[768]{0:T(1024)S(1)} %get-tuple-element.133, f32[768]{0:T(1024)S(1)} %get-tuple-element.132, bf16[1,768,1280]{2,1,0:T(8,128)(2,1)S(1)} %copy-done.4), kind=kLoop, calls=%fused_computation.22 | loop fusion | flops 5898240 | bytes 13771776 | tf_op jit(solution)/shard_map/broadcast_in_dim | solution.py:595
  (306 shorter events, 116.6 us)
Async XLA Ops:
  7.2 49.6 %all-gather.6.cloned.1.call-start = ((), (), s32[]{:S(2)}) async-start(), calls=%async_computation.6 | async-start | bytes 2949120 | tf_op jit(solution)/shard_map/all_gather | solution.py:482
  10.4 150.9 %all-gather.8.cloned.1.call-start = ((), (), s32[]{:S(2)}) async-start(), calls=%async_computation.7 | async-start | bytes 3686400 | tf_op jit(solution)/shard_map/all_gather | solution.py:483
  11.2 154.0 %all-gather.12.cloned.1.call-start = ((), (), s32[]{:S(2)}) async-start(), calls=%async_computation.9 | async-start | bytes 3686400 | tf_op jit(solution)/shard_map/all_gather | solution.py:485
  11.9 171.6 %all-gather.10.cloned.1.call-start = ((), (), s32[]{:S(2)}) async-start(), calls=%async_computation.8 | async-start | bytes 3686400 | tf_op jit(solution)/shard_map/all_gather | solution.py:484
  12.5 373.5 %all-gather.14.cloned.1.call-start = ((), (), s32[]{:S(2)}) async-start(), calls=%async_computation.10 | async-start | bytes 11059200 | tf_op jit(solution)/shard_map/all_gather | solution.py:486
  14.0 33.6 %collective-permute-start.2 = (bf16[384,1280]{1,0:T(8,128)(2,1)}, bf16[384,1280]{1,0:T(8,128)(2,1)}, u32[]{:S(2)}, u32[]{:S(2)}) collective-permute-start(bf16[384,1280]{1,0:T(8,128)(2,1)} %get-tuple-element.46), channel_id=1, source_target_pairs={{0,8},{8,0},{16,24},{24,16},{1,9},{9,1},{17,25},{25,17},{2,10},{10... | collective-permute-start | bytes 2949128 | tf_op jit(solution)/shard_map/ppermute | solution.py:378
  15.2 31.1 %collective-permute-start = (bf16[384,1280]{1,0:T(8,128)(2,1)}, bf16[384,1280]{1,0:T(8,128)(2,1)}, u32[]{:S(2)}, u32[]{:S(2)}) collective-permute-start(bf16[384,1280]{1,0:T(8,128)(2,1)} %get-tuple-element.47), channel_id=1, source_target_pairs={{0,16},{8,24},{16,0},{24,8},{1,17},{9,25},{17,1},{25,9},{2,18},{10... | collective-permute-start | bytes 2949128 | tf_op jit(solution)/shard_map/ppermute | solution.py:378
  18.9 50.9 %collective-permute-start.5 = (bf16[384,1280]{1,0:T(8,128)(2,1)}, bf16[384,1280]{1,0:T(8,128)(2,1)}, u32[]{:S(2)}, u32[]{:S(2)}) collective-permute-start(bf16[384,1280]{1,0:T(8,128)(2,1)} %get-tuple-element.47), channel_id=1, source_target_pairs={{0,8},{8,0},{16,24},{24,16},{1,9},{9,1},{17,25},{25,17},{2,10},{10... | collective-permute-start | bytes 2949128 | tf_op jit(solution)/shard_map/ppermute | solution.py:378
  19.2 59.3 %collective-permute-start.4 = (bf16[384,1280]{1,0:T(8,128)(2,1)}, bf16[384,1280]{1,0:T(8,128)(2,1)}, u32[]{:S(2)}, u32[]{:S(2)}) collective-permute-start(bf16[384,1280]{1,0:T(8,128)(2,1)} %get-tuple-element.46), channel_id=1, source_target_pairs={{0,16},{8,24},{16,0},{24,8},{1,17},{9,25},{17,1},{25,9},{2,18},{10... | collective-permute-start | bytes 2949128 | tf_op jit(solution)/shard_map/ppermute | solution.py:378
  46.3 40.9 %collective-permute-start.1 = (bf16[384,1280]{1,0:T(8,128)(2,1)}, bf16[384,1280]{1,0:T(8,128)(2,1)}, u32[]{:S(2)}, u32[]{:S(2)}) collective-permute-start(bf16[384,1280]{1,0:T(8,128)(2,1)} %collective-permute-done.low_ref), channel_id=1, source_target_pairs={{0,8},{8,0},{16,24},{24,16},{1,9},{9,1},{17,25},{25,17},{2,10},{10... | collective-permute-start | bytes 2949128 | tf_op jit(solution)/shard_map/ppermute | solution.py:378
  47.6 39.6 %collective-permute-start.3 = (bf16[384,1280]{1,0:T(8,128)(2,1)}, bf16[384,1280]{1,0:T(8,128)(2,1)}, u32[]{:S(2)}, u32[]{:S(2)}) collective-permute-start(bf16[384,1280]{1,0:T(8,128)(2,1)} %collective-permute-done.2.high_ref), channel_id=1, source_target_pairs={{0,16},{8,24},{16,0},{24,8},{1,17},{9,25},{17,1},{25,9},{2,18},{10... | collective-permute-start | bytes 2949128 | tf_op jit(solution)/shard_map/ppermute | solution.py:378
  128.6 29.2 %all-to-all-start = ((bf16[4,320,512]{2,1,0:T(8,128)(2,1)}), bf16[4,320,512]{2,1,0:T(8,128)(2,1)}, u32[]{:S(2)}, u32[]{:S(2)}) async-start(bf16[4,320,512]{2,1,0:T(8,128)(2,1)} %get-tuple-element.61), calls=%async_computation | async-start | bytes 2621440 | tf_op jit(solution)/shard_map/all_to_all | solution.py:373
  157.7 19.1 %all-to-all-start.1 = ((bf16[4,320,256]{2,1,0:T(8,128)(2,1)}), bf16[4,320,256]{2,1,0:T(8,128)(2,1)S(1)}, u32[]{:S(2)}, u32[]{:S(2)}) async-start(bf16[4,320,256]{2,1,0:T(8,128)(2,1)} %get-tuple-element.63), calls=%async_computation.1 | async-start | bytes 1310720 | tf_op jit(solution)/shard_map/all_to_all | solution.py:373
  199.0 22.3 %collective-permute-start.6 = (bf16[256,1280]{1,0:T(8,128)(2,1)}, bf16[256,1280]{1,0:T(8,128)(2,1)}, u32[]{:S(2)}, u32[]{:S(2)}) collective-permute-start(bf16[256,1280]{1,0:T(8,128)(2,1)} %constant_dynamic-slice_fusion.8), channel_id=1, source_target_pairs={{0,1},{1,0},{2,3},{3,2},{4,5},{5,4},{6,7},{7,6},{8,9},{9,8},{10,11... | collective-permute-start | bytes 1966088 | tf_op jit(solution)/shard_map/ppermute | solution.py:378
  207.6 17.0 %all-to-all-start.2 = ((bf16[4,160,768]{2,1,0:T(8,128)(2,1)}), bf16[4,160,768]{2,1,0:T(8,128)(2,1)}, u32[]{:S(2)}, u32[]{:S(2)}) async-start(bf16[4,160,768]{2,1,0:T(8,128)(2,1)} %bitcast.191), calls=%async_computation.2 | async-start | bytes 1966080 | tf_op jit(solution)/shard_map/all_to_all | solution.py:373
  224.6 56.5 %all-to-all-start.3 = ((bf16[4,160,768]{2,1,0:T(8,128)(2,1)}), bf16[4,160,768]{2,1,0:T(8,128)(2,1)S(1)}, u32[]{:S(2)}, u32[]{:S(2)}) async-start(bf16[4,160,768]{2,1,0:T(8,128)(2,1)} %bitcast.46), calls=%async_computation.3 | async-start | bytes 1966080 | tf_op jit(solution)/shard_map/all_to_all | solution.py:373
  228.1 50.1 %collective-permute-start.7 = (bf16[64,1280]{1,0:T(8,128)(2,1)S(1)}, bf16[64,1280]{1,0:T(8,128)(2,1)S(1)}, u32[]{:S(2)}, u32[]{:S(2)}) collective-permute-start(bf16[64,1280]{1,0:T(8,128)(2,1)S(1)} %get-tuple-element.126), channel_id=1, source_target_pairs={{0,8},{8,0},{16,24},{24,16},{1,9},{9,1},{17,25},{25,17},{2,10},{10... | collective-permute-start | bytes 491528 | tf_op jit(solution)/shard_map/ppermute | solution.py:378
  229.6 48.7 %collective-permute-start.8 = (bf16[64,1280]{1,0:T(8,128)(2,1)S(1)}, bf16[64,1280]{1,0:T(8,128)(2,1)S(1)}, u32[]{:S(2)}, u32[]{:S(2)}) collective-permute-start(bf16[64,1280]{1,0:T(8,128)(2,1)S(1)} %get-tuple-element.128), channel_id=1, source_target_pairs={{0,16},{8,24},{16,0},{24,8},{1,17},{9,25},{17,1},{25,9},{2,18},{10... | collective-permute-start | bytes 491528 | tf_op jit(solution)/shard_map/ppermute | solution.py:378
  230.8 47.5 %collective-permute-start.9 = (bf16[64,1280]{1,0:T(8,128)(2,1)S(1)}, bf16[64,1280]{1,0:T(8,128)(2,1)S(1)}, u32[]{:S(2)}, u32[]{:S(2)}) collective-permute-start(bf16[64,1280]{1,0:T(8,128)(2,1)S(1)} %get-tuple-element.127), channel_id=1, source_target_pairs={{0,24},{8,16},{16,8},{24,0},{1,25},{9,17},{17,9},{25,1},{2,26},{10... | collective-permute-start | bytes 491528 | tf_op jit(solution)/shard_map/ppermute | solution.py:378
  278.4 54.8 %collective-permute-start.10 = (bf16[64,1280]{1,0:T(8,128)(2,1)S(1)}, bf16[64,1280]{1,0:T(8,128)(2,1)S(1)}, u32[]{:S(2)}, u32[]{:S(2)}) collective-permute-start(bf16[64,1280]{1,0:T(8,128)(2,1)S(1)} %add_convert_fusion.4), channel_id=1, source_target_pairs={{0,2},{1,3},{2,0},{3,1},{4,6},{5,7},{6,4},{7,5},{8,10},{9,11},{10,... | collective-permute-start | bytes 491528 | tf_op jit(solution)/shard_map/ppermute | solution.py:378
  278.5 54.7 %collective-permute-start.11 = (bf16[64,1280]{1,0:T(8,128)(2,1)S(1)}, bf16[64,1280]{1,0:T(8,128)(2,1)S(1)}, u32[]{:S(2)}, u32[]{:S(2)}) collective-permute-start(bf16[64,1280]{1,0:T(8,128)(2,1)S(1)} %add_convert_fusion.4), channel_id=1, source_target_pairs={{0,4},{1,5},{2,6},{3,7},{4,0},{5,1},{6,2},{7,3},{8,12},{9,13},{10,... | collective-permute-start | bytes 491528 | tf_op jit(solution)/shard_map/ppermute | solution.py:378
  278.5 55.3 %collective-permute-start.12 = (bf16[64,1280]{1,0:T(8,128)(2,1)S(1)}, bf16[64,1280]{1,0:T(8,128)(2,1)}, u32[]{:S(2)}, u32[]{:S(2)}) collective-permute-start(bf16[64,1280]{1,0:T(8,128)(2,1)S(1)} %add_convert_fusion.4), channel_id=1, source_target_pairs={{0,6},{1,7},{2,4},{3,5},{4,2},{5,3},{6,0},{7,1},{8,14},{9,15},{10,... | collective-permute-start | bytes 491528 | tf_op jit(solution)/shard_map/ppermute | solution.py:378
  282.1 52.9 %all-to-all-start.4 = ((bf16[4,480,768]{2,1,0:T(8,128)(2,1)}), bf16[4,480,768]{2,1,0:T(8,128)(2,1)S(1)}, u32[]{:S(2)}, u32[]{:S(2)}) async-start(bf16[4,480,768]{2,1,0:T(8,128)(2,1)} %bitcast.161), calls=%async_computation.4 | async-start | bytes 5898240 | tf_op jit(solution)/shard_map/all_to_all | solution.py:373
  336.6 69.1 %all-to-all-start.5 = ((bf16[4,480,768]{2,1,0:T(8,128)(2,1)}), bf16[4,480,768]{2,1,0:T(8,128)(2,1)S(1)}, u32[]{:S(2)}, u32[]{:S(2)}) async-start(bf16[4,480,768]{2,1,0:T(8,128)(2,1)} %bitcast.159), calls=%async_computation.5 | async-start | bytes 5898240 | tf_op jit(solution)/shard_map/all_to_all | solution.py:373
  351.5 27.4 %collective-permute-start.25 = (bf16[64,1280]{1,0:T(8,128)(2,1)S(1)}, bf16[64,1280]{1,0:T(8,128)(2,1)S(1)}, u32[]{:S(2)}, u32[]{:S(2)}) collective-permute-start(bf16[64,1280]{1,0:T(8,128)(2,1)S(1)} %add_convert_fusion.3), channel_id=1, source_target_pairs={{0,24},{8,16},{16,8},{24,0},{1,25},{9,17},{17,9},{25,1},{2,26},{10... | collective-permute-start | bytes 491528 | tf_op jit(solution)/shard_map/ppermute | solution.py:378
  353.9 26.1 %collective-permute-start.26 = (bf16[64,1280]{1,0:T(8,128)(2,1)S(1)}, bf16[64,1280]{1,0:T(8,128)(2,1)S(1)}, u32[]{:S(2)}, u32[]{:S(2)}) collective-permute-start(bf16[64,1280]{1,0:T(8,128)(2,1)S(1)} %add_convert_fusion.3), channel_id=1, source_target_pairs={{0,16},{8,24},{16,0},{24,8},{1,17},{9,25},{17,1},{25,9},{2,18},{10... | collective-permute-start | bytes 491528 | tf_op jit(solution)/shard_map/ppermute | solution.py:378
  354.1 25.9 %collective-permute-start.27 = (bf16[64,1280]{1,0:T(8,128)(2,1)S(1)}, bf16[64,1280]{1,0:T(8,128)(2,1)S(1)}, u32[]{:S(2)}, u32[]{:S(2)}) collective-permute-start(bf16[64,1280]{1,0:T(8,128)(2,1)S(1)} %add_convert_fusion.3), channel_id=1, source_target_pairs={{0,8},{8,0},{16,24},{24,16},{1,9},{9,1},{17,25},{25,17},{2,10},{10... | collective-permute-start | bytes 491528 | tf_op jit(solution)/shard_map/ppermute | solution.py:378
  355.2 29.2 %collective-permute-start.13 = (bf16[10,128,128]{2,1,0:T(8,128)(2,1)S(1)}, bf16[10,128,128]{2,1,0:T(8,128)(2,1)S(1)}, u32[]{:S(2)}, u32[]{:S(2)}) collective-permute-start(bf16[10,128,128]{2,1,0:T(8,128)(2,1)S(1)} %constant_dynamic-slice_fusion.4), channel_id=1, source_target_pairs={{0,1},{1,0},{2,3},{3,2},{4,5},{5,4},{6,7},{7,6},{8,9},{9,8},{10,11... | collective-permute-start | bytes 983048 | tf_op jit(solution)/shard_map/ppermute | solution.py:378
  356.2 28.2 %collective-permute-start.17 = (bf16[10,32,128]{2,1,0:T(8,128)(2,1)S(1)}, bf16[10,32,128]{2,1,0:T(8,128)(2,1)S(1)}, u32[]{:S(2)}, u32[]{:S(2)}) collective-permute-start(bf16[10,32,128]{2,1,0:T(8,128)(2,1)S(1)} %constant_dynamic-slice_fusion), channel_id=1, source_target_pairs={{0,1},{1,0},{2,3},{3,2},{4,5},{5,4},{6,7},{7,6},{8,9},{9,8},{10,11... | collective-permute-start | bytes 245768 | tf_op jit(solution)/shard_map/ppermute | solution.py:378
  403.0 14.0 %collective-permute-start.18 = (bf16[20,32,128]{2,1,0:T(8,128)(2,1)S(1)}, bf16[20,32,128]{2,1,0:T(8,128)(2,1)S(1)}, u32[]{:S(2)}, u32[]{:S(2)}) collective-permute-start(bf16[20,32,128]{2,1,0:T(8,128)(2,1)S(1)} %pad_maximum_fusion.9), channel_id=1, source_target_pairs={{0,2},{1,3},{2,0},{3,1},{4,6},{5,7},{6,4},{7,5},{8,10},{9,11},{10,... | collective-permute-start | bytes 491528 | tf_op jit(solution)/shard_map/ppermute | solution.py:378
  403.1 13.9 %collective-permute-start.19 = (bf16[20,32,128]{2,1,0:T(8,128)(2,1)S(1)}, bf16[20,32,128]{2,1,0:T(8,128)(2,1)}, u32[]{:S(2)}, u32[]{:S(2)}) collective-permute-start(bf16[20,32,128]{2,1,0:T(8,128)(2,1)S(1)} %pad_maximum_fusion.9), channel_id=1, source_target_pairs={{0,4},{1,5},{2,6},{3,7},{4,0},{5,1},{6,2},{7,3},{8,12},{9,13},{10,... | collective-permute-start | bytes 491528 | tf_op jit(solution)/shard_map/ppermute | solution.py:378
  403.1 17.6 %collective-permute-start.20 = (bf16[20,32,128]{2,1,0:T(8,128)(2,1)S(1)}, bf16[20,32,128]{2,1,0:T(8,128)(2,1)}, u32[]{:S(2)}, u32[]{:S(2)}) collective-permute-start(bf16[20,32,128]{2,1,0:T(8,128)(2,1)S(1)} %pad_maximum_fusion.9), channel_id=1, source_target_pairs={{0,6},{1,7},{2,4},{3,5},{4,2},{5,3},{6,0},{7,1},{8,14},{9,15},{10,... | collective-permute-start | bytes 491528 | tf_op jit(solution)/shard_map/ppermute | solution.py:378
  (65 other events, 511.1 us)
Sparse Core Ops, SparseCore 0:
  10.5 34.7 all-gather.5
  47.0 37.9 all-gather.7
  86.6 38.1 all-gather.11
  126.4 38.1 all-gather.9
  166.1 90.9 all-gather.13

commit v5 on v4

--- a/solution.py
+++ b/solution.py
@@ -21,6 +21,7 @@
 PH = LH // 2
 PW = PH * HD
 WIDTH = LH * HD
+SR = WIDTH * 128 // D
 EPSILON = 1e-06
 B = 256
 f32, bf16 = jnp.float32, jnp.bfloat16
@@ -69,8 +70,10 @@
     chosen = (lane % AR) // RANK == token_adapter(pos, meta)
     inner = jnp.where(chosen, nn(normed, down_ref[...]), 0.0).astype(bf16)
     inner_ref[...] = inner
-    out = nt(wt_ref[...], normed) + nt(up_ref[...], inner)
-    out_ref[...] = (out * scale_ref[...]).astype(bf16)
+    out = nt(wt_ref[0:WIDTH, :], normed) + nt(up_ref[0], inner[:, :AR])
+    out_ref[0:WIDTH, :] = (out * scale_ref[...]).astype(bf16)
+    out_ref[WIDTH : 2 * WIDTH, :] = nt(wt_ref[WIDTH : 2 * WIDTH, :], normed).astype(bf16)
+    out_ref[2 * WIDTH :, :] = (nt(wt_ref[2 * WIDTH :, :], normed) + nt(up_ref[1], inner[:, AR:])).astype(bf16)
 
 
 def qkv_project(meta, chunk, low, high, gain, wt, down, up, scale, done):
@@ -93,8 +96,8 @@
                 whole((1, D)),
                 whole((3 * WIDTH, D)),
                 whole((D, 2 * AR)),
-                whole((3 * WIDTH, 2 * AR)),
-                whole((3 * WIDTH, 1)),
+                pl.BlockSpec((2, WIDTH, AR), lambda i, *_: (0, 0, 0)),
+                whole((WIDTH, 1)),
             ]
             + [pl.BlockSpec(memory_space=pl.ANY)] * len(done),
             out_specs=[
@@ -111,7 +114,7 @@
     )(meta, first, low, low if high is None else high, gain, wt, down, up, scale, *done)
 
 
-def adapter_kernel(meta, g0_ref, g1_ref, normed_ref, inner_ref, up_ref, first_ref, second_ref, facc, sacc):
+def adapter_kernel(meta, g0_ref, g1_ref, normed_ref, inner_ref, up_ref, keep_ref, send_ref, facc, sacc):
     step = pl.program_id(0)
 
     @pl.when(step == 0)
@@ -119,47 +122,106 @@
         facc[...] = jnp.zeros_like(facc)
         sacc[...] = jnp.zeros_like(sacc)
 
-    grads = [g0_ref[0], g1_ref[0]]
-    spread = nn(up_ref[0], grads[0]) + nn(up_ref[1], grads[1])
+    query = jnp.concatenate([g0_ref[0, 0], g1_ref[0, 0]], axis=0)
+    value = jnp.concatenate([g0_ref[0, 2], g1_ref[0, 2]], axis=0)
     pos = step * ROWS + lax.broadcasted_iota(jnp.int32, (1, ROWS), 1)
-    rank = lax.broadcasted_iota(jnp.int32, (2 * AR, ROWS), 0)
-    chosen = (rank % AR) // RANK == token_adapter(pos, meta)
-    spread = jnp.where(chosen, spread, 0.0).astype(bf16)
-    facc[...] += nn(spread, normed_ref[...])
-    for p in range(2):
-        sacc[p, 0] += nn(grads[p][0:PW], inner_ref[:, :AR])
-        sacc[p, 1] += nn(grads[p][2 * PW :], inner_ref[:, AR:])
+    rank = lax.broadcasted_iota(jnp.int32, (AR, ROWS), 0)
+    chosen = rank // RANK == token_adapter(pos, meta)
+    for a, grad in enumerate((query, value)):
+        spread = jnp.where(chosen, nn(up_ref[a], grad), 0.0).astype(bf16)
+        facc[a] += nn(spread, normed_ref[...])
+        sacc[a] += nn(grad, inner_ref[:, a * AR : (a + 1) * AR])
 
     @pl.when(step == PARTS - 1)
     def _():
-        for c in range(D // 128):
-            first_ref[c] = facc[:, c * 128 : (c + 1) * 128].astype(bf16)
-        second_ref[...] = sacc[...].astype(bf16)
+        for ref, a in ((keep_ref, meta[7]), (send_ref, 1 - meta[7])):
+            ref[0:AR, :] = facc[a].astype(bf16)
+            for c in range(D // 128):
+                ref[AR : AR + SR, c * 128 : (c + 1) * 128] = sacc[a, c * SR : (c + 1) * SR, :].astype(bf16)
 
 
 def adapter_grads(meta, grads, normed, inner, up):
     return pl.pallas_call(
         adapter_kernel,
-        out_shape=(jax.ShapeDtypeStruct((D // 128, 2 * AR, 128), bf16), jax.ShapeDtypeStruct((2, 2, PW, AR), bf16)),
+        out_shape=[jax.ShapeDtypeStruct((AR + SR, D), bf16)] * 2,
         grid_spec=pltpu.PrefetchScalarGridSpec(
             num_scalar_prefetch=1,
             grid=(PARTS,),
-            in_specs=[pl.BlockSpec((1, 3 * PW, ROWS), lambda i, m: (i, 0, 0))] * 2
+            in_specs=[pl.BlockSpec((1, 3, PW, ROWS), lambda i, m: (i, 0, 0, 0))] * 2
             + [
                 pl.BlockSpec((ROWS, D), lambda i, m: (i, 0)),
                 pl.BlockSpec((ROWS, 2 * AR), lambda i, m: (i, 0)),
-                pl.BlockSpec((2, 2 * AR, 3 * PW), lambda i, m: (0, 0, 0)),
+                pl.BlockSpec((2, AR, WIDTH), lambda i, m: (0, 0, 0)),
             ],
-            out_specs=[
-                pl.BlockSpec((D // 128, 2 * AR, 128), lambda i, m: (0, 0, 0)),
-                pl.BlockSpec((2, 2, PW, AR), lambda i, m: (0, 0, 0, 0)),
-            ],
-            scratch_shapes=[pltpu.VMEM((2 * AR, D), f32), pltpu.VMEM((2, 2, PW, AR), f32)],
+            out_specs=[pl.BlockSpec((AR + SR, D), lambda i, m: (0, 0))] * 2,
+            scratch_shapes=[pltpu.VMEM((2, AR, D), f32), pltpu.VMEM((2, WIDTH, AR), f32)],
         ),
         compiler_params=pltpu.CompilerParams(dimension_semantics=("arbitrary",), vmem_limit_bytes=60 << 20),
         cost_estimate=pl.CostEstimate(flops=4 * TOK * D * 2 * AR, bytes_accessed=20 << 20, transcendentals=0),
         name="adapter_grads",
     )(meta, *grads, normed, inner, up)
+
+
+def back_kernel(meta, b0_ref, b1_ref, w_ref, up_ref, down_ref, rows_ref, gain_ref, middle_ref, out_ref, cols, total, spread):
+    step = pl.program_id(0)
+    for s in range(PARTS):
+        for p, ref in enumerate((b0_ref, b1_ref)):
+            r = (2 * s + p) * PW
+            cols[r : r + PW, :] = ref[s, 0]
+
+    part_sum = nn(w_ref[...], cols[...])
+
+    @pl.when(step == 0)
+    def _():
+        total[...] = part_sum
+        spread[0] = nn(up_ref[0], cols[...])
+
+    @pl.when(step > 0)
+    def _():
+        total[...] += part_sum
+
+    @pl.when(step == 2)
+    def _():
+        spread[1] = nn(up_ref[1], cols[...])
+        pos = meta[6] * ROWS + lax.broadcasted_iota(jnp.int32, (1, ROWS), 1)
+        rank = lax.broadcasted_iota(jnp.int32, (AR, ROWS), 0)
+        chosen = rank // RANK == token_adapter(pos, meta)
+        both = jnp.concatenate([jnp.where(chosen, spread[a], 0.0).astype(bf16) for a in range(2)], axis=0)
+        total[...] += nn(down_ref[...], both)
+        gain = gain_ref[...]
+        for t in range(ROWS // 128):
+            own = slice(t * 128, (t + 1) * 128)
+            x = rows_ref[own, :].astype(f32)
+            q = lax.rsqrt(jnp.mean(x * x, axis=1, keepdims=True) + EPSILON)
+            weighted = gain * total[:, own].T
+            inside = jnp.mean(x * weighted, axis=1, keepdims=True)
+            out_ref[own, :] = middle_ref[own, :] + (q * weighted - x * (q * q * q * inside))
+
+
+def back_inputs(meta, arrived, weights, up, down, rows, gain, grad_middle):
+    whole = lambda shape: pl.BlockSpec(shape, lambda i, m: (0,) * len(shape))
+    return pl.pallas_call(
+        back_kernel,
+        out_shape=jax.ShapeDtypeStruct((ROWS, D), f32),
+        grid_spec=pltpu.PrefetchScalarGridSpec(
+            num_scalar_prefetch=1,
+            grid=(3,),
+            in_specs=[pl.BlockSpec((PARTS, 1, PW, ROWS), lambda i, m: (0, i, 0, 0))] * 2
+            + [
+                pl.BlockSpec((D, D), lambda i, m: (0, i)),
+                whole((2, AR, D)),
+                whole((D, 2 * AR)),
+                whole((ROWS, D)),
+                whole((1, D)),
+                whole((ROWS, D)),
+            ],
+            out_specs=whole((ROWS, D)),
+            scratch_shapes=[pltpu.VMEM((D, ROWS), bf16), pltpu.VMEM((D, ROWS), f32), pltpu.VMEM((2, AR, ROWS), f32)],
+        ),
+        compiler_params=pltpu.CompilerParams(dimension_semantics=("arbitrary",), vmem_limit_bytes=60 << 20),
+        cost_estimate=pl.CostEstimate(flops=6 * ROWS * D * D, bytes_accessed=24 << 20, transcendentals=0),
+        name="back_inputs",
+    )(meta, *arrived, weights, up, down, rows, gain, grad_middle)
 
 
 HPB = LH
@@ -363,12 +425,6 @@
     return scaling * weighted - values * scaling**3 * jnp.mean(values * weighted, axis=-1, keepdims=True)
 
 
-def by_pair(query, key, value):
-    rows = query.shape[0]
-    split = jnp.stack([query, key, value], axis=1).reshape(rows, 3, PARTS, 2, PW)
-    return jnp.transpose(split, (0, 3, 2, 1, 4)).reshape(rows, 3 * D)
-
-
 def exchange(value):
     return lax.all_to_all(value, "heads", split_axis=0, concat_axis=0, tiled=True)
 
@@ -465,11 +521,11 @@
     ends = PROMPT + jnp.cumsum(lengths[0])
     bounds = ends[:2].astype(jnp.int32)
     ids = adapter_ids[0]
-    meta = jnp.concatenate([bounds, ids, part[None].astype(jnp.int32)])
-    places = offset + jnp.arange(ROWS, dtype=jnp.int32)
-    token = token_adapter(places, meta)
-    chosen = (token[:, None] == (jnp.arange(AR, dtype=jnp.int32) // RANK)[None, :]).astype(f32)
-    chosen2 = jnp.concatenate([chosen, chosen], axis=1)
+    core = lax.axis_index("fsdp") & 1
+    meta = jnp.concatenate([bounds, ids, jnp.stack([part, core]).astype(jnp.int32)])
+    places = offset + lax.broadcasted_iota(jnp.int32, (ROWS, AR), 0)
+    lanes = lax.broadcasted_iota(jnp.int32, (ROWS, AR), 1)
+    chosen = (lanes // RANK == token_adapter(places, meta)).astype(f32)
     flat_down = jnp.transpose(adapter_in, (0, 2, 1, 3)).reshape(4, D, AR)
     flat_up = adapter_out.reshape(4, AR, D)
     gain_attn = attn_gain.astype(f32)
@@ -483,24 +539,19 @@
     w_out = lax.all_gather(out_weight, "fsdp", axis=0, tiled=True)
     w_up = lax.all_gather(up_weight, "fsdp", axis=0, tiled=True)
     w_down = lax.all_gather(down_weight, "fsdp", axis=0, tiled=True)
-    weights_all = lax.all_gather(by_pair(query_weight, key_weight, value_weight), "fsdp", axis=0, tiled=True)
+    weights_all = lax.all_gather(jnp.concatenate([query_weight, key_weight, value_weight], axis=1), "fsdp", axis=0, tiled=True)
 
     down_pair = jnp.concatenate([flat_down[0], flat_down[1]], axis=1)
-    zero = jnp.zeros((AR, D), bf16)
-    up_query = jnp.concatenate([flat_up[0], zero])
-    up_value = jnp.concatenate([zero, flat_up[1]])
-    up_pairs = by_pair(up_query, jnp.zeros_like(up_query), up_value)
-    up_mine = jnp.concatenate([mine(up_query), jnp.zeros((2 * AR, WIDTH), bf16), mine(up_value)], axis=1)
-    up_heads = jnp.transpose(up_mine.reshape(2 * AR, 3, 2, PW), (2, 0, 1, 3)).reshape(2, 2 * AR, 3 * PW)
-    low_late, high_late, up_heads, up_mine = lax.optimization_barrier((low, high, up_heads, up_mine))
+    up_mine = lax.dynamic_slice_in_dim(flat_up[:2], part * WIDTH, WIDTH, axis=2)
+    low_late, high_late, down_pair = lax.optimization_barrier((low, high, down_pair))
     near_low = swap(low_late, "heads", 1)
     far_high = swap(high_late, "heads", 2)
     both_low = swap(far_low, "heads", 1)
     both_high = swap(near_high, "heads", 2)
     scale_row = query_scale * HD ** (-0.5)
-    scale_mine = jnp.concatenate([jnp.tile(scale_row, LH), jnp.ones((2 * WIDTH,), f32)])[:, None]
-
-    wt, ut = weights_mine.T, up_mine.T
+    scale_mine = jnp.tile(scale_row, LH)[:, None]
+
+    wt, ut = weights_mine.T, jnp.transpose(up_mine, (0, 2, 1))
     done = ()
     for m, low, high in ((0, rows, None), (1, near_low, near_high), (2, far_low, far_high), (3, both_low, both_high)):
         done = qkv_project(meta, part ^ m, low, high, gain_attn[None, :], wt, down_pair, ut, scale_mine, done)
@@ -517,7 +568,6 @@
     logsum = jnp.concatenate([head_log, tail_log], axis=3)
 
     rows_in = inputs[0].astype(f32)
-    scaling_attn = lax.rsqrt(jnp.mean(rows_in * rows_in, axis=-1, keepdims=True) + EPSILON)
 
     branch = [tn(m.reshape(D, m.shape[2]), w_out) for m in (mixed_head, mixed_tail)]
     middle = rows_in + jnp.concatenate(branch)
@@ -528,7 +578,6 @@
     gate = jax.nn.sigmoid(before)
     hidden_low = (before * gate).astype(bf16)
     inner_down = (nn(hidden_low, flat_down[3]) * chosen).astype(bf16)
-    outputs = (middle + (nn(hidden_low, w_down) + nn(inner_down, flat_up[3]))).astype(bf16)
 
     upstream = cotangent[0].astype(f32)
     grad_after = cotangent[0]
@@ -554,44 +603,28 @@
     mlp_total, grad_second_pair = lax.optimization_barrier((mlp_total, grad_second_pair))
     arrived.append(exchange(grad_second_pair.reshape(PARTS, 3 * PW, ROWS)))
 
-    grads = [g.reshape(PARTS, 3 * PW, ROWS) for g in (grad_first_pair, grad_second_pair)]
     meta, arrived[0] = lax.optimization_barrier((meta, arrived[0]))
-    first_attn, second_attn = adapter_grads(meta, grads, normed_all, inner_all, up_heads)
-
-    slot = PARTS * 3 * PW
-
-    def back(p):
-        both, cut = arrived[p].reshape(slot, ROWS), slice(p * slot, (p + 1) * slot)
-        contract = (((0,), (1,)), ((), ()))
-        return (
-            lax.dot_general(both, weights_all[:, cut], contract, preferred_element_type=f32),
-            lax.dot_general(both, up_pairs[:, cut], contract, preferred_element_type=f32),
-        )
-
-    tiles = D // 128
-    mlp_total, first_attn = lax.optimization_barrier((mlp_total, first_attn))
-    mlp_total = gather_heads(mlp_total)
-    near_first = scatter_near(first_attn)
-    near_second = scatter_near(second_attn.reshape(tiles, -1, 128))
-    grad_normed, spread = back(0)
-    near_first, grad_normed = lax.optimization_barrier((near_first, grad_normed))
-    total = sum_far(jnp.concatenate([scatter_heads(near_first), near_second]))
-    grad_second_part, spread_second = back(1)
-    total, grad_second_part = lax.optimization_barrier((total, grad_second_part))
-    total = gather_near(gather_heads(total))
-    mlp_total = gather_near(mlp_total)
-    grad_normed, spread = grad_normed + grad_second_part, spread + spread_second
-    first_total = total[:tiles]
-    second_total = total[tiles:].reshape(tiles, 2, PARTS, -1, 128)
-    second_total = jnp.transpose(second_total, (2, 0, 1, 3, 4))
-    grad_normed = grad_normed + nt((spread * chosen2).astype(bf16), down_pair)
-    grad_inputs = grad_middle + normalize_back(rows_in, scaling_attn, gain_attn, grad_normed)
-
-    first_pair = jnp.transpose(first_total.reshape(tiles, 2, ADAPTERS, RANK, 128), (1, 2, 0, 4, 3))
-    first_rest = jnp.transpose(mlp_total[: 2 * AR].reshape(2, ADAPTERS, RANK, D), (0, 1, 3, 2))
-    grad_first = jnp.concatenate([first_pair.reshape(2, ADAPTERS, D, RANK), first_rest]).astype(f32)
-    second_pair = jnp.transpose(second_total.reshape(PARTS, 2, 2, PW, AR), (2, 4, 0, 1, 3)).reshape(2 * AR, D)
-    grad_second = jnp.concatenate([second_pair, mlp_total[2 * AR :]]).astype(f32).reshape(4, ADAPTERS, RANK, D)
+    keep, send = adapter_grads(meta, [grad_first_pair, grad_second_pair], normed_all, inner_all, up_mine)
+    hidden_late, inner_late, keep = lax.optimization_barrier((hidden_low, inner_down, keep))
+    outputs = (middle + (nn(hidden_late, w_down) + nn(inner_late, flat_up[3]))).astype(bf16)
+    total = sum_low(keep, swap(send, "fsdp", 1))
+    total = jnp.concatenate([scatter_heads(total[:AR]), total[AR:]])
+    total, arrived = lax.optimization_barrier((total, arrived))
+    total = sum_far(total)
+    meta, total, arrived = lax.optimization_barrier((meta, total, arrived))
+    total = gather_heads(jnp.concatenate([total, mlp_total]))
+    arrived = [a.reshape(PARTS, 3, PW, ROWS) for a in arrived]
+    grad_inputs = back_inputs(meta, arrived, weights_all, flat_up[:2], down_pair, rows, gain_attn[None, :], grad_middle)
+    total, grad_inputs = lax.optimization_barrier((total, grad_inputs))
+    total = gather_near(total).reshape(2, PARTS, 2 * SR + 2 * SR, D)
+
+    first_pair = total[:, :, :SR].reshape(2, AR, D)
+    second_pair = total[:, :, SR : 2 * SR].reshape(2, PARTS, SR, D // 128, AR)
+    second_pair = jnp.transpose(second_pair, (0, 4, 1, 3, 2)).reshape(2, AR, D)
+    mlp_pair = total[:, :, 2 * SR :].reshape(2, 2, AR, D)
+    grad_first = jnp.concatenate([first_pair, mlp_pair[0]]).reshape(4, ADAPTERS, RANK, D)
+    grad_first = jnp.transpose(grad_first, (0, 1, 3, 2)).astype(f32)
+    grad_second = jnp.concatenate([second_pair, mlp_pair[1]]).reshape(4, ADAPTERS, RANK, D).astype(f32)
     return (outputs[None], grad_inputs[None], grad_first, grad_second)
 
 

time: 460 us -> 474 us (1.030); the launches traced: 456 us -> 465 us
  waiting for transfers between devices: 34.6 us -> 75 us
  matrix products: 75.3 us -> 52.8 us
  local copies, waits for them, and re-layouts: 57.8 us -> 44.4 us
  Pallas kernels: 195 us -> 207 us
  other arithmetic: 29.5 us -> 19.2 us
    ppermute x29 -> x24, waiting for transfers between devices: 30.6 us -> 65.6 us  [swap(): return lax.ppermute(value, axis, [(i, i ^ mask) for i in range(count)])]
    dot_general x3 -> x0, matrix products: 21.1 us -> none  [the longest x2 19.2 us: back(): lax.dot_general(both, weights_all[:, cut], contract, preferred_element_ty...]
    pallas_call x1 -> x2, Pallas kernels: 11.2 us -> 30.1 us  [the longest x1 19.9 us: back_inputs(): pl.pallas_call(back_kernel, out_shape=jax.ShapeDtypeStruct((ROWS, D), f32...]
    another operation x9 -> x2, local copies, waits for them, and re-layouts: 10.6 us -> 0.82 us  [body(): scale_mine = jnp.tile(scale_row, LH)[:, None]]
    transpose x0 -> x3, local copies, waits for them, and re-layouts: none -> 8.34 us  [the longest x1 7.39 us: body(): second_pair = jnp.transpose(second_pair, (0, 4, 1, 3, 2)).reshape(2, AR, D)]
    unnamed x122 -> x89, local copies, waits for them, and re-layouts: 12.4 us -> 6.28 us
    pallas_call x2, Pallas kernels: 94.8 us -> 88.9 us  [attn_bwd(): pl.pallas_call(bwd_kernel, out_shape=jax.ShapeDtypeStruct((PARTS, 3, PW,...]
    reshape x7 -> x1, local copies, waits for them, and re-layouts: 5.96 us -> 0.39 us  [body(): second_pair = total[:, :, SR:2 * SR].reshape(2, PARTS, SR, D // 128, AR)]
  transfers between devices with their start and end apart: 40 -> 35, of which waited for: 6 -> 13; matrix products, arithmetic and copies ran while one was open for 31% -> 19% of each run, Pallas kernels for 43% -> 40%
where the time goes in v5:
time: 474 us; the launch traced here: 465 us
  Pallas kernels  207 us (44%)
  waiting for transfers between devices  75 us (16%)
  matrix products  52.8 us (11%)
  starting transfers between devices  50.8 us (11%)
  local copies, waits for them, and re-layouts  44.4 us (9%)
  other arithmetic  19.2 us (4%)
  between operations  15 us (3%)
    pallas_call x2, Pallas kernels, attn_bwd(): pl.pallas_call(bwd_kernel, out_shape=jax.ShapeDtypeStruct((PARTS, 3, PW,...  88.9 us
    ppermute x24, waiting for transfers between devices, swap(): return lax.ppermute(value, axis, [(i, i ^ mask) for i in range(count)])  65.6 us
    pallas_call x2, Pallas kernels, attn_fwd(): pl.pallas_call(fwd_kernel, out_shape=(jax.ShapeDtypeStruct((PARTS, WIDTH,...  51.4 us
    pallas_call x4, Pallas kernels, qkv_project(): pl.pallas_call(qkv_kernel, out_shape=(jax.ShapeDtypeStruct((3 * WIDTH, TO...  37 us
    ppermute x24, starting transfers between devices, swap(): return lax.ppermute(value, axis, [(i, i ^ mask) for i in range(count)])  26.1 us
    all_to_all x6, starting transfers between devices, exchange(): lax.all_to_all(value, 'heads', split_axis=0, concat_axis=0, tiled=True)  24.5 us
    dot_general x8, matrix products, nt(): lax.dot_general(a, b, (((1,), (1,)), ((), ())), preferred_element_type=f32)  23.8 us
    pallas_call x1, Pallas kernels, back_inputs(): pl.pallas_call(back_kernel, out_shape=jax.ShapeDtypeStruct((ROWS, D), f32...  19.9 us
  transfers between devices with their start and end apart: 35, of which 13 were waited for; matrix products, arithmetic and copies ran while one was open for 19% of the time, Pallas kernels for 40%

profile of v5, /device:TPU:9, one launch (start us, length us, event | category | flops | bytes accessed | tf_op | source)
XLA Modules:
  0.0 464.7 jit_solution(4455425978138574835)
XLA Ops:
  28.3 9.5 %collective-permute-done.low_ref = bf16[384,1280]{1,0:T(8,128)(2,1)} collective-permute-done((bf16[384,1280]{1,0:T(8,128)(2,1)}, bf16[384,1280]{1,0:T(8,128)(2,1)}, u32[]{:S(2)}, u32[]{:S(2)}) %collective-permute-start) | collective-permute-done | bytes 983072 | tf_op jit(solution)/shard_map/ppermute | solution.py:434
  45.3 4.3 copy.56
  49.6 9.2 %qkv_project.4 = (bf16[960,3072]{1,0:T(8,128)(2,1)}, bf16[3072,1280]{1,0:T(8,128)(2,1)}, bf16[3072,256]{1,0:T(8,128)(2,1)}) custom-call(s32[8]{0:T(128)} %pad_add_fusion.meta, s32[1]{0:T(128)} %bitcast.17.first, bf16[768,1280]{1,0:T(8,128)(2,1)} %bitcast.124, bf16[768,1280]{1,0:T(8,128)(2,1)} %bitcast.125, f32[1,1280]{1,0:T(1,128)} %reshape.163.gain_ref, ...), custom_call_target="tpu_custom_call" | custom-call | flops 2390753280 | bytes 8388608 | tf_op jit(solution)/shard_map/qkv_project/pallas_call | solution.py:83
  58.8 9.3 %qkv_project.5 = (bf16[960,3072]{1,0:T(8,128)(2,1)}, bf16[3072,1280]{1,0:T(8,128)(2,1)}, bf16[3072,256]{1,0:T(8,128)(2,1)}) custom-call(s32[8]{0:T(128)} %pad_add_fusion.meta, s32[1]{0:T(128)} %bitcast.16.first, bf16[384,1280]{1,0:T(8,128)(2,1)} %collective-permute-done.5.low_ref, ...), custom_call_target="tpu_custom_call", output_to_operand_aliasing={{0}: (9, {}), {1}: (10, {}), {2}: (11, {})} | custom-call | flops 2390753280 | bytes 8388608 | tf_op jit(solution)/shard_map/qkv_project/pallas_call | solution.py:83
  68.1 9.3 %qkv_project.6 = (bf16[960,3072]{1,0:T(8,128)(2,1)}, bf16[3072,1280]{1,0:T(8,128)(2,1)}, bf16[3072,256]{1,0:T(8,128)(2,1)}) custom-call(s32[8]{0:T(128)} %pad_add_fusion.meta, s32[1]{0:T(128)} %bitcast.15.first, bf16[384,1280]{1,0:T(8,128)(2,1)} %collective-permute-done.low_ref, ...), custom_call_target="tpu_custom_call", output_to_operand_aliasing={{0}: (9, {}), {1}: (10, {}), {2}: (11, {})} | custom-call | flops 2390753280 | bytes 8388608 | tf_op jit(solution)/shard_map/qkv_project/pallas_call | solution.py:83
  80.0 9.2 %qkv_project.7 = (bf16[960,3072]{1,0:T(8,128)(2,1)}, bf16[3072,1280]{1,0:T(8,128)(2,1)}, bf16[3072,256]{1,0:T(8,128)(2,1)}) custom-call(s32[8]{0:T(128)} %pad_add_fusion.meta, s32[1]{0:T(128)} %bitcast.6.first, bf16[384,1280]{1,0:T(8,128)(2,1)} %collective-permute-done.1.low_ref, ...), custom_call_target="tpu_custom_call", output_to_operand_aliasing={{0}: (9, {}), {1}: (10, {}), {2}: (11, {})} | custom-call | flops 2390753280 | bytes 8388608 | tf_op jit(solution)/shard_map/qkv_project/pallas_call | solution.py:83
  89.2 31.0 %attn_fwd.2 = (bf16[4,320,512]{2,1,0:T(8,128)(2,1)}, f32[4,4,1,512]{3,2,1,0:T(1,128)}) custom-call(s32[2]{0:T(128)} %copy-done.36, bf16[960,3072]{1,0:T(8,128)(2,1)} %get-tuple-element.62.q_ref.k_ref.v_ref, bf16[960,3072]{1,0:T(8,128)(2,1)} %get-tuple-element.62.q_ref.k_ref.v_ref, bf16[960,3072]{1,0:T(8,128)(2,1)} %get-tuple-element.62.q_ref.k_ref.v_ref), custom_call_target="tpu_custom_call" | custom-call | flops 25999998976 | bytes 5242880 | tf_op jit(solution)/shard_map/attn_fwd/pallas_call | solution.py:289
  120.2 4.7 %all-to-all-start = ((bf16[4,320,512]{2,1,0:T(8,128)(2,1)}), bf16[4,320,512]{2,1,0:T(8,128)(2,1)}, u32[]{:S(2)}, u32[]{:S(2)}) async-start(bf16[4,320,512]{2,1,0:T(8,128)(2,1)} %get-tuple-element.66), calls=%async_computation | async-start | bytes 2621440 | tf_op jit(solution)/shard_map/all_to_all | solution.py:429
  124.8 20.4 %attn_fwd.3 = (bf16[4,320,256]{2,1,0:T(8,128)(2,1)}, f32[4,4,1,256]{3,2,1,0:T(1,128)}) custom-call(s32[2]{0:T(128)} %copy-done.36, bf16[960,3072]{1,0:T(8,128)(2,1)} %get-tuple-element.62.q_ref.k_ref.v_ref, bf16[960,3072]{1,0:T(8,128)(2,1)} %get-tuple-element.62.q_ref.k_ref.v_ref, bf16[960,3072]{1,0:T(8,128)(2,1)} %get-tuple-element.62.q_ref.k_ref.v_ref), custom_call_target="tpu_custom_call" | custom-call | flops 12999999488 | bytes 5242880 | tf_op jit(solution)/shard_map/attn_fwd/pallas_call | solution.py:289
  151.7 3.9 fusion.41
  155.6 6.8 %fusion.14 = f32[768,1280]{1,0:T(8,128)} fusion(bf16[1280,1280]{1,0:T(8,128)(2,1)} %all-gather.12.cloned.1.call-done, bf16[1,768,1280]{2,1,0:T(8,128)(2,1)S(1)} %copy-done.2), kind=kOutput, calls=%fused_computation.32 | convolution fusion | flops 2516582400 | bytes 9175040 | tf_op jit(solution)/shard_map/dot_general | solution.py:31
  162.4 4.8 %fusion.48 = f32[512,1280]{1,0:T(8,128)} fusion(bf16[1280,512]{1,0:T(8,128)(2,1)} %bitcast.18, bf16[1280,1280]{1,0:T(8,128)(2,1)S(1)} %copy-done.7), kind=kOutput, calls=%fused_computation.115 | convolution fusion | flops 1677721600 | bytes 7208960 | tf_op jit(solution)/shard_map/dot_general | solution.py:35
  175.0 6.7 %fusion.40 = f32[768,1280]{1,0:T(8,128)S(1)} fusion(bf16[1280,1280]{1,0:T(8,128)(2,1)} %all-gather.10.cloned.1.call-done, f32[768,1280]{1,0:T(8,128)} %get-tuple-element.97, f32[1280]{0:T(1024)S(1)} %convert_element_type.147, f32[768]{0:T(1024)S(1)} %get-tuple-element.123), kind=kOutput, calls=%fused_computation.107 | convolution fusion | flops 2519531520 | bytes 11149312 | tf_op jit(solution)/shard_map/dot_general | solution.py:39
  202.9 4.2 all-to-all-start.2
  207.1 4.7 %convolution_convert_fusion.4 = bf16[768,640]{0,1:T(8,128)(2,1)} fusion(bf16[640,1280]{1,0:T(8,128)(2,1)S(1)} %bitcast.137, f32[768,1280]{1,0:T(8,128)} %copy-done.6), kind=kOutput, calls=%fused_computation.35 | convolution fusion | flops 1259765760 | bytes 6553600 | tf_op jit(solution)/shard_map/dot_general | solution.py:31
  213.1 7.2 %all-to-all-done.2.do_ref = bf16[4,160,768]{2,1,0:T(8,128)(2,1)} async-done(((bf16[4,160,768]{2,1,0:T(8,128)(2,1)}), bf16[4,160,768]{2,1,0:T(8,128)(2,1)}, u32[]{:S(2)}, u32[]{:S(2)}) %all-to-all-start.2) | async-done | bytes 983072 | tf_op jit(solution)/shard_map/all_to_all | solution.py:429
  226.7 44.5 %attn_bwd.2.g0_ref = bf16[4,3,160,768]{3,2,1,0:T(8,128)(2,1)} custom-call(s32[8]{0:T(128)} %pad_add_fusion.meta, f32[80,1]{1,0:T(8,128)} %copy.67.scale_ref, bf16[960,3072]{1,0:T(8,128)(2,1)} %get-tuple-element.62.q_ref.k_ref.v_ref, bf16[960,3072]{1,0:T(8,128)(2,1)} %get-tuple-element.62.q_ref.k_ref.v_ref, ...), custom_call_target="tpu_custom_call" | custom-call | flops 35999997952 | bytes 16777216 | tf_op jit(solution)/shard_map/attn_bwd/pallas_call | solution.py:390
  271.3 4.5 collective-permute-start.10
  278.9 3.7 all-to-all-start.3
  282.6 44.4 %attn_bwd.3.g1_ref = bf16[4,3,160,768]{3,2,1,0:T(8,128)(2,1)} custom-call(s32[8]{0:T(128)} %pad_add_fusion.meta, f32[80,1]{1,0:T(8,128)} %copy.67.scale_ref, bf16[960,3072]{1,0:T(8,128)(2,1)} %get-tuple-element.62.q_ref.k_ref.v_ref, bf16[960,3072]{1,0:T(8,128)(2,1)} %get-tuple-element.62.q_ref.k_ref.v_ref, ...), custom_call_target="tpu_custom_call" | custom-call | flops 35999997952 | bytes 16777216 | tf_op jit(solution)/shard_map/attn_bwd/pallas_call | solution.py:390
  330.5 4.8 %all-to-all-start.5 = ((bf16[4,480,768]{2,1,0:T(8,128)(2,1)}), bf16[4,480,768]{2,1,0:T(8,128)(2,1)}, u32[]{:S(2)}, u32[]{:S(2)}) async-start(bf16[4,480,768]{2,1,0:T(8,128)(2,1)} %bitcast.120), calls=%async_computation.5 | async-start | bytes 5898240 | tf_op jit(solution)/shard_map/all_to_all | solution.py:429
  335.3 10.2 %adapter_grads.1 = (bf16[160,1280]{1,0:T(8,128)(2,1)}, bf16[160,1280]{1,0:T(8,128)(2,1)}) custom-call(s32[8]{0:T(128)} %pad_add_fusion.meta, bf16[4,3,160,768]{3,2,1,0:T(8,128)(2,1)} %attn_bwd.2.g0_ref, bf16[4,3,160,768]{3,2,1,0:T(8,128)(2,1)} %attn_bwd.3.g1_ref, bf16[3072,1280]{1,0:T(8,128)(2,1)} %get-tuple-element.78.normed_ref, ...), custom_call_target="tpu_custom_call" | custom-call | flops 4026531840 | bytes 20971520 | tf_op jit(solution)/shard_map/adapter_grads/pallas_call | solution.py:144
  351.4 20.0 %collective-permute-done.14 = bf16[32,1280]{1,0:T(8,128)(2,1)S(1)} collective-permute-done((bf16[32,1280]{1,0:T(8,128)(2,1)S(1)}, bf16[32,1280]{1,0:T(8,128)(2,1)S(1)}, u32[]{:S(2)}, u32[]{:S(2)}) %collective-permute-start.14) | collective-permute-done | bytes 81952 | tf_op jit(solution)/shard_map/ppermute | solution.py:434
  378.1 4.1 collective-permute-done.17
  382.2 6.7 %collective-permute-done.18 = bf16[64,1280]{1,0:T(8,128)(2,1)S(1)} collective-permute-done((bf16[64,1280]{1,0:T(8,128)(2,1)S(1)}, bf16[64,1280]{1,0:T(8,128)(2,1)S(1)}, u32[]{:S(2)}, u32[]{:S(2)}) %collective-permute-start.18) | collective-permute-done | bytes 163872 | tf_op jit(solution)/shard_map/ppermute | solution.py:434
  388.9 4.5 collective-permute-done.19
  396.2 7.1 %collective-permute-done.20 = bf16[128,1280]{1,0:T(8,128)(2,1)S(1)} collective-permute-done((bf16[128,1280]{1,0:T(8,128)(2,1)S(1)}, bf16[128,1280]{1,0:T(8,128)(2,1)S(1)}, u32[]{:S(2)}, u32[]{:S(2)}) %collective-permute-start.20) | collective-permute-done | bytes 327712 | tf_op jit(solution)/shard_map/ppermute | solution.py:434
  403.3 6.5 %collective-permute-done.21 = bf16[128,1280]{1,0:T(8,128)(2,1)S(1)} collective-permute-done((bf16[128,1280]{1,0:T(8,128)(2,1)S(1)}, bf16[128,1280]{1,0:T(8,128)(2,1)S(1)}, u32[]{:S(2)}, u32[]{:S(2)}) %collective-permute-start.21) | collective-permute-done | bytes 327712 | tf_op jit(solution)/shard_map/ppermute | solution.py:434
  410.1 19.9 %back_inputs.1 = f32[768,1280]{1,0:T(8,128)} custom-call(s32[8]{0:T(128)} %pad_add_fusion.meta, bf16[4,3,160,768]{3,2,1,0:T(8,128)(2,1)} %bitcast.129, bf16[4,3,160,768]{3,2,1,0:T(8,128)(2,1)} %bitcast.46.b1_ref, bf16[1280,3840]{1,0:T(8,128)(2,1)} %all-gather.14.cloned.1.call-done.w_ref, bf16[2,128,1280]{2,1,0:T(8,128)(2,1)} %bitcast.136, ...), custom_call_target="tpu_custom_call" | custom-call | flops 7549747200 | bytes 25165824 | tf_op jit(solution)/shard_map/back_inputs/pallas_call | solution.py:203
  431.2 4.8 %fusion.51 = f32[768,1280]{1,0:T(8,128)S(1)} fusion(bf16[768,1280]{1,0:T(8,128)(2,1)S(1)} %copy-done.13, bf16[1280,1280]{1,0:T(8,128)(2,1)} %all-gather.12.cloned.1.call-done), kind=kOutput, calls=%fused_computation.118 | convolution fusion | flops 2516582400 | bytes 9175040 | tf_op jit(solution)/shard_map/dot_general | solution.py:39
  441.8 7.4 %copy.69 = bf16[2,128,4,10,32]{4,3,2,1,0:T(8,128)(2,1)} copy(bf16[2,128,4,10,32]{1,3,4,2,0:T(8,128)(2,1)S(1)} %bitcast.127) | data formatting | bytes 1310720 | tf_op jit(solution)/shard_map/transpose | solution.py:623
  449.2 5.2 %concatenate.82 = bf16[2,8,16,1280]{3,2,1,0:T(8,128)(2,1)S(1)} reshape(bf16[2,128,4,10,32]{4,3,2,1,0:T(8,128)(2,1)} %copy.69) | data formatting | bytes 1310720 | tf_op jit(solution)/shard_map/concatenate | solution.py:627
  (224 shorter events, 106.4 us)
Async XLA Ops:
  7.2 38.1 %all-gather.6.cloned.1.call-start = ((), (), s32[]{:S(2)}) async-start(), calls=%async_computation.6 | async-start | bytes 2949120 | tf_op jit(solution)/shard_map/all_gather | solution.py:538
  10.4 141.3 %all-gather.8.cloned.1.call-start = ((), (), s32[]{:S(2)}) async-start(), calls=%async_computation.7 | async-start | bytes 3686400 | tf_op jit(solution)/shard_map/all_gather | solution.py:539
  11.2 144.4 %all-gather.12.cloned.1.call-start = ((), (), s32[]{:S(2)}) async-start(), calls=%async_computation.9 | async-start | bytes 3686400 | tf_op jit(solution)/shard_map/all_gather | solution.py:541
  11.9 163.1 %all-gather.10.cloned.1.call-start = ((), (), s32[]{:S(2)}) async-start(), calls=%async_computation.8 | async-start | bytes 3686400 | tf_op jit(solution)/shard_map/all_gather | solution.py:540
  12.5 397.6 %all-gather.14.cloned.1.call-start = ((), (), s32[]{:S(2)}) async-start(), calls=%async_computation.10 | async-start | bytes 11059200 | tf_op jit(solution)/shard_map/all_gather | solution.py:542
  13.9 24.1 %collective-permute-start.2 = (bf16[384,1280]{1,0:T(8,128)(2,1)}, bf16[384,1280]{1,0:T(8,128)(2,1)}, u32[]{:S(2)}, u32[]{:S(2)}) collective-permute-start(bf16[384,1280]{1,0:T(8,128)(2,1)} %get-tuple-element.51), channel_id=1, source_target_pairs={{0,8},{8,0},{16,24},{24,16},{1,9},{9,1},{17,25},{25,17},{2,10},{10... | collective-permute-start | bytes 2949128 | tf_op jit(solution)/shard_map/ppermute | solution.py:434
  15.1 22.7 %collective-permute-start = (bf16[384,1280]{1,0:T(8,128)(2,1)}, bf16[384,1280]{1,0:T(8,128)(2,1)}, u32[]{:S(2)}, u32[]{:S(2)}) collective-permute-start(bf16[384,1280]{1,0:T(8,128)(2,1)} %get-tuple-element.52), channel_id=1, source_target_pairs={{0,16},{8,24},{16,0},{24,8},{1,17},{9,25},{17,1},{25,9},{2,18},{10... | collective-permute-start | bytes 2949128 | tf_op jit(solution)/shard_map/ppermute | solution.py:434
  18.7 40.1 %collective-permute-start.5 = (bf16[384,1280]{1,0:T(8,128)(2,1)}, bf16[384,1280]{1,0:T(8,128)(2,1)}, u32[]{:S(2)}, u32[]{:S(2)}) collective-permute-start(bf16[384,1280]{1,0:T(8,128)(2,1)} %get-tuple-element.52), channel_id=1, source_target_pairs={{0,8},{8,0},{16,24},{24,16},{1,9},{9,1},{17,25},{25,17},{2,10},{10... | collective-permute-start | bytes 2949128 | tf_op jit(solution)/shard_map/ppermute | solution.py:434
  19.0 49.1 %collective-permute-start.4 = (bf16[384,1280]{1,0:T(8,128)(2,1)}, bf16[384,1280]{1,0:T(8,128)(2,1)}, u32[]{:S(2)}, u32[]{:S(2)}) collective-permute-start(bf16[384,1280]{1,0:T(8,128)(2,1)} %get-tuple-element.51), channel_id=1, source_target_pairs={{0,16},{8,24},{16,0},{24,8},{1,17},{9,25},{17,1},{25,9},{2,18},{10... | collective-permute-start | bytes 2949128 | tf_op jit(solution)/shard_map/ppermute | solution.py:434
  37.8 41.2 %collective-permute-start.1 = (bf16[384,1280]{1,0:T(8,128)(2,1)}, bf16[384,1280]{1,0:T(8,128)(2,1)}, u32[]{:S(2)}, u32[]{:S(2)}) collective-permute-start(bf16[384,1280]{1,0:T(8,128)(2,1)} %collective-permute-done.low_ref), channel_id=1, source_target_pairs={{0,8},{8,0},{16,24},{24,16},{1,9},{9,1},{17,25},{25,17},{2,10},{10... | collective-permute-start | bytes 2949128 | tf_op jit(solution)/shard_map/ppermute | solution.py:434
  38.1 41.9 %collective-permute-start.3 = (bf16[384,1280]{1,0:T(8,128)(2,1)}, bf16[384,1280]{1,0:T(8,128)(2,1)}, u32[]{:S(2)}, u32[]{:S(2)}) collective-permute-start(bf16[384,1280]{1,0:T(8,128)(2,1)} %collective-permute-done.2.high_ref), channel_id=1, source_target_pairs={{0,16},{8,24},{16,0},{24,8},{1,17},{9,25},{17,1},{25,9},{2,18},{10... | collective-permute-start | bytes 2949128 | tf_op jit(solution)/shard_map/ppermute | solution.py:434
  120.2 28.0 %all-to-all-start = ((bf16[4,320,512]{2,1,0:T(8,128)(2,1)}), bf16[4,320,512]{2,1,0:T(8,128)(2,1)}, u32[]{:S(2)}, u32[]{:S(2)}) async-start(bf16[4,320,512]{2,1,0:T(8,128)(2,1)} %get-tuple-element.66), calls=%async_computation | async-start | bytes 2621440 | tf_op jit(solution)/shard_map/all_to_all | solution.py:429
  148.1 19.0 %all-to-all-start.1 = ((bf16[4,320,256]{2,1,0:T(8,128)(2,1)}), bf16[4,320,256]{2,1,0:T(8,128)(2,1)S(1)}, u32[]{:S(2)}, u32[]{:S(2)}) async-start(bf16[4,320,256]{2,1,0:T(8,128)(2,1)} %get-tuple-element.68), calls=%async_computation.1 | async-start | bytes 1310720 | tf_op jit(solution)/shard_map/all_to_all | solution.py:429
  193.8 18.0 %collective-permute-start.6 = (bf16[256,1280]{1,0:T(8,128)(2,1)}, bf16[256,1280]{1,0:T(8,128)(2,1)}, u32[]{:S(2)}, u32[]{:S(2)}) collective-permute-start(bf16[256,1280]{1,0:T(8,128)(2,1)} %constant_dynamic-slice_fusion.6), channel_id=1, source_target_pairs={{0,1},{1,0},{2,3},{3,2},{4,5},{5,4},{6,7},{7,6},{8,9},{9,8},{10,11... | collective-permute-start | bytes 1966088 | tf_op jit(solution)/shard_map/ppermute | solution.py:434
  202.9 17.4 %all-to-all-start.2 = ((bf16[4,160,768]{2,1,0:T(8,128)(2,1)}), bf16[4,160,768]{2,1,0:T(8,128)(2,1)}, u32[]{:S(2)}, u32[]{:S(2)}) async-start(bf16[4,160,768]{2,1,0:T(8,128)(2,1)} %bitcast.148), calls=%async_computation.2 | async-start | bytes 1966080 | tf_op jit(solution)/shard_map/all_to_all | solution.py:429
  220.3 57.7 %all-to-all-start.4 = ((bf16[4,160,768]{2,1,0:T(8,128)(2,1)}), bf16[4,160,768]{2,1,0:T(8,128)(2,1)S(1)}, u32[]{:S(2)}, u32[]{:S(2)}) async-start(bf16[4,160,768]{2,1,0:T(8,128)(2,1)} %bitcast.147), calls=%async_computation.4 | async-start | bytes 1966080 | tf_op jit(solution)/shard_map/all_to_all | solution.py:429
  223.9 47.2 %collective-permute-start.7 = (bf16[64,1280]{1,0:T(8,128)(2,1)S(1)}, bf16[64,1280]{1,0:T(8,128)(2,1)S(1)}, u32[]{:S(2)}, u32[]{:S(2)}) collective-permute-start(bf16[64,1280]{1,0:T(8,128)(2,1)S(1)} %get-tuple-element.116), channel_id=1, source_target_pairs={{0,8},{8,0},{16,24},{24,16},{1,9},{9,1},{17,25},{25,17},{2,10},{10... | collective-permute-start | bytes 491528 | tf_op jit(solution)/shard_map/ppermute | solution.py:434
  225.4 45.8 %collective-permute-start.8 = (bf16[64,1280]{1,0:T(8,128)(2,1)S(1)}, bf16[64,1280]{1,0:T(8,128)(2,1)S(1)}, u32[]{:S(2)}, u32[]{:S(2)}) collective-permute-start(bf16[64,1280]{1,0:T(8,128)(2,1)S(1)} %get-tuple-element.118), channel_id=1, source_target_pairs={{0,16},{8,24},{16,0},{24,8},{1,17},{9,25},{17,1},{25,9},{2,18},{10... | collective-permute-start | bytes 491528 | tf_op jit(solution)/shard_map/ppermute | solution.py:434
  226.6 44.6 %collective-permute-start.9 = (bf16[64,1280]{1,0:T(8,128)(2,1)S(1)}, bf16[64,1280]{1,0:T(8,128)(2,1)S(1)}, u32[]{:S(2)}, u32[]{:S(2)}) collective-permute-start(bf16[64,1280]{1,0:T(8,128)(2,1)S(1)} %get-tuple-element.117), channel_id=1, source_target_pairs={{0,24},{8,16},{16,8},{24,0},{1,25},{9,17},{17,9},{25,1},{2,26},{10... | collective-permute-start | bytes 491528 | tf_op jit(solution)/shard_map/ppermute | solution.py:434
  271.3 55.8 %collective-permute-start.10 = (bf16[64,1280]{1,0:T(8,128)(2,1)S(1)}, bf16[64,1280]{1,0:T(8,128)(2,1)S(1)}, u32[]{:S(2)}, u32[]{:S(2)}) collective-permute-start(bf16[64,1280]{1,0:T(8,128)(2,1)S(1)} %add_convert_fusion.4), channel_id=1, source_target_pairs={{0,2},{1,3},{2,0},{3,1},{4,6},{5,7},{6,4},{7,5},{8,10},{9,11},{10,... | collective-permute-start | bytes 491528 | tf_op jit(solution)/shard_map/ppermute | solution.py:434
  275.8 51.3 %collective-permute-start.11 = (bf16[64,1280]{1,0:T(8,128)(2,1)S(1)}, bf16[64,1280]{1,0:T(8,128)(2,1)}, u32[]{:S(2)}, u32[]{:S(2)}) collective-permute-start(bf16[64,1280]{1,0:T(8,128)(2,1)S(1)} %add_convert_fusion.4), channel_id=1, source_target_pairs={{0,4},{1,5},{2,6},{3,7},{4,0},{5,1},{6,2},{7,3},{8,12},{9,13},{10,... | collective-permute-start | bytes 491528 | tf_op jit(solution)/shard_map/ppermute | solution.py:434
  277.8 50.0 %collective-permute-start.12 = (bf16[64,1280]{1,0:T(8,128)(2,1)S(1)}, bf16[64,1280]{1,0:T(8,128)(2,1)}, u32[]{:S(2)}, u32[]{:S(2)}) collective-permute-start(bf16[64,1280]{1,0:T(8,128)(2,1)S(1)} %add_convert_fusion.4), channel_id=1, source_target_pairs={{0,6},{1,7},{2,4},{3,5},{4,2},{5,3},{6,0},{7,1},{8,14},{9,15},{10,... | collective-permute-start | bytes 491528 | tf_op jit(solution)/shard_map/ppermute | solution.py:434
  278.9 50.0 %all-to-all-start.3 = ((bf16[4,480,768]{2,1,0:T(8,128)(2,1)}), bf16[4,480,768]{2,1,0:T(8,128)(2,1)S(1)}, u32[]{:S(2)}, u32[]{:S(2)}) async-start(bf16[4,480,768]{2,1,0:T(8,128)(2,1)} %bitcast.121), calls=%async_computation.3 | async-start | bytes 5898240 | tf_op jit(solution)/shard_map/all_to_all | solution.py:429
  330.5 43.6 %all-to-all-start.5 = ((bf16[4,480,768]{2,1,0:T(8,128)(2,1)}), bf16[4,480,768]{2,1,0:T(8,128)(2,1)}, u32[]{:S(2)}, u32[]{:S(2)}) async-start(bf16[4,480,768]{2,1,0:T(8,128)(2,1)} %bitcast.120), calls=%async_computation.5 | async-start | bytes 5898240 | tf_op jit(solution)/shard_map/all_to_all | solution.py:429
  348.6 22.8 %collective-permute-start.14 = (bf16[32,1280]{1,0:T(8,128)(2,1)S(1)}, bf16[32,1280]{1,0:T(8,128)(2,1)S(1)}, u32[]{:S(2)}, u32[]{:S(2)}) collective-permute-start(bf16[32,1280]{1,0:T(8,128)(2,1)S(1)} %get-tuple-element.119), channel_id=1, source_target_pairs={{0,8},{8,0},{16,24},{24,16},{1,9},{9,1},{17,25},{25,17},{2,10},{10... | collective-permute-start | bytes 245768 | tf_op jit(solution)/shard_map/ppermute | solution.py:434
  350.1 21.3 %collective-permute-start.15 = (bf16[32,1280]{1,0:T(8,128)(2,1)S(1)}, bf16[32,1280]{1,0:T(8,128)(2,1)S(1)}, u32[]{:S(2)}, u32[]{:S(2)}) collective-permute-start(bf16[32,1280]{1,0:T(8,128)(2,1)S(1)} %get-tuple-element.121), channel_id=1, source_target_pairs={{0,16},{8,24},{16,0},{24,8},{1,17},{9,25},{17,1},{25,9},{2,18},{10... | collective-permute-start | bytes 245768 | tf_op jit(solution)/shard_map/ppermute | solution.py:434
  351.3 22.7 %collective-permute-start.16 = (bf16[32,1280]{1,0:T(8,128)(2,1)S(1)}, bf16[32,1280]{1,0:T(8,128)(2,1)S(1)}, u32[]{:S(2)}, u32[]{:S(2)}) collective-permute-start(bf16[32,1280]{1,0:T(8,128)(2,1)S(1)} %get-tuple-element.120), channel_id=1, source_target_pairs={{0,24},{8,16},{16,8},{24,0},{1,25},{9,17},{17,9},{25,1},{2,26},{10... | collective-permute-start | bytes 245768 | tf_op jit(solution)/shard_map/ppermute | solution.py:434
  375.6 13.3 %collective-permute-start.18 = (bf16[64,1280]{1,0:T(8,128)(2,1)S(1)}, bf16[64,1280]{1,0:T(8,128)(2,1)S(1)}, u32[]{:S(2)}, u32[]{:S(2)}) collective-permute-start(bf16[64,1280]{1,0:T(8,128)(2,1)S(1)} %pad_maximum_fusion.5), channel_id=1, source_target_pairs={{0,4},{1,5},{2,6},{3,7},{4,0},{5,1},{6,2},{7,3},{8,12},{9,13},{10,... | collective-permute-start | bytes 491528 | tf_op jit(solution)/shard_map/ppermute | solution.py:434
  377.9 15.5 %collective-permute-start.19 = (bf16[64,1280]{1,0:T(8,128)(2,1)S(1)}, bf16[64,1280]{1,0:T(8,128)(2,1)S(1)}, u32[]{:S(2)}, u32[]{:S(2)}) collective-permute-start(bf16[64,1280]{1,0:T(8,128)(2,1)S(1)} %pad_maximum_fusion.5), channel_id=1, source_target_pairs={{0,6},{1,7},{2,4},{3,5},{4,2},{5,3},{6,0},{7,1},{8,14},{9,15},{10,... | collective-permute-start | bytes 491528 | tf_op jit(solution)/shard_map/ppermute | solution.py:434
  393.5 9.8 %collective-permute-start.20 = (bf16[128,1280]{1,0:T(8,128)(2,1)S(1)}, bf16[128,1280]{1,0:T(8,128)(2,1)S(1)}, u32[]{:S(2)}, u32[]{:S(2)}) collective-permute-start(bf16[128,1280]{1,0:T(8,128)(2,1)S(1)} %constant_dynamic-update-slice_fusion.4), channel_id=1, source_target_pairs={{0,24},{8,16},{16,8},{24,0},{1,25},{9,17},{17,9},{25,1},{2,26},{10... | collective-permute-start | bytes 983048 | tf_op jit(solution)/shard_map/ppermute | solution.py:434
  393.8 16.0 %collective-permute-start.21 = (bf16[128,1280]{1,0:T(8,128)(2,1)S(1)}, bf16[128,1280]{1,0:T(8,128)(2,1)S(1)}, u32[]{:S(2)}, u32[]{:S(2)}) collective-permute-start(bf16[128,1280]{1,0:T(8,128)(2,1)S(1)} %constant_dynamic-update-slice_fusion.4), channel_id=1, source_target_pairs={{0,16},{8,24},{16,0},{24,8},{1,17},{9,25},{17,1},{25,9},{2,18},{10... | collective-permute-start | bytes 983048 | tf_op jit(solution)/shard_map/ppermute | solution.py:434
  395.0 14.8 %collective-permute-start.22 = (bf16[128,1280]{1,0:T(8,128)(2,1)S(1)}, bf16[128,1280]{1,0:T(8,128)(2,1)S(1)}, u32[]{:S(2)}, u32[]{:S(2)}) collective-permute-start(bf16[128,1280]{1,0:T(8,128)(2,1)S(1)} %constant_dynamic-update-slice_fusion.4), channel_id=1, source_target_pairs={{0,8},{8,0},{16,24},{24,16},{1,9},{9,1},{17,25},{25,17},{2,10},{10... | collective-permute-start | bytes 983048 | tf_op jit(solution)/shard_map/ppermute | solution.py:434
  (46 other events, 483.7 us)
Sparse Core Ops, SparseCore 0:
  10.5 34.7 all-gather.5
  47.0 37.9 all-gather.7
  86.6 38.1 all-gather.11
  126.3 38.1 all-gather.9
  166.0 90.9 all-gather.13

commit v6 on v5

--- a/solution.py
+++ b/solution.py
@@ -70,10 +70,11 @@
     chosen = (lane % AR) // RANK == token_adapter(pos, meta)
     inner = jnp.where(chosen, nn(normed, down_ref[...]), 0.0).astype(bf16)
     inner_ref[...] = inner
-    out = nt(wt_ref[0:WIDTH, :], normed) + nt(up_ref[0], inner[:, :AR])
-    out_ref[0:WIDTH, :] = (out * scale_ref[...]).astype(bf16)
-    out_ref[WIDTH : 2 * WIDTH, :] = nt(wt_ref[WIDTH : 2 * WIDTH, :], normed).astype(bf16)
-    out_ref[2 * WIDTH :, :] = (nt(wt_ref[2 * WIDTH :, :], normed) + nt(up_ref[1], inner[:, AR:])).astype(bf16)
+    out = nt(wt_ref[...], normed)
+    query = out[:WIDTH] + nt(up_ref[0], inner[:, :AR])
+    out_ref[0:WIDTH, :] = (query * scale_ref[...]).astype(bf16)
+    out_ref[WIDTH : 2 * WIDTH, :] = out[WIDTH : 2 * WIDTH].astype(bf16)
+    out_ref[2 * WIDTH :, :] = (out[2 * WIDTH :] + nt(up_ref[1], inner[:, AR:])).astype(bf16)
 
 
 def qkv_project(meta, chunk, low, high, gain, wt, down, up, scale, done):
@@ -224,6 +225,48 @@
     )(meta, *arrived, weights, up, down, rows, gain, grad_middle)
 
 
+def assemble_kernel(meta, own_ref, other_ref, first_ref, second_ref, turned):
+    part, core = meta[6], meta[7]
+    for ref, a in ((own_ref, core), (other_ref, 1 - core)):
+        for m in range(PARTS):
+            where = part ^ m
+            piece_rows = lambda n: pl.ds(pl.multiple_of(where * n, n), n)
+            first_ref[a, piece_rows(SR), :] = ref[m, 0:SR, :].astype(f32)
+            for c in range(D // 128):
+                turned[pl.ds(pl.multiple_of(where * WIDTH + c * SR, SR), SR), :] = ref[m, SR : 2 * SR, c * 128 : (c + 1) * 128]
+            rows = pl.ds(pl.multiple_of((where % 2) * 2 * SR, 2 * SR), 2 * SR)
+            mlp = ref[m, 2 * SR :, :].astype(f32)
+
+            @pl.when(a == 0)
+            def _(mlp=mlp, rows=rows, where=where):
+                first_ref[2 + where // 2, rows, :] = mlp
+
+            @pl.when(a == 1)
+            def _(mlp=mlp, rows=rows, where=where):
+                second_ref[2 + where // 2, rows, :] = mlp
+
+        for c in range(D // 128):
+            second_ref[a, :, c * 128 : (c + 1) * 128] = turned[c * 128 : (c + 1) * 128, :].T.astype(f32)
+
+
+def assemble(meta, own, other):
+    whole = lambda shape: pl.BlockSpec(shape, lambda i, m: (0,) * len(shape))
+    return pl.pallas_call(
+        assemble_kernel,
+        out_shape=[jax.ShapeDtypeStruct((4, AR, D), f32)] * 2,
+        grid_spec=pltpu.PrefetchScalarGridSpec(
+            num_scalar_prefetch=1,
+            grid=(1,),
+            in_specs=[whole((PARTS, 4 * SR, D))] * 2,
+            out_specs=[whole((4, AR, D))] * 2,
+            scratch_shapes=[pltpu.VMEM((D, AR), bf16)],
+        ),
+        compiler_params=pltpu.CompilerParams(dimension_semantics=("arbitrary",), vmem_limit_bytes=60 << 20),
+        cost_estimate=pl.CostEstimate(flops=1 << 20, bytes_accessed=8 << 20, transcendentals=0),
+        name="assemble",
+    )(meta, own, other)
+
+
 HPB = LH
 BLOCKS = ROWS // B
 NEG = -1e30
@@ -467,32 +510,10 @@
     return sum_low(piece(value, core, 2), swap(piece(value, 1 - core, 2), "fsdp", 1))
 
 
-def paired(value, axis, mask, high):
-    other = swap(value, axis, mask)
-    return jnp.where(
-        high, jnp.concatenate([other, value], axis=-2), jnp.concatenate([value, other], axis=-2)
-    )
-
-
-def gather_near(value):
-    return paired(value, "fsdp", 1, lax.axis_index("fsdp") % 2 == 1)
-
-
 def scatter_heads(value):
     part = lax.axis_index("heads")
     terms = [swap(piece(value, part ^ m, PARTS), "heads", m) for m in (1, 2, 3)]
     return sum_low(piece(value, part, PARTS), *terms)
-
-
-def gather_heads(value):
-    part = lax.axis_index("heads")
-    near, far, both = [swap(value, "heads", m) for m in (1, 2, 3)]
-    odd, high = part % 2 == 1, part >= 2
-    low_pair = [jnp.where(odd, near, value), jnp.where(odd, value, near)]
-    high_pair = [jnp.where(odd, both, far), jnp.where(odd, far, both)]
-    pieces = [jnp.where(high, b, a) for a, b in zip(low_pair, high_pair)]
-    pieces += [jnp.where(high, a, b) for a, b in zip(low_pair, high_pair)]
-    return jnp.concatenate(pieces, axis=-2)
 
 
 def body(
@@ -609,22 +630,18 @@
     outputs = (middle + (nn(hidden_late, w_down) + nn(inner_late, flat_up[3]))).astype(bf16)
     total = sum_low(keep, swap(send, "fsdp", 1))
     total = jnp.concatenate([scatter_heads(total[:AR]), total[AR:]])
-    total, arrived = lax.optimization_barrier((total, arrived))
+    total, arrived, outputs = lax.optimization_barrier((total, arrived, outputs))
     total = sum_far(total)
-    meta, total, arrived = lax.optimization_barrier((meta, total, arrived))
-    total = gather_heads(jnp.concatenate([total, mlp_total]))
+    meta, total = lax.optimization_barrier((meta, total))
+    own = jnp.concatenate([total, mlp_total])
+    pieces = [own] + [swap(own, "heads", m) for m in (1, 2, 3)]
     arrived = [a.reshape(PARTS, 3, PW, ROWS) for a in arrived]
     grad_inputs = back_inputs(meta, arrived, weights_all, flat_up[:2], down_pair, rows, gain_attn[None, :], grad_middle)
-    total, grad_inputs = lax.optimization_barrier((total, grad_inputs))
-    total = gather_near(total).reshape(2, PARTS, 2 * SR + 2 * SR, D)
-
-    first_pair = total[:, :, :SR].reshape(2, AR, D)
-    second_pair = total[:, :, SR : 2 * SR].reshape(2, PARTS, SR, D // 128, AR)
-    second_pair = jnp.transpose(second_pair, (0, 4, 1, 3, 2)).reshape(2, AR, D)
-    mlp_pair = total[:, :, 2 * SR :].reshape(2, 2, AR, D)
-    grad_first = jnp.concatenate([first_pair, mlp_pair[0]]).reshape(4, ADAPTERS, RANK, D)
-    grad_first = jnp.transpose(grad_first, (0, 1, 3, 2)).astype(f32)
-    grad_second = jnp.concatenate([second_pair, mlp_pair[1]]).reshape(4, ADAPTERS, RANK, D).astype(f32)
+    pieces, grad_inputs = lax.optimization_barrier((pieces, grad_inputs))
+    own = jnp.stack(pieces)
+    grad_first, grad_second = assemble(meta, own, swap(own, "fsdp", 1))
+    grad_first = jnp.transpose(grad_first.reshape(4, ADAPTERS, RANK, D), (0, 1, 3, 2))
+    grad_second = grad_second.reshape(4, ADAPTERS, RANK, D)
     return (outputs[None], grad_inputs[None], grad_first, grad_second)
 
 

time: 474 us -> 448 us (0.945); the launches traced: 465 us -> 444 us
  waiting for transfers between devices: 75 us -> 53.4 us
  starting transfers between devices: 50.8 us -> 72.1 us
  local copies, waits for them, and re-layouts: 44.4 us -> 30.5 us
  other arithmetic: 19.2 us -> 12.6 us
    ppermute x24, waiting for transfers between devices: 65.6 us -> 44 us  [swap(): return lax.ppermute(value, axis, [(i, i ^ mask) for i in range(count)])]
    ppermute x24, starting transfers between devices: 26.1 us -> 37.2 us  [swap(): return lax.ppermute(value, axis, [(i, i ^ mask) for i in range(count)])]
    all_to_all x6, starting transfers between devices: 24.5 us -> 34.7 us  [exchange(): lax.all_to_all(value, 'heads', split_axis=0, concat_axis=0, tiled=True)]
    transpose x1 -> x0, local copies, waits for them, and re-layouts: 7.39 us -> none  [body(): second_pair = jnp.transpose(second_pair, (0, 4, 1, 3, 2)).reshape(2, AR, D)]
    pallas_call x0 -> x1, Pallas kernels: none -> 5.32 us  [assemble(): pl.pallas_call(assemble_kernel, out_shape=[jax.ShapeDtypeStruct((4, AR, D...]
    concatenate x2 -> x1, local copies, waits for them, and re-layouts: 5.23 us -> 0.01 us  [body(): own = jnp.concatenate([total, mlp_total])]
    pallas_call x4, Pallas kernels: 37 us -> 32.3 us  [qkv_project(): pl.pallas_call(qkv_kernel, out_shape=(jax.ShapeDtypeStruct((3 * WIDTH, TO...]
  transfers between devices with their start and end apart: 35 -> 35, of which waited for: 13 -> 11; matrix products, arithmetic and copies ran while one was open for 19% -> 20% of each run, Pallas kernels for 40% -> 46%
where the time goes in v6:
time: 448 us; the launch traced here: 444 us
  Pallas kernels  208 us (46%)
  starting transfers between devices  72.1 us (16%)
  waiting for transfers between devices  53.4 us (12%)
  matrix products  53 us (12%)
  local copies, waits for them, and re-layouts  30.5 us (7%)
  between operations  14.7 us (3%)
  other arithmetic  12.6 us (3%)
    pallas_call x2, Pallas kernels, attn_bwd(): pl.pallas_call(bwd_kernel, out_shape=jax.ShapeDtypeStruct((PARTS, 3, PW,...  88.9 us
    pallas_call x2, Pallas kernels, attn_fwd(): pl.pallas_call(fwd_kernel, out_shape=(jax.ShapeDtypeStruct((PARTS, WIDTH,...  51.4 us
    ppermute x24, waiting for transfers between devices, swap(): return lax.ppermute(value, axis, [(i, i ^ mask) for i in range(count)])  44 us
    ppermute x24, starting transfers between devices, swap(): return lax.ppermute(value, axis, [(i, i ^ mask) for i in range(count)])  37.2 us
    all_to_all x6, starting transfers between devices, exchange(): lax.all_to_all(value, 'heads', split_axis=0, concat_axis=0, tiled=True)  34.7 us
    pallas_call x4, Pallas kernels, qkv_project(): pl.pallas_call(qkv_kernel, out_shape=(jax.ShapeDtypeStruct((3 * WIDTH, TO...  32.3 us
    dot_general x8, matrix products, nt(): lax.dot_general(a, b, (((1,), (1,)), ((), ())), preferred_element_type=f32)  23.9 us
    pallas_call x1, Pallas kernels, back_inputs(): pl.pallas_call(back_kernel, out_shape=jax.ShapeDtypeStruct((ROWS, D), f32...  19.8 us
  transfers between devices with their start and end apart: 35, of which 11 were waited for; matrix products, arithmetic and copies ran while one was open for 20% of the time, Pallas kernels for 46%

profile of v6, /device:TPU:9, one launch (start us, length us, event | category | flops | bytes accessed | tf_op | source)
XLA Modules:
  0.0 444.2 jit_solution(8529080309068383159)
XLA Ops:
  28.4 9.4 %collective-permute-done.low_ref = bf16[384,1280]{1,0:T(8,128)(2,1)} collective-permute-done((bf16[384,1280]{1,0:T(8,128)(2,1)}, bf16[384,1280]{1,0:T(8,128)(2,1)}, u32[]{:S(2)}, u32[]{:S(2)}) %collective-permute-start) | collective-permute-done | bytes 983072 | tf_op jit(solution)/shard_map/ppermute | solution.py:477
  45.3 4.3 copy.54
  49.6 8.0 %qkv_project.4 = (bf16[960,3072]{1,0:T(8,128)(2,1)}, bf16[3072,1280]{1,0:T(8,128)(2,1)}, bf16[3072,256]{1,0:T(8,128)(2,1)}) custom-call(s32[8]{0:T(128)} %pad_add_fusion.meta, s32[1]{0:T(128)} %bitcast.17.first, bf16[768,1280]{1,0:T(8,128)(2,1)} %bitcast.120, bf16[768,1280]{1,0:T(8,128)(2,1)} %bitcast.121, f32[1,1280]{1,0:T(1,128)} %reshape.145.gain_ref, ...), custom_call_target="tpu_custom_call" | custom-call | flops 2390753280 | bytes 8388608 | tf_op jit(solution)/shard_map/qkv_project/pallas_call | solution.py:84
  58.0 8.1 %qkv_project.5 = (bf16[960,3072]{1,0:T(8,128)(2,1)}, bf16[3072,1280]{1,0:T(8,128)(2,1)}, bf16[3072,256]{1,0:T(8,128)(2,1)}) custom-call(s32[8]{0:T(128)} %pad_add_fusion.meta, s32[1]{0:T(128)} %bitcast.16.first, bf16[384,1280]{1,0:T(8,128)(2,1)} %collective-permute-done.5.low_ref, ...), custom_call_target="tpu_custom_call", output_to_operand_aliasing={{0}: (9, {}), {1}: (10, {}), {2}: (11, {})} | custom-call | flops 2390753280 | bytes 8388608 | tf_op jit(solution)/shard_map/qkv_project/pallas_call | solution.py:84
  66.1 8.1 %qkv_project.6 = (bf16[960,3072]{1,0:T(8,128)(2,1)}, bf16[3072,1280]{1,0:T(8,128)(2,1)}, bf16[3072,256]{1,0:T(8,128)(2,1)}) custom-call(s32[8]{0:T(128)} %pad_add_fusion.meta, s32[1]{0:T(128)} %bitcast.15.first, bf16[384,1280]{1,0:T(8,128)(2,1)} %collective-permute-done.low_ref, ...), custom_call_target="tpu_custom_call", output_to_operand_aliasing={{0}: (9, {}), {1}: (10, {}), {2}: (11, {})} | custom-call | flops 2390753280 | bytes 8388608 | tf_op jit(solution)/shard_map/qkv_project/pallas_call | solution.py:84
  74.2 4.8 %collective-permute-done.1.low_ref = bf16[384,1280]{1,0:T(8,128)(2,1)} collective-permute-done((bf16[384,1280]{1,0:T(8,128)(2,1)}, bf16[384,1280]{1,0:T(8,128)(2,1)}, u32[]{:S(2)}, u32[]{:S(2)}) %collective-permute-start.1) | collective-permute-done | bytes 983072 | tf_op jit(solution)/shard_map/ppermute | solution.py:477
  80.0 8.1 %qkv_project.7 = (bf16[960,3072]{1,0:T(8,128)(2,1)}, bf16[3072,1280]{1,0:T(8,128)(2,1)}, bf16[3072,256]{1,0:T(8,128)(2,1)}) custom-call(s32[8]{0:T(128)} %pad_add_fusion.meta, s32[1]{0:T(128)} %bitcast.6.first, bf16[384,1280]{1,0:T(8,128)(2,1)} %collective-permute-done.1.low_ref, ...), custom_call_target="tpu_custom_call", output_to_operand_aliasing={{0}: (9, {}), {1}: (10, {}), {2}: (11, {})} | custom-call | flops 2390753280 | bytes 8388608 | tf_op jit(solution)/shard_map/qkv_project/pallas_call | solution.py:84
  88.0 31.0 %attn_fwd.2 = (bf16[4,320,512]{2,1,0:T(8,128)(2,1)}, f32[4,4,1,512]{3,2,1,0:T(1,128)}) custom-call(s32[2]{0:T(128)} %copy-done.38, bf16[960,3072]{1,0:T(8,128)(2,1)} %get-tuple-element.66.q_ref.k_ref.v_ref, bf16[960,3072]{1,0:T(8,128)(2,1)} %get-tuple-element.66.q_ref.k_ref.v_ref, bf16[960,3072]{1,0:T(8,128)(2,1)} %get-tuple-element.66.q_ref.k_ref.v_ref), custom_call_target="tpu_custom_call" | custom-call | flops 25999998976 | bytes 5242880 | tf_op jit(solution)/shard_map/attn_fwd/pallas_call | solution.py:332
  119.0 15.0 %all-to-all-start = ((bf16[4,320,512]{2,1,0:T(8,128)(2,1)}), bf16[4,320,512]{2,1,0:T(8,128)(2,1)}, u32[]{:S(2)}, u32[]{:S(2)}) async-start(bf16[4,320,512]{2,1,0:T(8,128)(2,1)} %get-tuple-element.70), calls=%async_computation | async-start | bytes 2621440 | tf_op jit(solution)/shard_map/all_to_all | solution.py:472
  134.0 20.4 %attn_fwd.3 = (bf16[4,320,256]{2,1,0:T(8,128)(2,1)}, f32[4,4,1,256]{3,2,1,0:T(1,128)}) custom-call(s32[2]{0:T(128)} %copy-done.38, bf16[960,3072]{1,0:T(8,128)(2,1)} %get-tuple-element.66.q_ref.k_ref.v_ref, bf16[960,3072]{1,0:T(8,128)(2,1)} %get-tuple-element.66.q_ref.k_ref.v_ref, bf16[960,3072]{1,0:T(8,128)(2,1)} %get-tuple-element.66.q_ref.k_ref.v_ref), custom_call_target="tpu_custom_call" | custom-call | flops 12999999488 | bytes 5242880 | tf_op jit(solution)/shard_map/attn_fwd/pallas_call | solution.py:332
  160.8 3.9 fusion.40
  164.7 6.7 %fusion.13 = f32[768,1280]{1,0:T(8,128)} fusion(bf16[1280,1280]{1,0:T(8,128)(2,1)} %all-gather.12.cloned.1.call-done, bf16[1,768,1280]{2,1,0:T(8,128)(2,1)S(1)} %copy-done.2), kind=kOutput, calls=%fused_computation.29 | convolution fusion | flops 2516582400 | bytes 9175040 | tf_op jit(solution)/shard_map/dot_general | solution.py:31
  171.4 4.8 %fusion.45 = f32[512,1280]{1,0:T(8,128)} fusion(bf16[1280,512]{1,0:T(8,128)(2,1)} %bitcast.18, bf16[1280,1280]{1,0:T(8,128)(2,1)S(1)} %copy-done.8), kind=kOutput, calls=%fused_computation.101 | convolution fusion | flops 1677721600 | bytes 7208960 | tf_op jit(solution)/shard_map/dot_general | solution.py:35
  184.2 5.9 %fusion.39 = f32[768,1280]{1,0:T(8,128)S(1)} fusion(bf16[1280,1280]{1,0:T(8,128)(2,1)} %all-gather.10.cloned.1.call-done, f32[768,1280]{1,0:T(8,128)} %get-tuple-element.105, f32[1280]{0:T(1024)S(1)} %convert_element_type.138, f32[768]{0:T(1024)S(1)} %get-tuple-element.123), kind=kOutput, calls=%fused_computation.95 | convolution fusion | flops 2519531520 | bytes 11149312 | tf_op jit(solution)/shard_map/dot_general | solution.py:39
  211.7 4.2 all-to-all-start.2
  215.9 4.6 %convolution_convert_fusion.4 = bf16[768,640]{0,1:T(8,128)(2,1)} fusion(bf16[640,1280]{1,0:T(8,128)(2,1)S(1)} %bitcast.130, f32[768,1280]{1,0:T(8,128)} %copy-done.7), kind=kOutput, calls=%fused_computation.32 | convolution fusion | flops 1259765760 | bytes 6553600 | tf_op jit(solution)/shard_map/dot_general | solution.py:31
  221.8 7.1 %all-to-all-done.2.do_ref = bf16[4,160,768]{2,1,0:T(8,128)(2,1)} async-done(((bf16[4,160,768]{2,1,0:T(8,128)(2,1)}), bf16[4,160,768]{2,1,0:T(8,128)(2,1)}, u32[]{:S(2)}, u32[]{:S(2)}) %all-to-all-start.2) | async-done | bytes 983072 | tf_op jit(solution)/shard_map/all_to_all | solution.py:472
  228.9 3.5 all-to-all-start.4
  235.2 44.5 %attn_bwd.2.g0_ref = bf16[4,3,160,768]{3,2,1,0:T(8,128)(2,1)} custom-call(s32[8]{0:T(128)} %pad_add_fusion.meta, f32[80,1]{1,0:T(8,128)} %copy.65.scale_ref, bf16[960,3072]{1,0:T(8,128)(2,1)} %get-tuple-element.66.q_ref.k_ref.v_ref, bf16[960,3072]{1,0:T(8,128)(2,1)} %get-tuple-element.66.q_ref.k_ref.v_ref, ...), custom_call_target="tpu_custom_call" | custom-call | flops 35999997952 | bytes 16777216 | tf_op jit(solution)/shard_map/attn_bwd/pallas_call | solution.py:433
  280.1 8.3 %collective-permute-start.11 = (bf16[64,1280]{1,0:T(8,128)(2,1)S(1)}, bf16[64,1280]{1,0:T(8,128)(2,1)}, u32[]{:S(2)}, u32[]{:S(2)}) collective-permute-start(bf16[64,1280]{1,0:T(8,128)(2,1)S(1)} %add_convert_fusion.4), channel_id=1, source_target_pairs={{0,4},{1,5},{2,6},{3,7},{4,0},{5,1},{6,2},{7,3},{8,12},{9,13},{10,... | collective-permute-start | bytes 491528 | tf_op jit(solution)/shard_map/ppermute | solution.py:477
  289.5 3.7 all-to-all-start.3
  293.2 44.5 %attn_bwd.3.g1_ref = bf16[4,3,160,768]{3,2,1,0:T(8,128)(2,1)} custom-call(s32[8]{0:T(128)} %pad_add_fusion.meta, f32[80,1]{1,0:T(8,128)} %copy.65.scale_ref, bf16[960,3072]{1,0:T(8,128)(2,1)} %get-tuple-element.66.q_ref.k_ref.v_ref, bf16[960,3072]{1,0:T(8,128)(2,1)} %get-tuple-element.66.q_ref.k_ref.v_ref, ...), custom_call_target="tpu_custom_call" | custom-call | flops 35999997952 | bytes 16777216 | tf_op jit(solution)/shard_map/attn_bwd/pallas_call | solution.py:433
  341.1 4.8 %all-to-all-start.5 = ((bf16[4,480,768]{2,1,0:T(8,128)(2,1)}), bf16[4,480,768]{2,1,0:T(8,128)(2,1)}, u32[]{:S(2)}, u32[]{:S(2)}) async-start(bf16[4,480,768]{2,1,0:T(8,128)(2,1)} %bitcast.118), calls=%async_computation.5 | async-start | bytes 5898240 | tf_op jit(solution)/shard_map/all_to_all | solution.py:472
  345.9 10.3 %adapter_grads.1 = (bf16[160,1280]{1,0:T(8,128)(2,1)}, bf16[160,1280]{1,0:T(8,128)(2,1)}) custom-call(s32[8]{0:T(128)} %pad_add_fusion.meta, bf16[4,3,160,768]{3,2,1,0:T(8,128)(2,1)} %attn_bwd.2.g0_ref, bf16[4,3,160,768]{3,2,1,0:T(8,128)(2,1)} %attn_bwd.3.g1_ref, bf16[3072,1280]{1,0:T(8,128)(2,1)} %get-tuple-element.82.normed_ref, ...), custom_call_target="tpu_custom_call" | custom-call | flops 4026531840 | bytes 20971520 | tf_op jit(solution)/shard_map/adapter_grads/pallas_call | solution.py:145
  359.5 4.8 %fusion.48 = f32[768,1280]{1,0:T(8,128)S(1)} fusion(bf16[768,1280]{1,0:T(8,128)(2,1)S(1)} %copy-done.13, bf16[1280,1280]{1,0:T(8,128)(2,1)} %all-gather.12.cloned.1.call-done), kind=kOutput, calls=%fused_computation.104 | convolution fusion | flops 2516582400 | bytes 9175040 | tf_op jit(solution)/shard_map/dot_general | solution.py:39
  369.6 9.0 %collective-permute-done.14 = bf16[32,1280]{1,0:T(8,128)(2,1)S(1)} collective-permute-done((bf16[32,1280]{1,0:T(8,128)(2,1)S(1)}, bf16[32,1280]{1,0:T(8,128)(2,1)S(1)}, u32[]{:S(2)}, u32[]{:S(2)}) %collective-permute-start.14) | collective-permute-done | bytes 81952 | tf_op jit(solution)/shard_map/ppermute | solution.py:477
  378.5 3.6 collective-permute-done.15
  383.4 5.1 %collective-permute-start.18 = (bf16[64,1280]{1,0:T(8,128)(2,1)S(1)}, bf16[64,1280]{1,0:T(8,128)(2,1)S(1)}, u32[]{:S(2)}, u32[]{:S(2)}) collective-permute-start(bf16[64,1280]{1,0:T(8,128)(2,1)S(1)} %pad_maximum_fusion.5), channel_id=1, source_target_pairs={{0,4},{1,5},{2,6},{3,7},{4,0},{5,1},{6,2},{7,3},{8,12},{9,13},{10,... | collective-permute-start | bytes 491528 | tf_op jit(solution)/shard_map/ppermute | solution.py:477
  388.8 9.8 %collective-permute-done.18 = bf16[64,1280]{1,0:T(8,128)(2,1)S(1)} collective-permute-done((bf16[64,1280]{1,0:T(8,128)(2,1)S(1)}, bf16[64,1280]{1,0:T(8,128)(2,1)S(1)}, u32[]{:S(2)}, u32[]{:S(2)}) %collective-permute-start.18) | collective-permute-done | bytes 163872 | tf_op jit(solution)/shard_map/ppermute | solution.py:477
  398.6 3.5 collective-permute-done.19
  405.3 19.8 %back_inputs.1 = f32[768,1280]{1,0:T(8,128)} custom-call(s32[8]{0:T(128)} %pad_add_fusion.meta, bf16[4,3,160,768]{3,2,1,0:T(8,128)(2,1)} %bitcast.124, bf16[4,3,160,768]{3,2,1,0:T(8,128)(2,1)} %bitcast.46.b1_ref, bf16[1280,3840]{1,0:T(8,128)(2,1)} %all-gather.14.cloned.1.call-done.w_ref, bf16[2,128,1280]{2,1,0:T(8,128)(2,1)} %bitcast.129, ...), custom_call_target="tpu_custom_call" | custom-call | flops 7549747200 | bytes 25165824 | tf_op jit(solution)/shard_map/back_inputs/pallas_call | solution.py:204
  432.2 5.3 %assemble.1 = (f32[4,128,1280]{2,1,0:T(8,128)}, f32[4,128,1280]{2,1,0:T(8,128)}) custom-call(s32[8]{0:T(128)} %pad_add_fusion.meta, bf16[4,128,1280]{2,1,0:T(8,128)(2,1)} %copy-done.6, bf16[4,128,1280]{2,1,0:T(8,128)(2,1)} %copy-done.22), custom_call_target="tpu_custom_call" | custom-call | flops 1048576 | bytes 8388608 | tf_op jit(solution)/shard_map/assemble/pallas_call | solution.py:254
  (220 shorter events, 94.7 us)
Async XLA Ops:
  7.2 38.1 %all-gather.6.cloned.1.call-start = ((), (), s32[]{:S(2)}) async-start(), calls=%async_computation.6 | async-start | bytes 2949120 | tf_op jit(solution)/shard_map/all_gather | solution.py:559
  10.4 150.4 %all-gather.8.cloned.1.call-start = ((), (), s32[]{:S(2)}) async-start(), calls=%async_computation.7 | async-start | bytes 3686400 | tf_op jit(solution)/shard_map/all_gather | solution.py:560
  11.2 153.5 %all-gather.12.cloned.1.call-start = ((), (), s32[]{:S(2)}) async-start(), calls=%async_computation.9 | async-start | bytes 3686400 | tf_op jit(solution)/shard_map/all_gather | solution.py:562
  11.9 172.3 %all-gather.10.cloned.1.call-start = ((), (), s32[]{:S(2)}) async-start(), calls=%async_computation.8 | async-start | bytes 3686400 | tf_op jit(solution)/shard_map/all_gather | solution.py:561
  12.5 392.9 %all-gather.14.cloned.1.call-start = ((), (), s32[]{:S(2)}) async-start(), calls=%async_computation.10 | async-start | bytes 11059200 | tf_op jit(solution)/shard_map/all_gather | solution.py:563
  13.9 24.1 %collective-permute-start.2 = (bf16[384,1280]{1,0:T(8,128)(2,1)}, bf16[384,1280]{1,0:T(8,128)(2,1)}, u32[]{:S(2)}, u32[]{:S(2)}) collective-permute-start(bf16[384,1280]{1,0:T(8,128)(2,1)} %get-tuple-element.55), channel_id=1, source_target_pairs={{0,8},{8,0},{16,24},{24,16},{1,9},{9,1},{17,25},{25,17},{2,10},{10... | collective-permute-start | bytes 2949128 | tf_op jit(solution)/shard_map/ppermute | solution.py:477
  15.1 22.7 %collective-permute-start = (bf16[384,1280]{1,0:T(8,128)(2,1)}, bf16[384,1280]{1,0:T(8,128)(2,1)}, u32[]{:S(2)}, u32[]{:S(2)}) collective-permute-start(bf16[384,1280]{1,0:T(8,128)(2,1)} %get-tuple-element.56), channel_id=1, source_target_pairs={{0,16},{8,24},{16,0},{24,8},{1,17},{9,25},{17,1},{25,9},{2,18},{10... | collective-permute-start | bytes 2949128 | tf_op jit(solution)/shard_map/ppermute | solution.py:477
  18.7 39.3 %collective-permute-start.5 = (bf16[384,1280]{1,0:T(8,128)(2,1)}, bf16[384,1280]{1,0:T(8,128)(2,1)}, u32[]{:S(2)}, u32[]{:S(2)}) collective-permute-start(bf16[384,1280]{1,0:T(8,128)(2,1)} %get-tuple-element.56), channel_id=1, source_target_pairs={{0,8},{8,0},{16,24},{24,16},{1,9},{9,1},{17,25},{25,17},{2,10},{10... | collective-permute-start | bytes 2949128 | tf_op jit(solution)/shard_map/ppermute | solution.py:477
  19.0 47.1 %collective-permute-start.4 = (bf16[384,1280]{1,0:T(8,128)(2,1)}, bf16[384,1280]{1,0:T(8,128)(2,1)}, u32[]{:S(2)}, u32[]{:S(2)}) collective-permute-start(bf16[384,1280]{1,0:T(8,128)(2,1)} %get-tuple-element.55), channel_id=1, source_target_pairs={{0,16},{8,24},{16,0},{24,8},{1,17},{9,25},{17,1},{25,9},{2,18},{10... | collective-permute-start | bytes 2949128 | tf_op jit(solution)/shard_map/ppermute | solution.py:477
  37.8 41.2 %collective-permute-start.1 = (bf16[384,1280]{1,0:T(8,128)(2,1)}, bf16[384,1280]{1,0:T(8,128)(2,1)}, u32[]{:S(2)}, u32[]{:S(2)}) collective-permute-start(bf16[384,1280]{1,0:T(8,128)(2,1)} %collective-permute-done.low_ref), channel_id=1, source_target_pairs={{0,8},{8,0},{16,24},{24,16},{1,9},{9,1},{17,25},{25,17},{2,10},{10... | collective-permute-start | bytes 2949128 | tf_op jit(solution)/shard_map/ppermute | solution.py:477
  38.1 41.9 %collective-permute-start.3 = (bf16[384,1280]{1,0:T(8,128)(2,1)}, bf16[384,1280]{1,0:T(8,128)(2,1)}, u32[]{:S(2)}, u32[]{:S(2)}) collective-permute-start(bf16[384,1280]{1,0:T(8,128)(2,1)} %collective-permute-done.2.high_ref), channel_id=1, source_target_pairs={{0,16},{8,24},{16,0},{24,8},{1,17},{9,25},{17,1},{25,9},{2,18},{10... | collective-permute-start | bytes 2949128 | tf_op jit(solution)/shard_map/ppermute | solution.py:477
  119.0 38.3 %all-to-all-start = ((bf16[4,320,512]{2,1,0:T(8,128)(2,1)}), bf16[4,320,512]{2,1,0:T(8,128)(2,1)}, u32[]{:S(2)}, u32[]{:S(2)}) async-start(bf16[4,320,512]{2,1,0:T(8,128)(2,1)} %get-tuple-element.70), calls=%async_computation | async-start | bytes 2621440 | tf_op jit(solution)/shard_map/all_to_all | solution.py:472
  157.3 18.9 %all-to-all-start.1 = ((bf16[4,320,256]{2,1,0:T(8,128)(2,1)}), bf16[4,320,256]{2,1,0:T(8,128)(2,1)S(1)}, u32[]{:S(2)}, u32[]{:S(2)}) async-start(bf16[4,320,256]{2,1,0:T(8,128)(2,1)} %get-tuple-element.72), calls=%async_computation.1 | async-start | bytes 1310720 | tf_op jit(solution)/shard_map/all_to_all | solution.py:472
  202.2 18.4 %collective-permute-start.6 = (bf16[256,1280]{1,0:T(8,128)(2,1)}, bf16[256,1280]{1,0:T(8,128)(2,1)}, u32[]{:S(2)}, u32[]{:S(2)}) collective-permute-start(bf16[256,1280]{1,0:T(8,128)(2,1)} %constant_dynamic-slice_fusion.6), channel_id=1, source_target_pairs={{0,1},{1,0},{2,3},{3,2},{4,5},{5,4},{6,7},{7,6},{8,9},{9,8},{10,11... | collective-permute-start | bytes 1966088 | tf_op jit(solution)/shard_map/ppermute | solution.py:477
  211.7 17.2 %all-to-all-start.2 = ((bf16[4,160,768]{2,1,0:T(8,128)(2,1)}), bf16[4,160,768]{2,1,0:T(8,128)(2,1)}, u32[]{:S(2)}, u32[]{:S(2)}) async-start(bf16[4,160,768]{2,1,0:T(8,128)(2,1)} %bitcast.141), calls=%async_computation.2 | async-start | bytes 1966080 | tf_op jit(solution)/shard_map/all_to_all | solution.py:472
  228.9 59.7 %all-to-all-start.4 = ((bf16[4,160,768]{2,1,0:T(8,128)(2,1)}), bf16[4,160,768]{2,1,0:T(8,128)(2,1)S(1)}, u32[]{:S(2)}, u32[]{:S(2)}) async-start(bf16[4,160,768]{2,1,0:T(8,128)(2,1)} %bitcast.140), calls=%async_computation.4 | async-start | bytes 1966080 | tf_op jit(solution)/shard_map/all_to_all | solution.py:472
  232.5 47.2 %collective-permute-start.7 = (bf16[64,1280]{1,0:T(8,128)(2,1)S(1)}, bf16[64,1280]{1,0:T(8,128)(2,1)S(1)}, u32[]{:S(2)}, u32[]{:S(2)}) collective-permute-start(bf16[64,1280]{1,0:T(8,128)(2,1)S(1)} %get-tuple-element.116), channel_id=1, source_target_pairs={{0,8},{8,0},{16,24},{24,16},{1,9},{9,1},{17,25},{25,17},{2,10},{10... | collective-permute-start | bytes 491528 | tf_op jit(solution)/shard_map/ppermute | solution.py:477
  233.9 45.7 %collective-permute-start.8 = (bf16[64,1280]{1,0:T(8,128)(2,1)S(1)}, bf16[64,1280]{1,0:T(8,128)(2,1)S(1)}, u32[]{:S(2)}, u32[]{:S(2)}) collective-permute-start(bf16[64,1280]{1,0:T(8,128)(2,1)S(1)} %get-tuple-element.118), channel_id=1, source_target_pairs={{0,16},{8,24},{16,0},{24,8},{1,17},{9,25},{17,1},{25,9},{2,18},{10... | collective-permute-start | bytes 491528 | tf_op jit(solution)/shard_map/ppermute | solution.py:477
  235.1 44.6 %collective-permute-start.9 = (bf16[64,1280]{1,0:T(8,128)(2,1)S(1)}, bf16[64,1280]{1,0:T(8,128)(2,1)S(1)}, u32[]{:S(2)}, u32[]{:S(2)}) collective-permute-start(bf16[64,1280]{1,0:T(8,128)(2,1)S(1)} %get-tuple-element.117), channel_id=1, source_target_pairs={{0,24},{8,16},{16,8},{24,0},{1,25},{9,17},{17,9},{25,1},{2,26},{10... | collective-permute-start | bytes 491528 | tf_op jit(solution)/shard_map/ppermute | solution.py:477
  279.8 57.9 %collective-permute-start.10 = (bf16[64,1280]{1,0:T(8,128)(2,1)S(1)}, bf16[64,1280]{1,0:T(8,128)(2,1)S(1)}, u32[]{:S(2)}, u32[]{:S(2)}) collective-permute-start(bf16[64,1280]{1,0:T(8,128)(2,1)S(1)} %add_convert_fusion.4), channel_id=1, source_target_pairs={{0,2},{1,3},{2,0},{3,1},{4,6},{5,7},{6,4},{7,5},{8,10},{9,11},{10,... | collective-permute-start | bytes 491528 | tf_op jit(solution)/shard_map/ppermute | solution.py:477
  280.1 57.6 %collective-permute-start.11 = (bf16[64,1280]{1,0:T(8,128)(2,1)S(1)}, bf16[64,1280]{1,0:T(8,128)(2,1)}, u32[]{:S(2)}, u32[]{:S(2)}) collective-permute-start(bf16[64,1280]{1,0:T(8,128)(2,1)S(1)} %add_convert_fusion.4), channel_id=1, source_target_pairs={{0,4},{1,5},{2,6},{3,7},{4,0},{5,1},{6,2},{7,3},{8,12},{9,13},{10,... | collective-permute-start | bytes 491528 | tf_op jit(solution)/shard_map/ppermute | solution.py:477
  288.3 50.0 %collective-permute-start.12 = (bf16[64,1280]{1,0:T(8,128)(2,1)S(1)}, bf16[64,1280]{1,0:T(8,128)(2,1)}, u32[]{:S(2)}, u32[]{:S(2)}) collective-permute-start(bf16[64,1280]{1,0:T(8,128)(2,1)S(1)} %add_convert_fusion.4), channel_id=1, source_target_pairs={{0,6},{1,7},{2,4},{3,5},{4,2},{5,3},{6,0},{7,1},{8,14},{9,15},{10,... | collective-permute-start | bytes 491528 | tf_op jit(solution)/shard_map/ppermute | solution.py:477
  289.5 50.0 %all-to-all-start.3 = ((bf16[4,480,768]{2,1,0:T(8,128)(2,1)}), bf16[4,480,768]{2,1,0:T(8,128)(2,1)S(1)}, u32[]{:S(2)}, u32[]{:S(2)}) async-start(bf16[4,480,768]{2,1,0:T(8,128)(2,1)} %bitcast.119), calls=%async_computation.3 | async-start | bytes 5898240 | tf_op jit(solution)/shard_map/all_to_all | solution.py:472
  341.1 41.1 %all-to-all-start.5 = ((bf16[4,480,768]{2,1,0:T(8,128)(2,1)}), bf16[4,480,768]{2,1,0:T(8,128)(2,1)}, u32[]{:S(2)}, u32[]{:S(2)}) async-start(bf16[4,480,768]{2,1,0:T(8,128)(2,1)} %bitcast.118), calls=%async_computation.5 | async-start | bytes 5898240 | tf_op jit(solution)/shard_map/all_to_all | solution.py:472
  364.5 14.0 %collective-permute-start.14 = (bf16[32,1280]{1,0:T(8,128)(2,1)S(1)}, bf16[32,1280]{1,0:T(8,128)(2,1)S(1)}, u32[]{:S(2)}, u32[]{:S(2)}) collective-permute-start(bf16[32,1280]{1,0:T(8,128)(2,1)S(1)} %get-tuple-element.119), channel_id=1, source_target_pairs={{0,8},{8,0},{16,24},{24,16},{1,9},{9,1},{17,25},{25,17},{2,10},{10... | collective-permute-start | bytes 245768 | tf_op jit(solution)/shard_map/ppermute | solution.py:477
  366.3 15.8 %collective-permute-start.15 = (bf16[32,1280]{1,0:T(8,128)(2,1)S(1)}, bf16[32,1280]{1,0:T(8,128)(2,1)S(1)}, u32[]{:S(2)}, u32[]{:S(2)}) collective-permute-start(bf16[32,1280]{1,0:T(8,128)(2,1)S(1)} %get-tuple-element.121), channel_id=1, source_target_pairs={{0,16},{8,24},{16,0},{24,8},{1,17},{9,25},{17,1},{25,9},{2,18},{10... | collective-permute-start | bytes 245768 | tf_op jit(solution)/shard_map/ppermute | solution.py:477
  367.5 14.6 %collective-permute-start.16 = (bf16[32,1280]{1,0:T(8,128)(2,1)S(1)}, bf16[32,1280]{1,0:T(8,128)(2,1)S(1)}, u32[]{:S(2)}, u32[]{:S(2)}) collective-permute-start(bf16[32,1280]{1,0:T(8,128)(2,1)S(1)} %get-tuple-element.120), channel_id=1, source_target_pairs={{0,24},{8,16},{16,8},{24,0},{1,25},{9,17},{17,9},{25,1},{2,26},{10... | collective-permute-start | bytes 245768 | tf_op jit(solution)/shard_map/ppermute | solution.py:477
  383.4 15.1 %collective-permute-start.18 = (bf16[64,1280]{1,0:T(8,128)(2,1)S(1)}, bf16[64,1280]{1,0:T(8,128)(2,1)S(1)}, u32[]{:S(2)}, u32[]{:S(2)}) collective-permute-start(bf16[64,1280]{1,0:T(8,128)(2,1)S(1)} %pad_maximum_fusion.5), channel_id=1, source_target_pairs={{0,4},{1,5},{2,6},{3,7},{4,0},{5,1},{6,2},{7,3},{8,12},{9,13},{10,... | collective-permute-start | bytes 491528 | tf_op jit(solution)/shard_map/ppermute | solution.py:477
  388.6 13.5 %collective-permute-start.19 = (bf16[64,1280]{1,0:T(8,128)(2,1)S(1)}, bf16[64,1280]{1,0:T(8,128)(2,1)S(1)}, u32[]{:S(2)}, u32[]{:S(2)}) collective-permute-start(bf16[64,1280]{1,0:T(8,128)(2,1)S(1)} %pad_maximum_fusion.5), channel_id=1, source_target_pairs={{0,6},{1,7},{2,4},{3,5},{4,2},{5,3},{6,0},{7,1},{8,14},{9,15},{10,... | collective-permute-start | bytes 491528 | tf_op jit(solution)/shard_map/ppermute | solution.py:477
  402.2 22.9 %collective-permute-start.20 = (bf16[128,1280]{1,0:T(8,128)(2,1)S(1)}, bf16[128,1280]{1,0:T(8,128)(2,1)S(1)}, u32[]{:S(2)}, u32[]{:S(2)}) collective-permute-start(bf16[128,1280]{1,0:T(8,128)(2,1)S(1)} %constant_dynamic-update-slice_fusion.4), channel_id=1, source_target_pairs={{0,8},{8,0},{16,24},{24,16},{1,9},{9,1},{17,25},{25,17},{2,10},{10... | collective-permute-start | bytes 983048 | tf_op jit(solution)/shard_map/ppermute | solution.py:477
  404.1 21.1 %collective-permute-start.21 = (bf16[128,1280]{1,0:T(8,128)(2,1)S(1)}, bf16[128,1280]{1,0:T(8,128)(2,1)S(1)}, u32[]{:S(2)}, u32[]{:S(2)}) collective-permute-start(bf16[128,1280]{1,0:T(8,128)(2,1)S(1)} %constant_dynamic-update-slice_fusion.4), channel_id=1, source_target_pairs={{0,16},{8,24},{16,0},{24,8},{1,17},{9,25},{17,1},{25,9},{2,18},{10... | collective-permute-start | bytes 983048 | tf_op jit(solution)/shard_map/ppermute | solution.py:477
  404.4 20.8 %collective-permute-start.22 = (bf16[128,1280]{1,0:T(8,128)(2,1)S(1)}, bf16[128,1280]{1,0:T(8,128)(2,1)S(1)}, u32[]{:S(2)}, u32[]{:S(2)}) collective-permute-start(bf16[128,1280]{1,0:T(8,128)(2,1)S(1)} %constant_dynamic-update-slice_fusion.4), channel_id=1, source_target_pairs={{0,24},{8,16},{16,8},{24,0},{1,25},{9,17},{17,9},{25,1},{2,26},{10... | collective-permute-start | bytes 983048 | tf_op jit(solution)/shard_map/ppermute | solution.py:477
  (48 other events, 504.2 us)
Sparse Core Ops, SparseCore 0:
  10.5 34.7 all-gather.5
  47.0 37.9 all-gather.7
  86.6 38.1 all-gather.11
  126.3 38.1 all-gather.9
  166.0 91.0 all-gather.13
